TPU v7x, 256 devices: a whole 4x4x8 slice. The times are simulated.
256 devices in a mesh: seq: 32 (over z, x), head: 4 (over y), batch: 2 (over core).
Axes of the slice: x: 4, y: 4, z: 8, core: 2. Of those that a mesh axis runs over, the one named last changes fastest.
Arguments:
- query_states: bfloat16 [16384, 2048], P(('batch', 'seq'), 'head'), parts along dimension 0, may hold values from -8 to 8
- key_states: bfloat16 [16384, 2048], P(('batch', 'seq'), 'head'), parts along dimension 0, may hold values from -8 to 8
- value_states: bfloat16 [16384, 2048], P(('batch', 'seq'), 'head'), parts along dimension 0, may hold values from -6 to 6
- out_grad: bfloat16 [16384, 2048], P(('batch', 'seq'), 'head'), parts along dimension 0, may hold values from -192 to 192
- head_offsets: int32 [16], P('head'), may hold values from 0 to 8191
Outputs:
- query_grad: bfloat16 [16384, 2048], P(('batch', 'seq'), 'head'), parts along dimension 0
- key_grad: bfloat16 [16384, 2048], P(('batch', 'seq'), 'head'), parts along dimension 0
- value_grad: bfloat16 [16384, 2048], P(('batch', 'seq'), 'head'), parts along dimension 0
There are 2 independent parts, one for each index of `batch`. A program takes and returns all parts, laid end to end along the dimension named above; an argument that names none is the same for every part. Nothing has to cross between parts.
All inputs are finite; a program needn't handle non-finite values.
Results may differ from a plain program's by a relative error of at most 0.0056.
Values may be sent and summed in bfloat16 or wider, within the bound.
No kernel may reach another device: no remote copies, remote signals or barrier semaphores. Data moves between devices by JAX's collectives and lax.ppermute only.
A program may use at most 128 MiB of HBM per device.

v0:
```python
import jax
import jax.numpy as jnp
from jax import lax
from jax.sharding import PartitionSpec as P

WINDOW = 1024


masked_score = -1e30


def from_partner(block, axis, apart):
    count = lax.axis_size(axis)
    route = []
    for low in range(count):
        high = low | 1 << apart
        if high != low and high < count:
            route += [(low, high), (high, low)]
    return lax.ppermute(block, axis, route)


def passed_along(value, axis, steps):
    count = lax.axis_size(axis)
    leading, last = (max(0, -steps), min(count, count - steps))
    return lax.ppermute(value, axis, [(source, source + steps) for source in range(leading, last)])


def forward_part(queries, keys_in, values_in, allowed, softmax_scale):
    scores = (
        jnp.einsum("qhd,khd->hqk", queries, keys_in, preferred_element_type=jnp.float32)
        * softmax_scale
    )
    scores = jnp.where(allowed[None], scores, masked_score)
    row_max = jnp.max(scores, axis=-1)
    weights = jnp.exp(scores - row_max[..., None])
    row_sum = jnp.sum(weights, axis=-1)
    row_out = jnp.einsum(
        "hqk,khd->qhd", weights.astype(jnp.bfloat16), values_in, preferred_element_type=jnp.float32
    )
    return (row_max.T, row_sum.T, row_out)


def backward_part(queries, keys_in, values_in, grads, allowed, log_norm, grad_dot, softmax_scale):
    scores = (
        jnp.einsum("qhd,khd->hqk", queries, keys_in, preferred_element_type=jnp.float32)
        * softmax_scale
    )
    scores = jnp.where(allowed[None], scores, masked_score)
    weights = jnp.exp(scores - log_norm.T[..., None])
    grad_values = jnp.einsum(
        "hqk,qhd->khd", weights.astype(jnp.bfloat16), grads, preferred_element_type=jnp.float32
    )
    grad_probs = jnp.einsum("qhd,khd->hqk", grads, values_in, preferred_element_type=jnp.float32)
    grad_scores = (weights * (grad_probs - grad_dot.T[..., None])).astype(jnp.bfloat16)
    grad_queries = (
        jnp.einsum("hqk,khd->qhd", grad_scores, keys_in, preferred_element_type=jnp.float32)
        * softmax_scale
    )
    grad_keys = (
        jnp.einsum("hqk,qhd->khd", grad_scores, queries, preferred_element_type=jnp.float32)
        * softmax_scale
    )
    return (grad_queries, grad_keys, grad_values)


def merge_stats(first_stats, second_stats):
    row_max = jnp.maximum(first_stats[0], second_stats[0])
    first_factor = jnp.exp(first_stats[0] - row_max)
    second_factor = jnp.exp(second_stats[0] - row_max)
    row_sum = first_stats[1] * first_factor + second_stats[1] * second_factor
    row_out = first_stats[2] * first_factor[..., None] + second_stats[2] * second_factor[..., None]
    return (row_max, row_sum, row_out)


def row_mask(source, chosen):
    return chosen.reshape((1,) + chosen.shape + (1,) * (source.ndim - 2))


def pick_rows(source, chosen):
    stride = chosen.shape[0]
    shaped = source.reshape((source.shape[0] // stride, stride) + source.shape[1:])
    return jnp.sum(jnp.where(row_mask(source, chosen), shaped, jnp.zeros((), source.dtype)), axis=1)


def put_rows(source, chosen, update):
    stride = chosen.shape[0]
    shaped = source.reshape((source.shape[0] // stride, stride) + source.shape[1:])
    return jnp.where(row_mask(source, chosen), update[:, None], shaped).reshape(source.shape)


def add_rows(source, chosen, update):
    stride = chosen.shape[0]
    shaped = source.reshape((source.shape[0] // stride, stride) + source.shape[1:])
    return (shaped + jnp.where(row_mask(source, chosen), update[:, None], 0.0)).reshape(
        source.shape
    )


def gather_pairs(group_pair, level_num, position):
    for bit_index in range(level_num):
        partner = from_partner(group_pair, "seq", bit_index)
        upper_half = position >> bit_index & 1 == 1
        group_pair = jnp.where(
            upper_half,
            jnp.concatenate([partner, group_pair], axis=1),
            jnp.concatenate([group_pair, partner], axis=1),
        )
    return group_pair


def block_view(grad_pair, level_num):
    blocks = 2**level_num
    return grad_pair.reshape((2, blocks, grad_pair.shape[1] // blocks) + grad_pair.shape[2:])


def halve_blocks(shaped, bit_index, position):
    paired = shaped.reshape((2, shaped.shape[1] // 2, 2) + shaped.shape[2:])
    upper_half = position >> bit_index & 1 == 1
    kept_half = jnp.where(upper_half, paired[:, :, 1], paired[:, :, 0])
    outgoing = jnp.where(upper_half, paired[:, :, 0], paired[:, :, 1])
    return (kept_half, outgoing)


def return_pairs(grad_pair, level_num, position):
    shaped = block_view(grad_pair, level_num)
    for bit_index in range(level_num):
        kept_half, outgoing = halve_blocks(shaped, bit_index, position)
        shaped = kept_half + from_partner(outgoing.astype(jnp.bfloat16), "seq", bit_index).astype(
            outgoing.dtype
        )
    return shaped[:, 0]


def body(query_states, key_states, value_states, out_grad, head_offsets):
    slab_rows = query_states.shape[0]
    head_count = head_offsets.shape[0]
    head_size = query_states.shape[1] // head_count
    softmax_scale = head_size ** (-0.5)
    queries = query_states.reshape(slab_rows, head_count, head_size)
    keys_own = key_states.reshape(slab_rows, head_count, head_size)
    values_own = value_states.reshape(slab_rows, head_count, head_size)
    grads = out_grad.reshape(slab_rows, head_count, head_size)
    position = lax.axis_index("seq")
    devices = lax.axis_size("seq")
    reach_slabs = WINDOW // slab_rows
    own_pair = jnp.stack([keys_own, values_own])
    earlier = []
    for shift_by in range(reach_slabs, 0, -1):
        earlier.append(passed_along(own_pair, "seq", shift_by))
    near_pair = jnp.concatenate(earlier + [own_pair], axis=1)
    span_cols = (reach_slabs + 1) * slab_rows
    local_rows = jnp.arange(slab_rows, dtype=jnp.int32)[:, None]
    key_cols = jnp.arange(span_cols, dtype=jnp.int32)[None, :]
    distance = local_rows - key_cols + reach_slabs * slab_rows
    near_allowed = (
        (distance >= 0)
        & (distance < WINDOW)
        & (position * slab_rows + key_cols - reach_slabs * slab_rows >= 0)
    )
    stats = forward_part(queries, near_pair[0], near_pair[1], near_allowed, softmax_scale)
    level_count = devices.bit_length() - 1
    saved = []
    for level_num in range(1, level_count + 1):
        stride = 2**level_num
        sparse_rows = slab_rows // stride
        chosen = jnp.arange(stride, dtype=jnp.int32)[:, None] == (head_offsets % stride)[None, :]
        sparse_pair = jnp.stack([pick_rows(keys_own, chosen), pick_rows(values_own, chosen)])
        group_pair = gather_pairs(sparse_pair, level_num, position)
        query_index = position % stride * sparse_rows + jnp.arange(sparse_rows, dtype=jnp.int32)
        level_allowed = jnp.arange(slab_rows, dtype=jnp.int32)[None, :] <= query_index[:, None]
        sparse_queries = pick_rows(queries, chosen)
        update = forward_part(
            sparse_queries, group_pair[0], group_pair[1], level_allowed, softmax_scale
        )
        current = tuple((pick_rows(member, chosen) for member in stats))
        merged = merge_stats(current, update)
        stats = tuple((put_rows(member, chosen, fresh) for member, fresh in zip(stats, merged)))
        saved.append((chosen, sparse_queries, group_pair, level_allowed, level_num))
    log_norm = stats[0] + jnp.log(stats[1])
    out_rows = stats[2] / stats[1][..., None]
    grad_dot = jnp.sum(grads.astype(jnp.float32) * out_rows, axis=-1)
    grad_query, near_key_grad, near_value_grad = backward_part(
        queries, near_pair[0], near_pair[1], grads, near_allowed, log_norm, grad_dot, softmax_scale
    )
    near_grads = jnp.stack([near_key_grad, near_value_grad])
    kv_grads = near_grads[:, reach_slabs * slab_rows :]
    for shift_by in range(1, reach_slabs + 1):
        block_start = (reach_slabs - shift_by) * slab_rows
        kv_grads = kv_grads + passed_along(
            near_grads[:, block_start : block_start + slab_rows], "seq", -shift_by
        )
    for chosen, sparse_queries, group_pair, level_allowed, level_num in saved:
        sparse_grads = pick_rows(grads, chosen)
        level_query, level_key, level_value = backward_part(
            sparse_queries,
            group_pair[0],
            group_pair[1],
            sparse_grads,
            level_allowed,
            pick_rows(log_norm, chosen),
            pick_rows(grad_dot, chosen),
            softmax_scale,
        )
        grad_query = add_rows(grad_query, chosen, level_query)
        returned = return_pairs(jnp.stack([level_key, level_value]), level_num, position)
        kv_grads = jnp.stack(
            [add_rows(kv_grads[0], chosen, returned[0]), add_rows(kv_grads[1], chosen, returned[1])]
        )
    shape_out = (slab_rows, head_count * head_size)
    return (
        grad_query.astype(jnp.bfloat16).reshape(shape_out),
        kv_grads[0].astype(jnp.bfloat16).reshape(shape_out),
        kv_grads[1].astype(jnp.bfloat16).reshape(shape_out),
    )


def solution(mesh):
    in_specs = (
        P(("batch", "seq"), "head"),
        P(("batch", "seq"), "head"),
        P(("batch", "seq"), "head"),
        P(("batch", "seq"), "head"),
        P("head"),
    )
    out_specs = (
        P(("batch", "seq"), "head"),
        P(("batch", "seq"), "head"),
        P(("batch", "seq"), "head"),
    )
    return jax.shard_map(body, mesh=mesh, in_specs=in_specs, out_specs=out_specs, check_vma=False)
```

profile of v0, /device:TPU:8, one launch (start us, length us, event | category | flops | bytes accessed | tf_op | source)
XLA Modules:
  0.0 459.1 jit_solution(3720014741055494934)
XLA Ops:
  4.1 4.6 %collective-permute-start = (bf16[2,256,4,128]{3,1,2,0:T(8,128)(2,1)}, bf16[2,256,4,128]{3,1,2,0:T(8,128)(2,1)}, u32[]{:S(2)}, u32[]{:S(2)}) collective-permute-start(bf16[2,256,4,128]{3,1,2,0:T(8,128)(2,1)} %pad_maximum_fusion.6), channel_id=1, source_target_pairs={{0,32},{8,40},{16,48},{24,56},{32,64},{40,72},{48,80},{56,88},{64,... | collective-permute-start | bytes 1572872 | tf_op jit(solution)/shard_map/ppermute | solution.py:25
  8.8 5.5 %collective-permute-start.1 = (bf16[2,256,4,128]{3,1,2,0:T(8,128)(2,1)}, bf16[2,256,4,128]{3,1,2,0:T(8,128)(2,1)}, u32[]{:S(2)}, u32[]{:S(2)}) collective-permute-start(bf16[2,256,4,128]{3,1,2,0:T(8,128)(2,1)} %pad_maximum_fusion.6), channel_id=1, source_target_pairs={{0,24},{8,32},{16,40},{24,48},{32,56},{40,64},{48,72},{56,80},{64,... | collective-permute-start | bytes 1572872 | tf_op jit(solution)/shard_map/ppermute | solution.py:25
  19.9 2.0 collective-permute-start.4
  52.9 2.0 collective-permute-start.10
  56.8 2.0 collective-permute-start.15
  58.8 3.4 collective-permute-done.15
  62.2 2.1 collective-permute-start.7
  64.3 2.2 collective-permute-done.7
  66.6 2.4 collective-permute-start.11
  69.0 3.4 collective-permute-done.11
  73.2 3.8 collective-permute-done.16
  77.0 1.9 collective-permute-start.8
  81.7 1.8 collective-permute-done.8
  83.5 3.9 collective-permute-start.17
  87.5 6.7 %collective-permute-start.2 = (bf16[2,256,4,128]{3,1,2,0:T(8,128)(2,1)}, bf16[2,256,4,128]{3,1,2,0:T(8,128)(2,1)}, u32[]{:S(2)}, u32[]{:S(2)}) collective-permute-start(bf16[2,256,4,128]{3,1,2,0:T(8,128)(2,1)} %pad_maximum_fusion.6), channel_id=1, source_target_pairs={{0,16},{8,24},{16,32},{24,40},{32,48},{40,56},{48,64},{56,72},{64,... | collective-permute-start | bytes 1572872 | tf_op jit(solution)/shard_map/ppermute | solution.py:25
  94.3 2.6 collective-permute-start.3
  101.4 10.4 %collective-permute-done.6 = bf16[2,128,4,128]{3,1,2,0:T(8,128)(2,1)S(1)} collective-permute-done((bf16[2,128,4,128]{3,1,2,0:T(8,128)(2,1)S(1)}, bf16[2,128,4,128]{3,1,2,0:T(8,128)(2,1)S(1)}, u32[]{:S(2)}, u32[]{:S(2)}) %collective-permute-start.6) | collective-permute-done | bytes 262176 | tf_op jit(solution)/shard_map/ppermute | solution.py:19
  111.7 7.6 %collective-permute-start.9 = (bf16[2,128,4,128]{3,1,2,0:T(8,128)(2,1)S(1)}, bf16[2,128,4,128]{3,1,2,0:T(8,128)(2,1)S(1)}, u32[]{:S(2)}, u32[]{:S(2)}) collective-permute-start(bf16[2,128,4,128]{3,1,2,0:T(8,128)(2,1)S(1)} %maximum_select_fusion.6), channel_id=1, source_target_pairs={{0,32},{32,0},{8,40},{40,8},{16,48},{48,16},{24,56},{56,24},{64,96... | collective-permute-start | bytes 786440 | tf_op jit(solution)/shard_map/ppermute | solution.py:19
  120.6 4.6 %collective-permute-done.9 = bf16[2,128,4,128]{3,1,2,0:T(8,128)(2,1)S(1)} collective-permute-done((bf16[2,128,4,128]{3,1,2,0:T(8,128)(2,1)S(1)}, bf16[2,128,4,128]{3,1,2,0:T(8,128)(2,1)S(1)}, u32[]{:S(2)}, u32[]{:S(2)}) %collective-permute-start.9) | collective-permute-done | bytes 262176 | tf_op jit(solution)/shard_map/ppermute | solution.py:19
  125.2 1.9 collective-permute-start.13
  128.4 12.6 %collective-permute-done.13 = bf16[2,128,4,128]{3,1,2,0:T(8,128)(2,1)S(1)} collective-permute-done((bf16[2,128,4,128]{3,1,2,0:T(8,128)(2,1)S(1)}, bf16[2,128,4,128]{3,1,2,0:T(8,128)(2,1)S(1)}, u32[]{:S(2)}, u32[]{:S(2)}) %collective-permute-start.13) | collective-permute-done | bytes 262176 | tf_op jit(solution)/shard_map/ppermute | solution.py:19
  144.0 8.6 %collective-permute-done.18 = bf16[2,128,4,128]{3,1,2,0:T(8,128)(2,1)S(1)} collective-permute-done((bf16[2,128,4,128]{3,1,2,0:T(8,128)(2,1)S(1)}, bf16[2,128,4,128]{3,1,2,0:T(8,128)(2,1)S(1)}, u32[]{:S(2)}, u32[]{:S(2)}) %collective-permute-start.18) | collective-permute-done | bytes 262176 | tf_op jit(solution)/shard_map/ppermute | solution.py:19
  196.7 1.9 select_reduce_fusion.4
  218.5 2.0 copy.1865
  220.6 2.1 copy.1864
  224.4 2.0 copy.1863
  227.3 2.1 copy.1862
  229.4 1.8 multiply_reduce_fusion
  256.4 3.7 convolution_bitcast_fusion
  260.1 2.6 fusion
  266.4 2.1 copy.1882
  270.1 2.0 copy.1880
  273.0 2.0 copy.1878
  275.9 1.9 broadcast_in_dim.1128
  277.8 2.1 copy.1876
  279.9 4.4 fusion.4
  284.4 2.3 fusion.30
  288.7 2.2 copy.1934
  294.0 2.2 copy.1916
  298.0 2.2 collective-permute-start.29
  301.5 2.1 copy.1896
  304.7 3.7 fusion.65
  311.0 2.1 stack.122
  313.1 2.1 copy.1891
  315.2 2.1 stack.121
  317.3 2.1 copy.1890
  319.4 2.1 copy.1907
  321.5 2.0 copy.1905
  326.2 2.1 collective-permute-start.23
  329.4 25.3 %collective-permute-done.23 = bf16[2,1,128,4,128]{4,2,3,1,0:T(8,128)(2,1)S(1)} collective-permute-done((bf16[2,1,128,4,128]{4,2,3,1,0:T(8,128)(2,1)S(1)}, bf16[2,1,128,4,128]{4,2,3,1,0:T(8,128)(2,1)S(1)}, u32[]{:S(2)}, u32[]{:S(2)}) %collective-permute-start.23) | collective-permute-done | bytes 262176 | tf_op jit(solution)/shard_map/ppermute | solution.py:19
  358.7 3.3 collective-permute-start.26
  363.4 33.2 %collective-permute-done.26 = bf16[2,4,32,4,128]{4,2,1,3,0:T(8,128)(2,1)S(1)} collective-permute-done((bf16[2,4,32,4,128]{4,2,1,3,0:T(8,128)(2,1)S(1)}, bf16[2,4,32,4,128]{4,2,1,3,0:T(8,128)(2,1)S(1)}, u32[]{:S(2)}, u32[]{:S(2)}) %collective-permute-start.26) | collective-permute-done | bytes 262176 | tf_op jit(solution)/shard_map/ppermute | solution.py:19
  397.0 6.0 %collective-permute-done.25 = bf16[2,1,64,4,128]{4,2,3,0,1:T(8,128)(2,1)S(1)} collective-permute-done((bf16[2,1,64,4,128]{4,2,3,0,1:T(8,128)(2,1)S(1)}, bf16[2,1,64,4,128]{4,2,3,0,1:T(8,128)(2,1)S(1)}, u32[]{:S(2)}, u32[]{:S(2)}) %collective-permute-start.25) | collective-permute-done | bytes 131104 | tf_op jit(solution)/shard_map/ppermute | solution.py:19
  403.1 6.4 %collective-permute-done.34 = bf16[2,8,8,4,128]{4,2,3,1,0:T(8,128)(2,1)S(1)} collective-permute-done((bf16[2,8,8,4,128]{4,2,3,1,0:T(8,128)(2,1)S(1)}, bf16[2,8,8,4,128]{4,2,3,1,0:T(8,128)(2,1)S(1)}, u32[]{:S(2)}, u32[]{:S(2)}) %collective-permute-start.34) | collective-permute-done | bytes 131104 | tf_op jit(solution)/shard_map/ppermute | solution.py:19
  409.6 6.4 %collective-permute-done.27 = bf16[2,2,32,4,128]{4,2,3,1,0:T(8,128)(2,1)S(1)} collective-permute-done((bf16[2,2,32,4,128]{4,2,3,1,0:T(8,128)(2,1)S(1)}, bf16[2,2,32,4,128]{4,2,3,1,0:T(8,128)(2,1)S(1)}, u32[]{:S(2)}, u32[]{:S(2)}) %collective-permute-start.27) | collective-permute-done | bytes 131104 | tf_op jit(solution)/shard_map/ppermute | solution.py:19
  416.1 6.4 %collective-permute-done.30 = bf16[2,4,16,4,128]{4,2,3,1,0:T(8,128)(2,1)S(1)} collective-permute-done((bf16[2,4,16,4,128]{4,2,3,1,0:T(8,128)(2,1)S(1)}, bf16[2,4,16,4,128]{4,2,3,1,0:T(8,128)(2,1)S(1)}, u32[]{:S(2)}, u32[]{:S(2)}) %collective-permute-start.30) | collective-permute-done | bytes 131104 | tf_op jit(solution)/shard_map/ppermute | solution.py:19
  422.7 4.0 collective-permute-done.28
  426.8 4.2 collective-permute-done.35
  431.0 4.2 collective-permute-done.31
  437.1 2.9 collective-permute-done.36
  441.8 3.1 collective-permute-done.32
  444.9 3.9 collective-permute-start.37
  450.0 2.5 collective-permute-done.37
  453.2 2.1 fusion.64
  (656 shorter events, 183.7 us)
Async XLA Ops:
  4.1 150.4 %collective-permute-start = (bf16[2,256,4,128]{3,1,2,0:T(8,128)(2,1)}, bf16[2,256,4,128]{3,1,2,0:T(8,128)(2,1)}, u32[]{:S(2)}, u32[]{:S(2)}) collective-permute-start(bf16[2,256,4,128]{3,1,2,0:T(8,128)(2,1)} %pad_maximum_fusion.6), channel_id=1, source_target_pairs={{0,32},{8,40},{16,48},{24,56},{32,64},{40,72},{48,80},{56,88},{64,... | collective-permute-start | bytes 1572872 | tf_op jit(solution)/shard_map/ppermute | solution.py:25
  8.8 146.9 %collective-permute-start.1 = (bf16[2,256,4,128]{3,1,2,0:T(8,128)(2,1)}, bf16[2,256,4,128]{3,1,2,0:T(8,128)(2,1)}, u32[]{:S(2)}, u32[]{:S(2)}) collective-permute-start(bf16[2,256,4,128]{3,1,2,0:T(8,128)(2,1)} %pad_maximum_fusion.6), channel_id=1, source_target_pairs={{0,24},{8,32},{16,40},{24,48},{32,56},{40,64},{48,72},{56,80},{64,... | collective-permute-start | bytes 1572872 | tf_op jit(solution)/shard_map/ppermute | solution.py:25
  17.1 35.8 %collective-permute-start.14 = (bf16[2,8,4,128]{3,1,2,0:T(8,128)(2,1)}, bf16[2,8,4,128]{3,1,2,0:T(8,128)(2,1)}, u32[]{:S(2)}, u32[]{:S(2)}) collective-permute-start(bf16[2,8,4,128]{3,1,2,0:T(8,128)(2,1)} %pad_maximum_fusion.11), channel_id=1, source_target_pairs={{0,8},{8,0},{16,24},{24,16},{32,40},{40,32},{48,56},{56,48},{64,72... | collective-permute-start | bytes 49160 | tf_op jit(solution)/shard_map/ppermute | solution.py:19
  19.9 77.1 %collective-permute-start.4 = (bf16[2,128,4,128]{3,1,2,0:T(8,128)(2,1)}, bf16[2,128,4,128]{3,1,2,0:T(8,128)(2,1)}, u32[]{:S(2)}, u32[]{:S(2)}) collective-permute-start(bf16[2,128,4,128]{3,1,2,0:T(8,128)(2,1)} %pad_maximum_fusion.7), channel_id=1, source_target_pairs={{0,8},{8,0},{16,24},{24,16},{32,40},{40,32},{48,56},{56,48},{64,72... | collective-permute-start | bytes 786440 | tf_op jit(solution)/shard_map/ppermute | solution.py:19
  23.8 95.7 %copy-start.59 = (bf16[64,4,128]{2,1,0:T(4,128)(2,1)}, bf16[64,4,128]{2,1,0:T(4,128)(2,1)S(1)}, u32[]{:S(2)}) copy-start(bf16[64,4,128]{2,1,0:T(4,128)(2,1)S(1)} %get-tuple-element.61) | copy-start | bytes 196612
  24.5 54.5 %collective-permute-start.5 = (bf16[2,64,4,128]{3,1,2,0:T(8,128)(2,1)}, bf16[2,64,4,128]{3,1,2,0:T(8,128)(2,1)}, u32[]{:S(2)}, u32[]{:S(2)}) collective-permute-start(bf16[2,64,4,128]{3,1,2,0:T(8,128)(2,1)} %pad_maximum_fusion.8), channel_id=1, source_target_pairs={{0,8},{8,0},{16,24},{24,16},{32,40},{40,32},{48,56},{56,48},{64,72... | collective-permute-start | bytes 393224 | tf_op jit(solution)/shard_map/ppermute | solution.py:19
  32.6 110.3 %copy-start.61 = (bf16[16,4,128]{2,1,0:T(4,128)(2,1)}, bf16[16,4,128]{2,1,0:T(4,128)(2,1)S(1)}, u32[]{:S(2)}) copy-start(bf16[16,4,128]{2,1,0:T(4,128)(2,1)S(1)} %get-tuple-element.51) | copy-start | bytes 49156
  32.7 22.2 %copy-start.72 = (bf16[1,8,4,128]{3,1,2,0:T(8,128)(2,1)S(1)}, bf16[1,8,4,128]{3,1,2,0:T(8,128)(2,1)}, u32[]{:S(2)}) copy-start(bf16[1,8,4,128]{3,1,2,0:T(8,128)(2,1)} %copy-done.71) | copy-start | bytes 24580
  35.6 46.1 %copy-start.40 = (pred[128,2,4]{1,0,2:T(8,128)(4,1)}, pred[128,2,4]{1,0,2:T(8,128)(4,1)S(1)}, u32[]{:S(2)}) copy-start(pred[128,2,4]{1,0,2:T(8,128)(4,1)S(1)} %broadcast_in_dim.1022) | copy-start | bytes 3076
  40.9 46.6 %copy-start.83 = (pred[256,4]{0,1:T(4,128)(4,1)}, pred[256,4]{0,1:T(4,128)(4,1)S(1)}, u32[]{:S(2)}) copy-start(pred[256,4]{0,1:T(4,128)(4,1)S(1)} %broadcast_in_dim.1015) | copy-start | bytes 3076
  41.0 46.5 %copy-start.85 = (pred[256,4]{0,1:T(4,128)(4,1)}, pred[256,4]{0,1:T(4,128)(4,1)S(1)}, u32[]{:S(2)}) copy-start(pred[256,4]{0,1:T(4,128)(4,1)S(1)} %broadcast_in_dim.1066) | copy-start | bytes 3076
  41.1 46.4 %copy-start.87 = (pred[256,4]{0,1:T(4,128)(4,1)}, pred[256,4]{0,1:T(4,128)(4,1)S(1)}, u32[]{:S(2)}) copy-start(pred[256,4]{0,1:T(4,128)(4,1)S(1)} %broadcast_in_dim.1068) | copy-start | bytes 3076
  41.2 46.3 %copy-start.89 = (pred[256,4]{0,1:T(4,128)(4,1)}, pred[256,4]{0,1:T(4,128)(4,1)S(1)}, u32[]{:S(2)}) copy-start(pred[256,4]{0,1:T(4,128)(4,1)S(1)} %broadcast_in_dim.1070) | copy-start | bytes 3076
  41.4 40.2 %copy-start.81 = (pred[256,4]{0,1:T(4,128)(4,1)}, pred[256,4]{0,1:T(4,128)(4,1)S(1)}, u32[]{:S(2)}) copy-start(pred[256,4]{0,1:T(4,128)(4,1)S(1)} %broadcast_in_dim.1072) | copy-start | bytes 3076
  43.1 56.3 %copy-start.32 = (bf16[128,4,128]{0,2,1:T(8,128)(2,1)}, bf16[128,4,128]{0,2,1:T(8,128)(2,1)S(1)}, u32[]{:S(2)}) copy-start(bf16[128,4,128]{0,2,1:T(8,128)(2,1)S(1)} %copy.1888) | copy-start | bytes 393220
  52.9 3.9 collective-permute-start.10
  56.8 5.4 %collective-permute-start.15 = (bf16[2,16,4,128]{3,1,2,0:T(8,128)(2,1)S(1)}, bf16[2,16,4,128]{3,1,2,0:T(8,128)(2,1)S(1)}, u32[]{:S(2)}, u32[]{:S(2)}) collective-permute-start(bf16[2,16,4,128]{3,1,2,0:T(8,128)(2,1)S(1)} %maximum_select_fusion.14), channel_id=1, source_target_pairs={{0,16},{16,0},{8,24},{24,8},{32,48},{48,32},{40,56},{56,40},{64,80... | collective-permute-start | bytes 98312 | tf_op jit(solution)/shard_map/ppermute | solution.py:19
  62.2 4.3 collective-permute-start.7
  66.6 5.8 %collective-permute-start.11 = (bf16[2,32,4,128]{3,1,2,0:T(8,128)(2,1)S(1)}, bf16[2,32,4,128]{3,1,2,0:T(8,128)(2,1)S(1)}, u32[]{:S(2)}, u32[]{:S(2)}) collective-permute-start(bf16[2,32,4,128]{3,1,2,0:T(8,128)(2,1)S(1)} %maximum_select_fusion.12), channel_id=1, source_target_pairs={{0,16},{16,0},{8,24},{24,8},{32,48},{48,32},{40,56},{56,40},{64,80... | collective-permute-start | bytes 196616 | tf_op jit(solution)/shard_map/ppermute | solution.py:19
  72.3 4.7 %collective-permute-start.16 = (bf16[2,32,4,128]{3,1,2,0:T(8,128)(2,1)S(1)}, bf16[2,32,4,128]{3,1,2,0:T(8,128)(2,1)S(1)}, u32[]{:S(2)}, u32[]{:S(2)}) collective-permute-start(bf16[2,32,4,128]{3,1,2,0:T(8,128)(2,1)S(1)} %maximum_select_fusion.13), channel_id=1, source_target_pairs={{0,32},{32,0},{8,40},{40,8},{16,48},{48,16},{24,56},{56,24},{64,96... | collective-permute-start | bytes 196616 | tf_op jit(solution)/shard_map/ppermute | solution.py:19
  77.0 6.5 %collective-permute-start.8 = (bf16[2,64,4,128]{3,1,2,0:T(8,128)(2,1)S(1)}, bf16[2,64,4,128]{3,1,2,0:T(8,128)(2,1)S(1)}, u32[]{:S(2)}, u32[]{:S(2)}) collective-permute-start(bf16[2,64,4,128]{3,1,2,0:T(8,128)(2,1)S(1)} %maximum_select_fusion.9), channel_id=1, source_target_pairs={{0,16},{16,0},{8,24},{24,8},{32,48},{48,32},{40,56},{56,40},{64,80... | collective-permute-start | bytes 393224 | tf_op jit(solution)/shard_map/ppermute | solution.py:19
  79.0 8.5 %collective-permute-start.12 = (bf16[2,64,4,128]{3,1,2,0:T(8,128)(2,1)S(1)}, bf16[2,64,4,128]{3,1,2,0:T(8,128)(2,1)S(1)}, u32[]{:S(2)}, u32[]{:S(2)}) collective-permute-start(bf16[2,64,4,128]{3,1,2,0:T(8,128)(2,1)S(1)} %maximum_select_fusion.10), channel_id=1, source_target_pairs={{0,32},{32,0},{8,40},{40,8},{16,48},{48,16},{24,56},{56,24},{64,96... | collective-permute-start | bytes 393224 | tf_op jit(solution)/shard_map/ppermute | solution.py:19
  81.7 37.9 %copy-start.101 = (pred[64,256]{1,0:T(8,128)(4,1)S(1)}, pred[64,256]{1,0:T(8,128)(4,1)}, u32[]{:S(2)}) copy-start(pred[64,256]{1,0:T(8,128)(4,1)} %iota_compare_fusion.1) | copy-start | bytes 49156
  83.5 10.8 %collective-permute-start.17 = (bf16[2,64,4,128]{3,1,2,0:T(8,128)(2,1)S(1)}, bf16[2,64,4,128]{3,1,2,0:T(8,128)(2,1)S(1)}, u32[]{:S(2)}, u32[]{:S(2)}) collective-permute-start(bf16[2,64,4,128]{3,1,2,0:T(8,128)(2,1)S(1)} %maximum_select_fusion.11), channel_id=1, source_target_pairs={{0,64},{64,0},{8,72},{72,8},{16,80},{80,16},{24,88},{88,24},{32,96... | collective-permute-start | bytes 393224 | tf_op jit(solution)/shard_map/ppermute | solution.py:19
  87.5 69.3 %collective-permute-start.2 = (bf16[2,256,4,128]{3,1,2,0:T(8,128)(2,1)}, bf16[2,256,4,128]{3,1,2,0:T(8,128)(2,1)}, u32[]{:S(2)}, u32[]{:S(2)}) collective-permute-start(bf16[2,256,4,128]{3,1,2,0:T(8,128)(2,1)} %pad_maximum_fusion.6), channel_id=1, source_target_pairs={{0,16},{8,24},{16,32},{24,40},{32,48},{40,56},{48,64},{56,72},{64,... | collective-permute-start | bytes 1572872 | tf_op jit(solution)/shard_map/ppermute | solution.py:25
  94.3 63.6 %collective-permute-start.3 = (bf16[2,256,4,128]{3,1,2,0:T(8,128)(2,1)}, bf16[2,256,4,128]{3,1,2,0:T(8,128)(2,1)}, u32[]{:S(2)}, u32[]{:S(2)}) collective-permute-start(bf16[2,256,4,128]{3,1,2,0:T(8,128)(2,1)} %pad_maximum_fusion.6), channel_id=1, source_target_pairs={{0,8},{8,16},{16,24},{24,32},{32,40},{40,48},{48,56},{56,64},{64,7... | collective-permute-start | bytes 1572872 | tf_op jit(solution)/shard_map/ppermute | solution.py:25
  97.0 30.3 %copy-start.64 = (bf16[32,4,128]{2,1,0:T(4,128)(2,1)S(1)}, bf16[32,4,128]{2,1,0:T(4,128)(2,1)}, u32[]{:S(2)}) copy-start(bf16[32,4,128]{2,1,0:T(4,128)(2,1)} %get-tuple-element.67) | copy-start | bytes 98308
  97.0 30.3 %copy-start.113 = (pred[32,256]{1,0:T(8,128)(4,1)S(1)}, pred[32,256]{1,0:T(8,128)(4,1)}, u32[]{:S(2)}) copy-start(pred[32,256]{1,0:T(8,128)(4,1)} %iota_compare_fusion.2) | copy-start | bytes 24580
  97.0 14.7 %collective-permute-start.6 = (bf16[2,128,4,128]{3,1,2,0:T(8,128)(2,1)S(1)}, bf16[2,128,4,128]{3,1,2,0:T(8,128)(2,1)S(1)}, u32[]{:S(2)}, u32[]{:S(2)}) collective-permute-start(bf16[2,128,4,128]{3,1,2,0:T(8,128)(2,1)S(1)} %maximum_select_fusion.5), channel_id=1, source_target_pairs={{0,16},{16,0},{8,24},{24,8},{32,48},{48,32},{40,56},{56,40},{64,80... | collective-permute-start | bytes 786440 | tf_op jit(solution)/shard_map/ppermute | solution.py:19
  100.5 42.4 %copy-start.99 = (pred[16,256]{1,0:T(8,128)(4,1)S(1)}, pred[16,256]{1,0:T(8,128)(4,1)}, u32[]{:S(2)}) copy-start(pred[16,256]{1,0:T(8,128)(4,1)} %iota_compare_fusion.3) | copy-start | bytes 12292
  111.7 13.5 %collective-permute-start.9 = (bf16[2,128,4,128]{3,1,2,0:T(8,128)(2,1)S(1)}, bf16[2,128,4,128]{3,1,2,0:T(8,128)(2,1)S(1)}, u32[]{:S(2)}, u32[]{:S(2)}) collective-permute-start(bf16[2,128,4,128]{3,1,2,0:T(8,128)(2,1)S(1)} %maximum_select_fusion.6), channel_id=1, source_target_pairs={{0,32},{32,0},{8,40},{40,8},{16,48},{48,16},{24,56},{56,24},{64,96... | collective-permute-start | bytes 786440 | tf_op jit(solution)/shard_map/ppermute | solution.py:19
  119.5 33.2 %copy-start.69 = (bf16[8,4,128]{2,1,0:T(4,128)(2,1)S(1)}, bf16[8,4,128]{2,1,0:T(4,128)(2,1)}, u32[]{:S(2)}) copy-start(bf16[8,4,128]{2,1,0:T(4,128)(2,1)} %get-tuple-element.47) | copy-start | bytes 24580
  119.5 33.2 %copy-start.106 = (pred[8,256]{1,0:T(8,128)(4,1)S(1)}, pred[8,256]{1,0:T(8,128)(4,1)}, u32[]{:S(2)}) copy-start(pred[8,256]{1,0:T(8,128)(4,1)} %iota_compare_fusion.4) | copy-start | bytes 6148
  125.2 15.7 %collective-permute-start.13 = (bf16[2,128,4,128]{3,1,2,0:T(8,128)(2,1)S(1)}, bf16[2,128,4,128]{3,1,2,0:T(8,128)(2,1)S(1)}, u32[]{:S(2)}, u32[]{:S(2)}) collective-permute-start(bf16[2,128,4,128]{3,1,2,0:T(8,128)(2,1)S(1)} %maximum_select_fusion.7), channel_id=1, source_target_pairs={{0,64},{64,0},{8,72},{72,8},{16,80},{80,16},{24,88},{88,24},{32,96... | collective-permute-start | bytes 786440 | tf_op jit(solution)/shard_map/ppermute | solution.py:19
  141.0 11.6 %collective-permute-start.18 = (bf16[2,128,4,128]{3,1,2,0:T(8,128)(2,1)S(1)}, bf16[2,128,4,128]{3,1,2,0:T(8,128)(2,1)S(1)}, u32[]{:S(2)}, u32[]{:S(2)}) collective-permute-start(bf16[2,128,4,128]{3,1,2,0:T(8,128)(2,1)S(1)} %maximum_select_fusion.8), channel_id=1, source_target_pairs={{0,128},{128,0},{8,136},{136,8},{16,144},{144,16},{24,152},{152,24... | collective-permute-start | bytes 786440 | tf_op jit(solution)/shard_map/ppermute | solution.py:19
  292.7 33.5 %collective-permute-start.33 = (bf16[2,16,8,4,128]{4,2,1,3,0:T(8,128)(2,1)}, bf16[2,16,8,4,128]{4,2,1,3,0:T(8,128)(2,1)}, u32[]{:S(2)}, u32[]{:S(2)}) collective-permute-start(bf16[2,16,8,4,128]{4,2,1,3,0:T(8,128)(2,1)} %fusion.95), channel_id=1, source_target_pairs={{0,8},{8,0},{16,24},{24,16},{32,40},{40,32},{48,56},{56,48},{64,72... | collective-permute-start | bytes 786440 | tf_op jit(solution)/shard_map/ppermute | solution.py:19
  298.0 58.2 %collective-permute-start.29 = (bf16[2,8,16,4,128]{4,2,1,3,0:T(8,128)(2,1)}, bf16[2,8,16,4,128]{4,2,1,3,0:T(8,128)(2,1)}, u32[]{:S(2)}, u32[]{:S(2)}) collective-permute-start(bf16[2,8,16,4,128]{4,2,1,3,0:T(8,128)(2,1)} %fusion.94), channel_id=1, source_target_pairs={{0,8},{8,0},{16,24},{24,16},{32,40},{40,32},{48,56},{56,48},{64,72... | collective-permute-start | bytes 786440 | tf_op jit(solution)/shard_map/ppermute | solution.py:19
  304.6 54.1 %collective-permute-start.24 = (bf16[2,2,64,4,128]{4,2,1,3,0:T(8,128)(2,1)S(1)}, bf16[2,2,64,4,128]{4,2,1,3,0:T(8,128)(2,1)}, u32[]{:S(2)}, u32[]{:S(2)}) collective-permute-start(bf16[2,2,64,4,128]{4,2,1,3,0:T(8,128)(2,1)S(1)} %fusion.92), channel_id=1, source_target_pairs={{0,8},{8,0},{16,24},{24,16},{32,40},{40,32},{48,56},{56,48},{64,72... | collective-permute-start | bytes 786440 | tf_op jit(solution)/shard_map/ppermute | solution.py:19
  308.4 144.8 %collective-permute-start.22 = (f32[2,256,4,128]{1,3,2,0:T(8,128)}, f32[2,256,4,128]{1,3,2,0:T(8,128)}, u32[]{:S(2)}, u32[]{:S(2)}) collective-permute-start(f32[2,256,4,128]{1,3,2,0:T(8,128)} %get-tuple-element.97), channel_id=1, source_target_pairs={{32,0},{40,8},{48,16},{56,24},{64,32},{72,40},{80,48},{88,56},{96,... | collective-permute-start | bytes 3145736 | tf_op jit(solution)/shard_map/ppermute | solution.py:25
  309.7 143.5 %collective-permute-start.21 = (f32[2,256,4,128]{1,3,2,0:T(8,128)}, f32[2,256,4,128]{1,3,2,0:T(8,128)}, u32[]{:S(2)}, u32[]{:S(2)}) collective-permute-start(f32[2,256,4,128]{1,3,2,0:T(8,128)} %get-tuple-element.98), channel_id=1, source_target_pairs={{24,0},{32,8},{40,16},{48,24},{56,32},{64,40},{72,48},{80,56},{88,... | collective-permute-start | bytes 3145736 | tf_op jit(solution)/shard_map/ppermute | solution.py:25
  323.5 31.2 %copy-start.35 = (f32[2,256,4,128]{1,3,2,0:T(8,128)S(1)}, f32[2,256,4,128]{1,3,2,0:T(8,128)}, u32[]{:S(2)}) copy-start(f32[2,256,4,128]{1,3,2,0:T(8,128)} %get-tuple-element.96) | copy-start | bytes 3145732
  323.5 32.5 %copy-start.19 = (f32[1,1,2,128,4,128]{5,3,4,0,2,1:T(8,128)S(1)}, f32[1,1,2,128,4,128]{5,3,4,0,2,1:T(8,128)}, u32[]{:S(2)}) copy-start(f32[1,1,2,128,4,128]{5,3,4,0,2,1:T(8,128)} %copy.1891) | copy-start | bytes 1572868
  323.5 32.5 %copy-start.20 = (f32[1,1,2,128,4,128]{5,3,4,0,2,1:T(8,128)S(1)}, f32[1,1,2,128,4,128]{5,3,4,0,2,1:T(8,128)}, u32[]{:S(2)}) copy-start(f32[1,1,2,128,4,128]{5,3,4,0,2,1:T(8,128)} %copy.1890) | copy-start | bytes 1572868
  326.2 30.0 %copy-start.34 = (f32[2,256,4,128]{1,3,2,0:T(8,128)S(1)}, f32[2,256,4,128]{1,3,2,0:T(8,128)}, u32[]{:S(2)}) copy-start(f32[2,256,4,128]{1,3,2,0:T(8,128)} %get-tuple-element.95) | copy-start | bytes 3145732
  326.2 31.4 %copy-start.12 = (f32[256,4,128]{2,0,1:T(8,128)S(1)}, f32[256,4,128]{2,0,1:T(8,128)}, u32[]{:S(2)}) copy-start(f32[256,4,128]{2,0,1:T(8,128)} %copy-done.11) | copy-start | bytes 1572868
  326.2 31.4 %copy-start.13 = (f32[256,4,128]{2,0,1:T(8,128)S(1)}, f32[256,4,128]{2,0,1:T(8,128)}, u32[]{:S(2)}) copy-start(f32[256,4,128]{2,0,1:T(8,128)} %copy.1916) | copy-start | bytes 1572868
  326.2 28.5 %collective-permute-start.23 = (bf16[2,1,128,4,128]{4,2,3,1,0:T(8,128)(2,1)S(1)}, bf16[2,1,128,4,128]{4,2,3,1,0:T(8,128)(2,1)S(1)}, u32[]{:S(2)}, u32[]{:S(2)}) collective-permute-start(bf16[2,1,128,4,128]{4,2,3,1,0:T(8,128)(2,1)S(1)} %fusion.91), channel_id=1, source_target_pairs={{0,8},{8,0},{16,24},{24,16},{32,40},{40,32},{48,56},{56,48},{64,72... | collective-permute-start | bytes 786440 | tf_op jit(solution)/shard_map/ppermute | solution.py:19
  329.4 32.7 %copy-start.10 = (f32[256,4,128]{2,0,1:T(8,128)S(1)}, f32[256,4,128]{2,0,1:T(8,128)}, u32[]{:S(2)}) copy-start(f32[256,4,128]{2,0,1:T(8,128)} %copy.1896) | copy-start | bytes 1572868
  354.8 98.4 %collective-permute-start.20 = (f32[2,256,4,128]{1,3,2,0:T(8,128)S(1)}, f32[2,256,4,128]{1,3,2,0:T(8,128)S(1)}, u32[]{:S(2)}, u32[]{:S(2)}) collective-permute-start(f32[2,256,4,128]{1,3,2,0:T(8,128)S(1)} %copy-done.35), channel_id=1, source_target_pairs={{16,0},{24,8},{32,16},{40,24},{48,32},{56,40},{64,48},{72,56},{80,... | collective-permute-start | bytes 3145736 | tf_op jit(solution)/shard_map/ppermute | solution.py:25
  356.2 40.4 %copy-start.14 = (f32[256,4,128]{2,0,1:T(8,128)S(1)}, f32[256,4,128]{2,0,1:T(8,128)}, u32[]{:S(2)}) copy-start(f32[256,4,128]{2,0,1:T(8,128)} %copy.1907) | copy-start | bytes 1572868
  356.2 40.3 %copy-start.15 = (f32[256,4,128]{2,0,1:T(8,128)S(1)}, f32[256,4,128]{2,0,1:T(8,128)}, u32[]{:S(2)}) copy-start(f32[256,4,128]{2,0,1:T(8,128)} %copy.1905) | copy-start | bytes 1572868
  356.2 97.0 %collective-permute-start.19 = (f32[2,256,4,128]{1,3,2,0:T(8,128)S(1)}, f32[2,256,4,128]{1,3,2,0:T(8,128)S(1)}, u32[]{:S(2)}, u32[]{:S(2)}) collective-permute-start(f32[2,256,4,128]{1,3,2,0:T(8,128)S(1)} %copy-done.34), channel_id=1, source_target_pairs={{8,0},{16,8},{24,16},{32,24},{40,32},{48,40},{56,48},{64,56},{72,6... | collective-permute-start | bytes 3145736 | tf_op jit(solution)/shard_map/ppermute | solution.py:25
  358.7 37.8 %collective-permute-start.26 = (bf16[2,4,32,4,128]{4,2,1,3,0:T(8,128)(2,1)S(1)}, bf16[2,4,32,4,128]{4,2,1,3,0:T(8,128)(2,1)S(1)}, u32[]{:S(2)}, u32[]{:S(2)}) collective-permute-start(bf16[2,4,32,4,128]{4,2,1,3,0:T(8,128)(2,1)S(1)} %fusion.93), channel_id=1, source_target_pairs={{0,8},{8,0},{16,24},{24,16},{32,40},{40,32},{48,56},{56,48},{64,72... | collective-permute-start | bytes 786440 | tf_op jit(solution)/shard_map/ppermute | solution.py:19
  396.6 6.5 %collective-permute-start.25 = (bf16[2,1,64,4,128]{4,2,3,0,1:T(8,128)(2,1)S(1)}, bf16[2,1,64,4,128]{4,2,3,0,1:T(8,128)(2,1)S(1)}, u32[]{:S(2)}, u32[]{:S(2)}) collective-permute-start(bf16[2,1,64,4,128]{4,2,3,0,1:T(8,128)(2,1)S(1)} %fusion.108), channel_id=1, source_target_pairs={{0,16},{16,0},{8,24},{24,8},{32,48},{48,32},{40,56},{56,40},{64,80... | collective-permute-start | bytes 393224 | tf_op jit(solution)/shard_map/ppermute | solution.py:19
  403.0 6.5 %collective-permute-start.34 = (bf16[2,8,8,4,128]{4,2,3,1,0:T(8,128)(2,1)S(1)}, bf16[2,8,8,4,128]{4,2,3,1,0:T(8,128)(2,1)S(1)}, u32[]{:S(2)}, u32[]{:S(2)}) collective-permute-start(bf16[2,8,8,4,128]{4,2,3,1,0:T(8,128)(2,1)S(1)} %fusion.111), channel_id=1, source_target_pairs={{0,16},{16,0},{8,24},{24,8},{32,48},{48,32},{40,56},{56,40},{64,80... | collective-permute-start | bytes 393224 | tf_op jit(solution)/shard_map/ppermute | solution.py:19
  409.5 6.5 %collective-permute-start.27 = (bf16[2,2,32,4,128]{4,2,3,1,0:T(8,128)(2,1)S(1)}, bf16[2,2,32,4,128]{4,2,3,1,0:T(8,128)(2,1)S(1)}, u32[]{:S(2)}, u32[]{:S(2)}) collective-permute-start(bf16[2,2,32,4,128]{4,2,3,1,0:T(8,128)(2,1)S(1)} %fusion.109), channel_id=1, source_target_pairs={{0,16},{16,0},{8,24},{24,8},{32,48},{48,32},{40,56},{56,40},{64,80... | collective-permute-start | bytes 393224 | tf_op jit(solution)/shard_map/ppermute | solution.py:19
  416.0 6.5 %collective-permute-start.30 = (bf16[2,4,16,4,128]{4,2,3,1,0:T(8,128)(2,1)S(1)}, bf16[2,4,16,4,128]{4,2,3,1,0:T(8,128)(2,1)S(1)}, u32[]{:S(2)}, u32[]{:S(2)}) collective-permute-start(bf16[2,4,16,4,128]{4,2,3,1,0:T(8,128)(2,1)S(1)} %fusion.110), channel_id=1, source_target_pairs={{0,16},{16,0},{8,24},{24,8},{32,48},{48,32},{40,56},{56,40},{64,80... | collective-permute-start | bytes 393224 | tf_op jit(solution)/shard_map/ppermute | solution.py:19
  416.0 37.2 %copy-start.1 = (f32[1,1280,4,128]{1,3,2,0:T(8,128)S(1)}, f32[1,1280,4,128]{1,3,2,0:T(8,128)}, u32[]{:S(2)}) copy-start(f32[1,1280,4,128]{1,3,2,0:T(8,128)} %fusion.4) | copy-start | bytes 7864324
  422.4 4.3 collective-permute-start.28
  426.7 4.3 collective-permute-start.35
  431.0 4.3 collective-permute-start.31
  435.2 4.8 %collective-permute-start.36 = (bf16[2,2,8,4,128]{4,2,3,1,0:T(8,128)(2,1)S(1)}, bf16[2,2,8,4,128]{4,2,3,1,0:T(8,128)(2,1)S(1)}, u32[]{:S(2)}, u32[]{:S(2)}) collective-permute-start(bf16[2,2,8,4,128]{4,2,3,1,0:T(8,128)(2,1)S(1)} %fusion.142), channel_id=1, source_target_pairs={{0,64},{64,0},{8,72},{72,8},{16,80},{80,16},{24,88},{88,24},{32,96... | collective-permute-start | bytes 98312 | tf_op jit(solution)/shard_map/ppermute | solution.py:19
  440.1 4.8 %collective-permute-start.32 = (bf16[2,1,16,4,128]{4,2,3,0,1:T(8,128)(2,1)S(1)}, bf16[2,1,16,4,128]{4,2,3,0,1:T(8,128)(2,1)S(1)}, u32[]{:S(2)}, u32[]{:S(2)}) collective-permute-start(bf16[2,1,16,4,128]{4,2,3,0,1:T(8,128)(2,1)S(1)} %fusion.141), channel_id=1, source_target_pairs={{0,64},{64,0},{8,72},{72,8},{16,80},{80,16},{24,88},{88,24},{32,96... | collective-permute-start | bytes 98312 | tf_op jit(solution)/shard_map/ppermute | solution.py:19
  444.9 7.6 %collective-permute-start.37 = (bf16[2,1,8,4,128]{4,2,3,0,1:T(8,128)(2,1)S(1)}, bf16[2,1,8,4,128]{4,2,3,0,1:T(8,128)(2,1)S(1)}, u32[]{:S(2)}, u32[]{:S(2)}) collective-permute-start(bf16[2,1,8,4,128]{4,2,3,0,1:T(8,128)(2,1)S(1)} %fusion.156), channel_id=1, source_target_pairs={{0,128},{128,0},{8,136},{136,8},{16,144},{144,16},{24,152},{152,24... | collective-permute-start | bytes 49160 | tf_op jit(solution)/shard_map/ppermute | solution.py:19
  (103 other events, 662.3 us)
where the time goes:
time: 467 us; the launch traced here: 459 us
  waiting for transfers between devices  157 us (34%)
  local copies, waits for them, and re-layouts  123 us (26%)
  starting transfers between devices  71.2 us (15%)
  other arithmetic  65.2 us (14%)
  matrix products  39.7 us (9%)
    ppermute x30, waiting for transfers between devices, from_partner(): return lax.ppermute(block, axis, route)  156 us
    ppermute x30, starting transfers between devices, from_partner(): return lax.ppermute(block, axis, route)  46.5 us
    broadcast_in_dim x72, local copies, waits for them, and re-layouts, put_rows(): jnp.where(row_mask(source, chosen), update[:, None], shaped)  33.5 us
    ppermute x8, starting transfers between devices, passed_along(): lax.ppermute(value, axis, [(source, source + steps) for source in range(l...  24.7 us
    reduce_sum x32, other arithmetic, pick_rows(): jnp.sum(jnp.where(row_mask(source, chosen), shaped, jnp.zeros((), source....  22.2 us
    broadcast_in_dim x33, local copies, waits for them, and re-layouts, add_rows(): jnp.where(row_mask(source, chosen), update[:, None], 0.0)  19.4 us
    unnamed x268, local copies, waits for them, and re-layouts  13.2 us
    reshape x18, local copies, waits for them, and re-layouts, pick_rows(): source.reshape((source.shape[0] // stride, stride) + source.shape[1:])  12.3 us
  transfers between devices with their start and end apart: 38, of which 22 were waited for; matrix products, arithmetic and copies ran while one was open for 18% of the time, Pallas kernels for 0%

commit v1 on v0

v1 whole, which is shorter than its diff:
```python
import functools

import jax
import jax.numpy as jnp
from jax import lax
from jax.experimental import pallas as pl
from jax.experimental.pallas import tpu as pltpu
from jax.sharding import PartitionSpec as P

COLS = 4
SLAB = 256
HD = 128
ROW = COLS * SLAB
SPAN = ROW + SLAB
NEG = -1e30
SCALE = HD**-0.5
LOG2E = 1.4426950408889634
FAR8 = ROW // 8
FAR16 = ROW // 16
FARK = FAR8 + 6 * FAR16
F32 = jnp.float32
BF16 = jnp.bfloat16


def across(value, step, planes):
    pairs = [
        (p * COLS + c, p * COLS + (c + step) % COLS) for p in range(planes) for c in range(COLS)
    ]
    return lax.ppermute(value, "seq", pairs)


def along(value, step, planes):
    pairs = [
        (p * COLS + c, (p + step) * COLS + c)
        for p in range(planes)
        for c in range(COLS)
        if 0 <= p + step < planes
    ]
    return lax.ppermute(value, "seq", pairs)


def place():
    pos = lax.axis_index("seq")
    return pos // COLS, pos % COLS


def mm(left, right, dims):
    return lax.dot_general(left, right, (dims, ((), ())), preferred_element_type=F32)


def nn(left, right):
    return mm(left, right, ((1,), (0,)))


def nt(left, right):
    return mm(left, right, ((1,), (1,)))


def tn(left, right):
    return mm(left, right, ((0,), (0,)))


def call(kernel, out, scratch=(), flops=1000000, smem=(), nin=0):
    specs = [
        pl.BlockSpec(memory_space=pltpu.SMEM if i in smem else pltpu.VMEM) for i in range(nin)
    ]
    return pl.pallas_call(
        kernel,
        out_shape=out,
        in_specs=specs,
        out_specs=jax.tree.map(lambda _: pl.BlockSpec(memory_space=pltpu.VMEM), out),
        scratch_shapes=scratch,
        compiler_params=pltpu.CompilerParams(vmem_limit_bytes=48 << 20),
        cost_estimate=pl.CostEstimate(flops=flops, bytes_accessed=2 << 20, transcendentals=0),
    )


def pack_kernel(one_ref, two_ref, *out_refs):
    _, col = place()
    for step in range(COLS):
        lanes = pl.ds(pl.multiple_of(((col + step) % COLS) * HD, HD), HD)
        out_refs[step][0] = one_ref[:, lanes]
        out_refs[step][1] = two_ref[:, lanes]


def pack(one, two):
    piece = jax.ShapeDtypeStruct((2, SLAB, HD), BF16)
    return call(pack_kernel, [piece] * COLS, nin=2)(one, two)


def pick(stride, rest, rows, width):
    r = lax.broadcasted_iota(jnp.int32, (rows, width), 0)
    c = lax.broadcasted_iota(jnp.int32, (rows, width), 1)
    return (c == r * stride + rest).astype(BF16)


def thin_kernel(off_ref, *refs):
    _, col = place()
    chosen = pick(16, off_ref[col] % 16, SLAB // 16, SLAB)
    out_ref = refs[COLS]
    for step in range(COLS):
        rows = pl.ds(pl.multiple_of(((col - step + COLS) % COLS) * (SLAB // 16), 16), SLAB // 16)
        for which in range(2):
            out_ref[which, rows] = nn(chosen, refs[step][which]).astype(BF16)


def thin(offsets, pieces):
    out = jax.ShapeDtypeStruct((2, FAR16, HD), BF16)
    return call(thin_kernel, out, smem=(0,), nin=1 + COLS)(offsets, *pieces)


def depth_of(index, off):
    rest = (index - off + 32768) % 32
    total = jnp.zeros(index.shape, F32)
    for level in range(1, 6):
        total = total + (rest % (2**level) == 0).astype(F32)
    return total


def main_kernel(*refs):
    off_ref = refs[0]
    kv = refs[1:5]
    qg = refs[5:9]
    pv = refs[9:13]
    g2_ref, g4_ref, g6_ref = refs[13:16]
    dq_out = refs[16:20]
    prev_out, h2_ref, h4_ref, h6_ref, own_ref = refs[20:25]
    (kk, vv, qq, gg, sc, ctab, m_b, l_b, o_b, d_b, dq, dk, dv, kf, vf) = refs[25:]
    plane, col = place()
    off = off_ref[col]
    for step in range(COLS):
        slab = (col - step + COLS) % COLS
        rows = pl.ds(pl.multiple_of(slab * SLAB, SLAB), SLAB)
        late = pl.ds(pl.multiple_of(slab * SLAB + ROW, SLAB), SLAB)
        kk[late] = kv[step][0]
        vv[late] = kv[step][1]
        kk[rows] = pv[step][0]
        vv[rows] = pv[step][1]
        qq[rows] = qg[step][0]
        gg[rows] = qg[step][1]

    deep_q = depth_of(lax.broadcasted_iota(jnp.int32, (SLAB, SLAB), 0), off)
    deep_k = depth_of(lax.broadcasted_iota(jnp.int32, (SLAB, SLAB), 1), off)
    both = jnp.minimum(deep_q, deep_k)
    ctab[0] = jnp.ones((SLAB, SLAB), F32)
    ctab[1] = 1.0 + jnp.maximum(both - 1.0, 0.0)
    ctab[2] = 1.0 + both

    rest8 = off % 8
    thin8 = pick(8, rest8, SLAB // 8, SLAB)

    def thinned(ref):
        parts = [nn(thin8, ref[pl.ds(b * SLAB, SLAB), :]) for b in range(COLS)]
        return jnp.concatenate(parts, axis=0).astype(BF16)

    kf[pl.ds(0, FAR8)] = thinned(kk)
    vf[pl.ds(0, FAR8)] = thinned(vv)
    for i, g_ref in enumerate((g2_ref, g4_ref, g6_ref)):
        for j in range(2):
            rows = pl.ds(FAR8 + (2 * i + j) * FAR16, FAR16)
            kf[rows] = g_ref[j, 0]
            vf[rows] = g_ref[j, 1]
    qs = thinned(qq)
    gs = thinned(gg)
    c = lax.broadcasted_iota(jnp.int32, (FAR8, FARK), 1)
    r = lax.broadcasted_iota(jnp.int32, (FAR8, FARK), 0)
    far = c - FAR8
    back = jnp.where(c < FAR8, 1, 2 + far // FAR16)
    spot = jnp.where(c < FAR8, c * 8 + rest8, (far % FAR16) * 16 + off % 16)
    other = plane - back
    first = jnp.where(
        other < 0,
        9,
        jnp.where(other // 2 == plane // 2, 3, jnp.where(other // 4 == plane // 4, 4, 5)),
    )
    deep = jnp.minimum(depth_of(r * 8 + rest8, off), depth_of(spot, off))
    times = jnp.maximum(deep - first.astype(F32) + 1.0, 0.0)
    s_far = jnp.where(times > 0.0, nt(qs, kf[...]), NEG)
    m_far = jnp.max(s_far, axis=1, keepdims=True)
    e_far = jnp.exp2((s_far - m_far) * (SCALE * LOG2E)) * times
    l_far = jnp.sum(e_far, axis=1, keepdims=True)
    o_far = nn(e_far.astype(BF16), vf[...])
    strided = pl.ds(rest8, FAR8, stride=8)
    m_b[...] = jnp.full((ROW, HD), NEG, F32)
    l_b[...] = jnp.zeros((ROW, HD), F32)
    o_b[...] = jnp.zeros((ROW, HD), F32)
    m_b[strided, :] = jnp.broadcast_to(m_far, (FAR8, HD))
    l_b[strided, :] = jnp.broadcast_to(l_far, (FAR8, HD))
    o_b[strided, :] = o_far
    dk[...] = jnp.zeros((2 * ROW, HD), F32)
    dv[...] = jnp.zeros((2 * ROW, HD), F32)
    lost = jnp.where(plane > 0, 0.0, NEG)

    def block(qb, carry):
        rows = pl.ds(pl.multiple_of(qb * SLAB, SLAB), SLAB)
        q = qq[rows]
        g = gg[rows]
        i = lax.broadcasted_iota(jnp.int32, (SLAB, SLAB), 0)
        j = lax.broadcasted_iota(jnp.int32, (SLAB, SLAB), 1)
        m_old = m_b[rows][:, :1]
        m = m_old
        for b in range(COLS + 1):
            cols = pl.ds(pl.multiple_of((qb + b) * SLAB, SLAB), SLAB)
            s = nt(q, kk[cols])
            if b < COLS:
                s = s + jnp.where(qb + b < COLS, lost, 0.0)
            if b == 0:
                s = jnp.where(j > i, s, NEG)
            if b == COLS:
                s = jnp.where(j <= i, s, NEG)
            sc[b] = s
            m = jnp.maximum(m, jnp.max(s, axis=1, keepdims=True))
        fade = jnp.exp2((m_old - m) * (SCALE * LOG2E))
        total = l_b[rows][:, :1] * fade
        out = o_b[rows] * fade
        for b in range(COLS + 1):
            cols = pl.ds(pl.multiple_of((qb + b) * SLAB, SLAB), SLAB)
            e = jnp.exp2((sc[b] - m) * (SCALE * LOG2E))
            if b > 0:
                same = (qb + b - COLS) // 2 == qb // 2
                e = e * ctab[jnp.where(qb + b < COLS, 0, jnp.where(same, 2, 1))]
            sc[b] = e
            total = total + jnp.sum(e, axis=1, keepdims=True)
            out = out + nn(e.astype(BF16), vv[cols])
        inv = 1.0 / total
        dot = jnp.sum(g.astype(F32) * out, axis=1, keepdims=True) * inv
        m_b[rows] = jnp.broadcast_to(m, (SLAB, HD))
        l_b[rows] = jnp.broadcast_to(inv, (SLAB, HD))
        d_b[rows] = jnp.broadcast_to(dot, (SLAB, HD))
        dq_acc = jnp.zeros((SLAB, HD), F32)
        for b in range(COLS + 1):
            cols = pl.ds(pl.multiple_of((qb + b) * SLAB, SLAB), SLAB)
            p = sc[b] * inv
            dv[cols] += tn(p.astype(BF16), g)
            ds = (p * (nt(g, vv[cols]) - dot)).astype(BF16)
            dq_acc = dq_acc + nn(ds, kk[cols])
            dk[cols] += tn(ds, q)
        dq[rows] = dq_acc
        return carry

    lax.fori_loop(0, COLS, block, 0)

    m_s = m_b[strided, :][:, :1]
    i_s = l_b[strided, :][:, :1]
    d_s = d_b[strided, :][:, :1]
    p = jnp.exp2((s_far - m_s) * (SCALE * LOG2E)) * times * i_s
    ds = (p * (nt(gs, vf[...]) - d_s)).astype(BF16)
    dk_far = tn(ds, qs)
    dv_far = tn(p.astype(BF16), gs)
    dq[strided, :] = dq[strided, :] + nn(ds, kf[...])
    dk[strided, :] = dk[strided, :] + dk_far[:FAR8]
    dv[strided, :] = dv[strided, :] + dv_far[:FAR8]
    for i, h_ref in enumerate((h2_ref, h4_ref, h6_ref)):
        for j in range(2):
            lo = FAR8 + (2 * i + j) * FAR16
            h_ref[j, 0] = dk_far[lo : lo + FAR16].astype(BF16)
            h_ref[j, 1] = dv_far[lo : lo + FAR16].astype(BF16)
    prev_out[0] = dk[pl.ds(0, ROW), :].astype(BF16)
    prev_out[1] = dv[pl.ds(0, ROW), :].astype(BF16)
    own_ref[0] = dk[pl.ds(ROW, ROW), :]
    own_ref[1] = dv[pl.ds(ROW, ROW), :]
    for step in range(COLS):
        rows = pl.ds(pl.multiple_of(((col + step) % COLS) * SLAB, SLAB), SLAB)
        dq_out[step][...] = (dq[rows] * SCALE).astype(BF16)


def main(offsets, kv, qg, pv, far):
    part = jax.ShapeDtypeStruct((SLAB, HD), BF16)
    pair = jax.ShapeDtypeStruct((2, 2, FAR16, HD), BF16)
    out = [part] * COLS + [
        jax.ShapeDtypeStruct((2, ROW, HD), BF16),
        pair,
        pair,
        pair,
        jax.ShapeDtypeStruct((2, ROW, HD), F32),
    ]
    scratch = [
        pltpu.VMEM((2 * ROW, HD), BF16),
        pltpu.VMEM((2 * ROW, HD), BF16),
        pltpu.VMEM((ROW, HD), BF16),
        pltpu.VMEM((ROW, HD), BF16),
        pltpu.VMEM((COLS + 1, SLAB, SLAB), F32),
        pltpu.VMEM((3, SLAB, SLAB), F32),
        pltpu.VMEM((ROW, HD), F32),
        pltpu.VMEM((ROW, HD), F32),
        pltpu.VMEM((ROW, HD), F32),
        pltpu.VMEM((ROW, HD), F32),
        pltpu.VMEM((ROW, HD), F32),
        pltpu.VMEM((2 * ROW, HD), F32),
        pltpu.VMEM((2 * ROW, HD), F32),
        pltpu.VMEM((FARK, HD), BF16),
        pltpu.VMEM((FARK, HD), BF16),
    ]
    return call(main_kernel, out, scratch, flops=2000000000, smem=(0,), nin=16)(
        offsets, *kv, *qg, *pv, *far
    )


def join_kernel(off_ref, own_ref, near_ref, a2_ref, a4_ref, a6_ref, b1_ref, *refs):
    out = refs[:COLS]
    acc = refs[COLS]
    _, col = place()
    strided = pl.ds(off_ref[col] % 16, FAR16, stride=16)
    for which in range(2):
        acc[...] = own_ref[which] + near_ref[which].astype(F32)
        extra = b1_ref[which].astype(F32)
        for ref in (a2_ref, a4_ref, a6_ref):
            extra = extra + ref[0, which].astype(F32)
        acc[strided, :] = acc[strided, :] + extra
        for step in range(COLS):
            rows = pl.ds(pl.multiple_of(((col + step) % COLS) * SLAB, SLAB), SLAB)
            value = acc[rows]
            if which == 0:
                value = value * SCALE
            out[step][which] = value.astype(BF16)


def join(offsets, own, near, a2, a4, a6, b1):
    piece = jax.ShapeDtypeStruct((2, SLAB, HD), BF16)
    return call(
        join_kernel, [piece] * COLS, [pltpu.VMEM((ROW, HD), F32)], smem=(0,), nin=7
    )(offsets, own, near, a2, a4, a6, b1)


def spread_kernel(*refs):
    dq_in = refs[:COLS]
    kv_in = refs[COLS : 2 * COLS]
    q_ref, k_ref, v_ref = refs[2 * COLS :]
    _, col = place()
    for step in range(COLS):
        lanes = pl.ds(pl.multiple_of(((col - step + COLS) % COLS) * HD, HD), HD)
        q_ref[:, lanes] = dq_in[step][...]
        k_ref[:, lanes] = kv_in[step][0]
        v_ref[:, lanes] = kv_in[step][1]


def spread(dq, dkv):
    out = jax.ShapeDtypeStruct((SLAB, COLS * HD), BF16)
    return call(spread_kernel, [out] * 3, nin=2 * COLS)(*dq, *dkv)


def body(planes, query_states, key_states, value_states, out_grad, head_offsets):
    def exchange(pieces):
        return [pieces[0]] + [across(pieces[s], s, planes) for s in range(1, COLS)]

    kv = exchange(pack(key_states, value_states))
    qg = exchange(pack(query_states, out_grad))
    pv = [along(piece, 1, planes) for piece in kv]
    mine = thin(head_offsets, kv)
    pair = jnp.stack([mine, along(mine, 1, planes)])
    far = [along(pair, step, planes) for step in (2, 4, 6)]
    results = main(head_offsets, kv, qg, pv, far)
    dq = exchange(results[:COLS])
    near, h2, h4, h6, own = results[COLS:]
    near = along(near, -1, planes)
    a2, a4, a6 = [along(h, -step, planes) for h, step in ((h2, 2), (h4, 4), (h6, 6))]
    older = (a2[1].astype(F32) + a4[1].astype(F32) + a6[1].astype(F32)).astype(BF16)
    b1 = along(older, -1, planes)
    dkv = exchange(join(head_offsets, own, near, a2, a4, a6, b1))
    return tuple(spread(dq, dkv))


def solution(mesh):
    spec = P(("batch", "seq"), "head")
    planes = mesh.shape["seq"] // COLS
    return jax.shard_map(
        functools.partial(body, planes),
        mesh=mesh,
        in_specs=(spec, spec, spec, spec, P("head")),
        out_specs=(spec, spec, spec),
        check_vma=False,
    )
```

time: 467 us -> 98.3 us (0.21); the launches traced: 459 us -> 97.8 us
  waiting for transfers between devices: 157 us -> 29.2 us
  local copies, waits for them, and re-layouts: 123 us -> 1.91 us
  other arithmetic: 65.2 us -> 0.03 us
  matrix products: 39.7 us -> 0 us
  starting transfers between devices: 71.2 us -> 50.6 us
  Pallas kernels: 0 us -> 15.2 us
    ppermute x38 -> x25, waiting for transfers between devices: 157 us -> 29.2 us  [the longest x13 21.2 us: along(): return lax.ppermute(value, 'seq', pairs)]
    broadcast_in_dim x121 -> x0, local copies, waits for them, and re-layouts: 62.4 us -> none  [the longest x72 33.5 us: put_rows(): jnp.where(row_mask(source, chosen), update[:, None], shaped)]
    dot_general x36 -> x0, matrix products: 39.7 us -> none  [the longest x6 9.9 us: backward_part(): jnp.einsum('hqk,qhd->khd', weights.astype(jnp.bfloat16), grads, preferred...]
    reduce_sum x39 -> x0, other arithmetic: 28 us -> none  [the longest x32 22.2 us: pick_rows(): jnp.sum(jnp.where(row_mask(source, chosen), shaped, jnp.zeros((), source....]
    ppermute x38 -> x25, starting transfers between devices: 71.2 us -> 50.6 us  [the longest x13 31.2 us: along(): return lax.ppermute(value, 'seq', pairs)]
    pallas_call x0 -> x6, Pallas kernels: none -> 15.2 us  [the longest x1 12.4 us: main(): call(main_kernel, out, scratch, flops=2000000000, smem=(0,), nin=16)]
    reshape x19 -> x0, local copies, waits for them, and re-layouts: 13.1 us -> none  [the longest x18 12.3 us: pick_rows(): source.reshape((source.shape[0] // stride, stride) + source.shape[1:])]
    add x23 -> x0, other arithmetic: 11.6 us -> none  [the longest x5 5.74 us: merge_stats(): row_sum = first_stats[1] * first_factor + second_stats[1] * second_factor]
  transfers between devices with their start and end apart: 38 -> 25, of which waited for: 22 -> 8; matrix products, arithmetic and copies ran while one was open for 18% -> 0% of each run, Pallas kernels for 0% -> 1%
where the time goes in v1:
time: 98.3 us; the launch traced here: 97.8 us
  starting transfers between devices  50.6 us (51%)
  waiting for transfers between devices  29.2 us (30%)
  Pallas kernels  15.2 us (15%)
  local copies, waits for them, and re-layouts  1.91 us (2%)
    ppermute x13, starting transfers between devices, along(): return lax.ppermute(value, 'seq', pairs)  31.2 us
    ppermute x13, waiting for transfers between devices, along(): return lax.ppermute(value, 'seq', pairs)  21.2 us
    ppermute x12, starting transfers between devices, across(): return lax.ppermute(value, 'seq', pairs)  19.3 us
    pallas_call x1, Pallas kernels, main(): call(main_kernel, out, scratch, flops=2000000000, smem=(0,), nin=16)  12.4 us
    ppermute x12, waiting for transfers between devices, across(): return lax.ppermute(value, 'seq', pairs)  8.03 us
  transfers between devices with their start and end apart: 25, of which 8 were waited for; matrix products, arithmetic and copies ran while one was open for 0% of the time, Pallas kernels for 1%

profile of v1, /device:TPU:8, one launch (start us, length us, event | category | flops | bytes accessed | tf_op | source)
XLA Modules:
  0.0 97.8 jit_solution(5880077993577734841)
XLA Ops:
  0.6 0.0 copy-start
  0.6 0.9 copy-done
  1.6 0.0 copy-start.1
  1.6 0.9 copy-done.1
  2.5 0.1 shard_map.76
  2.6 1.6 %collective-permute-start = (bf16[2,256,128]{2,1,0:T(8,128)(2,1)S(1)}, bf16[2,256,128]{2,1,0:T(8,128)(2,1)S(1)}, u32[]{:S(2)}, u32[]{:S(2)}) collective-permute-start(bf16[2,256,128]{2,1,0:T(8,128)(2,1)S(1)} %get-tuple-element.25), channel_id=1, source_target_pairs={{0,8},{8,16},{16,24},{24,0},{32,40},{40,48},{48,56},{56,32},{64,72... | collective-permute-start | bytes 393224 | tf_op jit(solution)/shard_map/ppermute | solution.py:29
  4.2 2.7 %collective-permute-start.1 = (bf16[2,256,128]{2,1,0:T(8,128)(2,1)S(1)}, bf16[2,256,128]{2,1,0:T(8,128)(2,1)S(1)}, u32[]{:S(2)}, u32[]{:S(2)}) collective-permute-start(bf16[2,256,128]{2,1,0:T(8,128)(2,1)S(1)} %get-tuple-element.26), channel_id=1, source_target_pairs={{0,16},{8,24},{16,0},{24,8},{32,48},{40,56},{48,32},{56,40},{64,80... | collective-permute-start | bytes 393224 | tf_op jit(solution)/shard_map/ppermute | solution.py:29
  6.9 1.4 %collective-permute-start.2 = (bf16[2,256,128]{2,1,0:T(8,128)(2,1)S(1)}, bf16[2,256,128]{2,1,0:T(8,128)(2,1)S(1)}, u32[]{:S(2)}, u32[]{:S(2)}) collective-permute-start(bf16[2,256,128]{2,1,0:T(8,128)(2,1)S(1)} %get-tuple-element.27), channel_id=1, source_target_pairs={{0,24},{8,0},{16,8},{24,16},{32,56},{40,32},{48,40},{56,48},{64,88... | collective-permute-start | bytes 393224 | tf_op jit(solution)/shard_map/ppermute | solution.py:29
  8.4 0.9 collective-permute-done.refs_1_.refs_2_
  9.3 3.6 %collective-permute-done.1.refs_2_.refs_3_ = bf16[2,256,128]{2,1,0:T(8,128)(2,1)S(1)} collective-permute-done((bf16[2,256,128]{2,1,0:T(8,128)(2,1)S(1)}, bf16[2,256,128]{2,1,0:T(8,128)(2,1)S(1)}, u32[]{:S(2)}, u32[]{:S(2)}) %collective-permute-start.1) | collective-permute-done | bytes 131104 | tf_op jit(solution)/shard_map/ppermute | solution.py:29
  13.0 0.0 collective-permute-done.2.refs_3_.refs_4_
  13.0 0.0 copy-done.4
  13.0 0.0 copy-start.3
  13.0 0.7 shard_map.78
  13.7 3.8 %collective-permute-start.10 = (bf16[2,64,128]{2,1,0:T(8,128)(2,1)S(1)}, bf16[2,64,128]{2,1,0:T(8,128)(2,1)S(1)}, u32[]{:S(2)}, u32[]{:S(2)}) collective-permute-start(bf16[2,64,128]{2,1,0:T(8,128)(2,1)S(1)} %shard_map.78), channel_id=1, source_target_pairs={{0,32},{8,40},{16,48},{24,56},{32,64},{40,72},{48,80},{56,88},{64,... | collective-permute-start | bytes 98312 | tf_op jit(solution)/shard_map/ppermute | solution.py:39
  17.5 0.0 copy-done.2
  17.5 0.0 copy-done.3
  17.5 0.1 shard_map.77
  17.7 1.4 %collective-permute-start.3 = (bf16[2,256,128]{2,1,0:T(8,128)(2,1)S(1)}, bf16[2,256,128]{2,1,0:T(8,128)(2,1)S(1)}, u32[]{:S(2)}, u32[]{:S(2)}) collective-permute-start(bf16[2,256,128]{2,1,0:T(8,128)(2,1)S(1)} %get-tuple-element.29), channel_id=1, source_target_pairs={{0,8},{8,16},{16,24},{24,0},{32,40},{40,48},{48,56},{56,32},{64,72... | collective-permute-start | bytes 393224 | tf_op jit(solution)/shard_map/ppermute | solution.py:29
  19.1 2.4 %collective-permute-start.4 = (bf16[2,256,128]{2,1,0:T(8,128)(2,1)S(1)}, bf16[2,256,128]{2,1,0:T(8,128)(2,1)S(1)}, u32[]{:S(2)}, u32[]{:S(2)}) collective-permute-start(bf16[2,256,128]{2,1,0:T(8,128)(2,1)S(1)} %get-tuple-element.30), channel_id=1, source_target_pairs={{0,16},{8,24},{16,0},{24,8},{32,48},{40,56},{48,32},{56,40},{64,80... | collective-permute-start | bytes 393224 | tf_op jit(solution)/shard_map/ppermute | solution.py:29
  21.5 1.6 %collective-permute-start.5 = (bf16[2,256,128]{2,1,0:T(8,128)(2,1)S(1)}, bf16[2,256,128]{2,1,0:T(8,128)(2,1)S(1)}, u32[]{:S(2)}, u32[]{:S(2)}) collective-permute-start(bf16[2,256,128]{2,1,0:T(8,128)(2,1)S(1)} %get-tuple-element.31), channel_id=1, source_target_pairs={{0,24},{8,0},{16,8},{24,16},{32,56},{40,32},{48,40},{56,48},{64,88... | collective-permute-start | bytes 393224 | tf_op jit(solution)/shard_map/ppermute | solution.py:29
  23.0 3.8 %collective-permute-start.6 = (bf16[2,256,128]{2,1,0:T(8,128)(2,1)S(1)}, bf16[2,256,128]{2,1,0:T(8,128)(2,1)S(1)}, u32[]{:S(2)}, u32[]{:S(2)}) collective-permute-start(bf16[2,256,128]{2,1,0:T(8,128)(2,1)S(1)} %get-tuple-element.24.refs_0_.refs_1_), channel_id=1, source_target_pairs={{0,32},{8,40},{16,48},{24,56},{32,64},{40,72},{48,80},{56,88},{64,... | collective-permute-start | bytes 393224 | tf_op jit(solution)/shard_map/ppermute | solution.py:39
  26.9 0.0 collective-permute-done.10
  26.9 5.4 %collective-permute-start.13 = (bf16[2,2,64,128]{3,2,1,0:T(8,128)(2,1)S(1)}, bf16[2,2,64,128]{3,2,1,0:T(8,128)(2,1)S(1)}, u32[]{:S(2)}, u32[]{:S(2)}) collective-permute-start(bf16[2,2,64,128]{3,2,1,0:T(8,128)(2,1)S(1)} %pad_maximum_fusion), channel_id=1, source_target_pairs={{0,192},{8,200},{16,208},{24,216},{32,224},{40,232},{48,240},{56,2... | collective-permute-start | bytes 196616 | tf_op jit(solution)/shard_map/ppermute | solution.py:39
  32.3 0.0 collective-permute-done.3.refs_6_
  32.3 1.3 %collective-permute-start.7 = (bf16[2,256,128]{2,1,0:T(8,128)(2,1)S(1)}, bf16[2,256,128]{2,1,0:T(8,128)(2,1)S(1)}, u32[]{:S(2)}, u32[]{:S(2)}) collective-permute-start(bf16[2,256,128]{2,1,0:T(8,128)(2,1)S(1)} %collective-permute-done.refs_1_.refs_2_), channel_id=1, source_target_pairs={{0,32},{8,40},{16,48},{24,56},{32,64},{40,72},{48,80},{56,88},{64,... | collective-permute-start | bytes 393224 | tf_op jit(solution)/shard_map/ppermute | solution.py:39
  33.6 0.0 collective-permute-done.4.refs_7_
  33.6 2.8 %collective-permute-start.8 = (bf16[2,256,128]{2,1,0:T(8,128)(2,1)S(1)}, bf16[2,256,128]{2,1,0:T(8,128)(2,1)S(1)}, u32[]{:S(2)}, u32[]{:S(2)}) collective-permute-start(bf16[2,256,128]{2,1,0:T(8,128)(2,1)S(1)} %collective-permute-done.1.refs_2_.refs_3_), channel_id=1, source_target_pairs={{0,32},{8,40},{16,48},{24,56},{32,64},{40,72},{48,80},{56,88},{64,... | collective-permute-start | bytes 393224 | tf_op jit(solution)/shard_map/ppermute | solution.py:39
  36.5 0.0 collective-permute-done.5.refs_8_
  36.5 2.9 %collective-permute-start.9 = (bf16[2,256,128]{2,1,0:T(8,128)(2,1)S(1)}, bf16[2,256,128]{2,1,0:T(8,128)(2,1)S(1)}, u32[]{:S(2)}, u32[]{:S(2)}) collective-permute-start(bf16[2,256,128]{2,1,0:T(8,128)(2,1)S(1)} %collective-permute-done.2.refs_3_.refs_4_), channel_id=1, source_target_pairs={{0,32},{8,40},{16,48},{24,56},{32,64},{40,72},{48,80},{56,88},{64,... | collective-permute-start | bytes 393224 | tf_op jit(solution)/shard_map/ppermute | solution.py:39
  39.4 0.0 collective-permute-done.6.refs_9_
  39.4 2.9 %collective-permute-start.12 = (bf16[2,2,64,128]{3,2,1,0:T(8,128)(2,1)S(1)}, bf16[2,2,64,128]{3,2,1,0:T(8,128)(2,1)S(1)}, u32[]{:S(2)}, u32[]{:S(2)}) collective-permute-start(bf16[2,2,64,128]{3,2,1,0:T(8,128)(2,1)S(1)} %pad_maximum_fusion), channel_id=1, source_target_pairs={{0,128},{8,136},{16,144},{24,152},{32,160},{40,168},{48,176},{56,1... | collective-permute-start | bytes 196616 | tf_op jit(solution)/shard_map/ppermute | solution.py:39
  42.3 0.0 collective-permute-done.13.refs_15_
  42.3 1.8 %collective-permute-start.11 = (bf16[2,2,64,128]{3,2,1,0:T(8,128)(2,1)S(1)}, bf16[2,2,64,128]{3,2,1,0:T(8,128)(2,1)S(1)}, u32[]{:S(2)}, u32[]{:S(2)}) collective-permute-start(bf16[2,2,64,128]{3,2,1,0:T(8,128)(2,1)S(1)} %pad_maximum_fusion), channel_id=1, source_target_pairs={{0,64},{8,72},{16,80},{24,88},{32,96},{40,104},{48,112},{56,120},{... | collective-permute-start | bytes 196616 | tf_op jit(solution)/shard_map/ppermute | solution.py:39
  44.1 0.1 collective-permute-done.12.refs_14_
  44.2 1.8 %collective-permute-done.11.refs_13_ = bf16[2,2,64,128]{3,2,1,0:T(8,128)(2,1)S(1)} collective-permute-done((bf16[2,2,64,128]{3,2,1,0:T(8,128)(2,1)S(1)}, bf16[2,2,64,128]{3,2,1,0:T(8,128)(2,1)S(1)}, u32[]{:S(2)}, u32[]{:S(2)}) %collective-permute-start.11) | collective-permute-done | bytes 65568 | tf_op jit(solution)/shard_map/ppermute | solution.py:39
  46.0 0.0 collective-permute-done.7.refs_10_
  46.0 0.0 collective-permute-done.8.refs_11_
  46.0 0.0 collective-permute-done.9.refs_12_
  46.0 12.4 %shard_map.79 = (bf16[256,128]{1,0:T(8,128)(2,1)S(1)}, bf16[256,128]{1,0:T(8,128)(2,1)S(1)}, bf16[256,128]{1,0:T(8,128)(2,1)S(1)}, bf16[256,128]{1,0:T(8,128)(2,...) custom-call(s32[4]{0:T(128)S(1)} %copy-done.4, ...), custom_call_target="tpu_custom_call" | custom-call | flops 2000000000 | bytes 2097152 | tf_op jit(solution)/shard_map/pallas_call | solution.py:294
  58.4 1.3 %collective-permute-start.17 = (bf16[2,1024,128]{2,1,0:T(8,128)(2,1)S(1)}, bf16[2,1024,128]{2,1,0:T(8,128)(2,1)S(1)}, u32[]{:S(2)}, u32[]{:S(2)}) collective-permute-start(bf16[2,1024,128]{2,1,0:T(8,128)(2,1)S(1)} %get-tuple-element.37), channel_id=1, source_target_pairs={{32,0},{40,8},{48,16},{56,24},{64,32},{72,40},{80,48},{88,56},{96,... | collective-permute-start | bytes 1572872 | tf_op jit(solution)/shard_map/ppermute | solution.py:39
  59.7 1.3 %collective-permute-start.18 = (bf16[2,2,64,128]{3,2,1,0:T(8,128)(2,1)S(1)}, bf16[2,2,64,128]{3,2,1,0:T(8,128)(2,1)S(1)}, u32[]{:S(2)}, u32[]{:S(2)}) collective-permute-start(bf16[2,2,64,128]{3,2,1,0:T(8,128)(2,1)S(1)} %get-tuple-element.38), channel_id=1, source_target_pairs={{64,0},{72,8},{80,16},{88,24},{96,32},{104,40},{112,48},{120,56},{... | collective-permute-start | bytes 196616 | tf_op jit(solution)/shard_map/ppermute | solution.py:39
  61.0 1.3 %collective-permute-start.19 = (bf16[2,2,64,128]{3,2,1,0:T(8,128)(2,1)S(1)}, bf16[2,2,64,128]{3,2,1,0:T(8,128)(2,1)S(1)}, u32[]{:S(2)}, u32[]{:S(2)}) collective-permute-start(bf16[2,2,64,128]{3,2,1,0:T(8,128)(2,1)S(1)} %get-tuple-element.39), channel_id=1, source_target_pairs={{128,0},{136,8},{144,16},{152,24},{160,32},{168,40},{176,48},{184,... | collective-permute-start | bytes 196616 | tf_op jit(solution)/shard_map/ppermute | solution.py:39
  62.3 1.3 %collective-permute-start.20 = (bf16[2,2,64,128]{3,2,1,0:T(8,128)(2,1)S(1)}, bf16[2,2,64,128]{3,2,1,0:T(8,128)(2,1)S(1)}, u32[]{:S(2)}, u32[]{:S(2)}) collective-permute-start(bf16[2,2,64,128]{3,2,1,0:T(8,128)(2,1)S(1)} %get-tuple-element.40), channel_id=1, source_target_pairs={{192,0},{200,8},{208,16},{216,24},{224,32},{232,40},{240,48},{248,... | collective-permute-start | bytes 196616 | tf_op jit(solution)/shard_map/ppermute | solution.py:39
  63.6 11.0 %collective-permute-done.18.a2_ref = bf16[2,2,64,128]{3,2,1,0:T(8,128)(2,1)S(1)} collective-permute-done((bf16[2,2,64,128]{3,2,1,0:T(8,128)(2,1)S(1)}, bf16[2,2,64,128]{3,2,1,0:T(8,128)(2,1)S(1)}, u32[]{:S(2)}, u32[]{:S(2)}) %collective-permute-start.18) | collective-permute-done | bytes 65568 | tf_op jit(solution)/shard_map/ppermute | solution.py:39
  74.6 0.0 collective-permute-done.19.a4_ref
  74.6 0.0 collective-permute-done.20.a6_ref
  74.7 1.3 %collective-permute-start.21 = (bf16[2,64,128]{2,1,0:T(8,128)(2,1)S(1)}, bf16[2,64,128]{2,1,0:T(8,128)(2,1)S(1)}, u32[]{:S(2)}, u32[]{:S(2)}) collective-permute-start(bf16[2,64,128]{2,1,0:T(8,128)(2,1)S(1)} %fusion), channel_id=1, source_target_pairs={{32,0},{40,8},{48,16},{56,24},{64,32},{72,40},{80,48},{88,56},{96,... | collective-permute-start | bytes 98312 | tf_op jit(solution)/shard_map/ppermute | solution.py:39
  76.0 1.2 %collective-permute-start.14 = (bf16[256,128]{1,0:T(8,128)(2,1)S(1)}, bf16[256,128]{1,0:T(8,128)(2,1)S(1)}, u32[]{:S(2)}, u32[]{:S(2)}) collective-permute-start(bf16[256,128]{1,0:T(8,128)(2,1)S(1)} %get-tuple-element.33), channel_id=1, source_target_pairs={{0,8},{8,16},{16,24},{24,0},{32,40},{40,48},{48,56},{56,32},{64,72... | collective-permute-start | bytes 196616 | tf_op jit(solution)/shard_map/ppermute | solution.py:29
  77.1 8.3 %collective-permute-done.21.b1_ref = bf16[2,64,128]{2,1,0:T(8,128)(2,1)S(1)} collective-permute-done((bf16[2,64,128]{2,1,0:T(8,128)(2,1)S(1)}, bf16[2,64,128]{2,1,0:T(8,128)(2,1)S(1)}, u32[]{:S(2)}, u32[]{:S(2)}) %collective-permute-start.21) | collective-permute-done | bytes 32800 | tf_op jit(solution)/shard_map/ppermute | solution.py:39
  85.4 0.0 collective-permute-done.17.near_ref
  85.5 0.8 shard_map.80
  86.2 1.4 %collective-permute-start.22 = (bf16[2,256,128]{2,1,0:T(8,128)(2,1)S(1)}, bf16[2,256,128]{2,1,0:T(8,128)(2,1)S(1)}, u32[]{:S(2)}, u32[]{:S(2)}) collective-permute-start(bf16[2,256,128]{2,1,0:T(8,128)(2,1)S(1)} %get-tuple-element.42), channel_id=1, source_target_pairs={{0,8},{8,16},{16,24},{24,0},{32,40},{40,48},{48,56},{56,32},{64,72... | collective-permute-start | bytes 393224 | tf_op jit(solution)/shard_map/ppermute | solution.py:29
  87.6 1.0 %collective-permute-start.23 = (bf16[2,256,128]{2,1,0:T(8,128)(2,1)S(1)}, bf16[2,256,128]{2,1,0:T(8,128)(2,1)S(1)}, u32[]{:S(2)}, u32[]{:S(2)}) collective-permute-start(bf16[2,256,128]{2,1,0:T(8,128)(2,1)S(1)} %get-tuple-element.43), channel_id=1, source_target_pairs={{0,16},{8,24},{16,0},{24,8},{32,48},{40,56},{48,32},{56,40},{64,80... | collective-permute-start | bytes 393224 | tf_op jit(solution)/shard_map/ppermute | solution.py:29
  88.6 1.9 %collective-permute-start.24 = (bf16[2,256,128]{2,1,0:T(8,128)(2,1)S(1)}, bf16[2,256,128]{2,1,0:T(8,128)(2,1)S(1)}, u32[]{:S(2)}, u32[]{:S(2)}) collective-permute-start(bf16[2,256,128]{2,1,0:T(8,128)(2,1)S(1)} %get-tuple-element.44), channel_id=1, source_target_pairs={{0,24},{8,0},{16,8},{24,16},{32,56},{40,32},{48,40},{56,48},{64,88... | collective-permute-start | bytes 393224 | tf_op jit(solution)/shard_map/ppermute | solution.py:29
  90.6 1.9 %collective-permute-start.15 = (bf16[256,128]{1,0:T(8,128)(2,1)S(1)}, bf16[256,128]{1,0:T(8,128)(2,1)S(1)}, u32[]{:S(2)}, u32[]{:S(2)}) collective-permute-start(bf16[256,128]{1,0:T(8,128)(2,1)S(1)} %get-tuple-element.34), channel_id=1, source_target_pairs={{0,16},{8,24},{16,0},{24,8},{32,48},{40,56},{48,32},{56,40},{64,80... | collective-permute-start | bytes 196616 | tf_op jit(solution)/shard_map/ppermute | solution.py:29
  92.5 0.0 collective-permute-done.14.refs_1_
  92.5 0.8 collective-permute-start.16
  93.3 3.0 %collective-permute-done.15.refs_2_ = bf16[256,128]{1,0:T(8,128)(2,1)S(1)} collective-permute-done((bf16[256,128]{1,0:T(8,128)(2,1)S(1)}, bf16[256,128]{1,0:T(8,128)(2,1)S(1)}, u32[]{:S(2)}, u32[]{:S(2)}) %collective-permute-start.15) | collective-permute-done | bytes 65568 | tf_op jit(solution)/shard_map/ppermute | solution.py:29
  96.3 0.4 collective-permute-done.16.refs_3_
  96.7 0.0 collective-permute-done.22.refs_5_
  96.7 0.0 collective-permute-done.23.refs_6_
  96.8 0.0 collective-permute-done.24.refs_7_
  96.8 1.0 %shard_map.81 = (bf16[256,512]{1,0:T(8,128)(2,1)}, bf16[256,512]{1,0:T(8,128)(2,1)}, bf16[256,512]{1,0:T(8,128)(2,1)}) custom-call(bf16[256,128]{1,0:T(8,128)(2,1)S(1)} %get-tuple-element.32.refs_0_, bf16[256,128]{1,0:T(8,128)(2,1)S(1)} %collective-permute-done.14.refs_1_, bf16[256,128]{1,0:T(8,128)(2,1)S(1)} %collective-permute-done.15.refs_2_, ...), custom_call_target="tpu_custom_call" | custom-call | flops 1000000 | bytes 2097152 | tf_op jit(solution)/shard_map/pallas_call | solution.py:339
  (4 shorter events, 0.0 us)
Async XLA Ops:
  0.6 1.0 copy-start
  1.6 0.9 copy-start.1
  2.6 6.7 %collective-permute-start = (bf16[2,256,128]{2,1,0:T(8,128)(2,1)S(1)}, bf16[2,256,128]{2,1,0:T(8,128)(2,1)S(1)}, u32[]{:S(2)}, u32[]{:S(2)}) collective-permute-start(bf16[2,256,128]{2,1,0:T(8,128)(2,1)S(1)} %get-tuple-element.25), channel_id=1, source_target_pairs={{0,8},{8,16},{16,24},{24,0},{32,40},{40,48},{48,56},{56,32},{64,72... | collective-permute-start | bytes 393224 | tf_op jit(solution)/shard_map/ppermute | solution.py:29
  4.2 8.7 %collective-permute-start.1 = (bf16[2,256,128]{2,1,0:T(8,128)(2,1)S(1)}, bf16[2,256,128]{2,1,0:T(8,128)(2,1)S(1)}, u32[]{:S(2)}, u32[]{:S(2)}) collective-permute-start(bf16[2,256,128]{2,1,0:T(8,128)(2,1)S(1)} %get-tuple-element.26), channel_id=1, source_target_pairs={{0,16},{8,24},{16,0},{24,8},{32,48},{40,56},{48,32},{56,40},{64,80... | collective-permute-start | bytes 393224 | tf_op jit(solution)/shard_map/ppermute | solution.py:29
  6.9 6.0 %copy-start.4 = (s32[4]{0:T(128)S(1)}, s32[4]{0:T(128)}, u32[]{:S(2)}) copy-start(s32[4]{0:T(128)} %off_ref.3) | copy-start | bytes 52
  6.9 6.0 %collective-permute-start.2 = (bf16[2,256,128]{2,1,0:T(8,128)(2,1)S(1)}, bf16[2,256,128]{2,1,0:T(8,128)(2,1)S(1)}, u32[]{:S(2)}, u32[]{:S(2)}) collective-permute-start(bf16[2,256,128]{2,1,0:T(8,128)(2,1)S(1)} %get-tuple-element.27), channel_id=1, source_target_pairs={{0,24},{8,0},{16,8},{24,16},{32,56},{40,32},{48,40},{56,48},{64,88... | collective-permute-start | bytes 393224 | tf_op jit(solution)/shard_map/ppermute | solution.py:29
  13.0 4.6 %copy-start.2 = (bf16[256,512]{1,0:T(8,128)(2,1)S(1)}, bf16[256,512]{1,0:T(8,128)(2,1)}, u32[]{:S(2)}) copy-start(bf16[256,512]{1,0:T(8,128)(2,1)} %one_ref.3) | copy-start | bytes 786436
  13.0 4.6 %copy-start.3 = (bf16[256,512]{1,0:T(8,128)(2,1)S(1)}, bf16[256,512]{1,0:T(8,128)(2,1)}, u32[]{:S(2)}) copy-start(bf16[256,512]{1,0:T(8,128)(2,1)} %two_ref.3) | copy-start | bytes 786436
  13.7 13.2 %collective-permute-start.10 = (bf16[2,64,128]{2,1,0:T(8,128)(2,1)S(1)}, bf16[2,64,128]{2,1,0:T(8,128)(2,1)S(1)}, u32[]{:S(2)}, u32[]{:S(2)}) collective-permute-start(bf16[2,64,128]{2,1,0:T(8,128)(2,1)S(1)} %shard_map.78), channel_id=1, source_target_pairs={{0,32},{8,40},{16,48},{24,56},{32,64},{40,72},{48,80},{56,88},{64,... | collective-permute-start | bytes 98312 | tf_op jit(solution)/shard_map/ppermute | solution.py:39
  17.7 14.6 %collective-permute-start.3 = (bf16[2,256,128]{2,1,0:T(8,128)(2,1)S(1)}, bf16[2,256,128]{2,1,0:T(8,128)(2,1)S(1)}, u32[]{:S(2)}, u32[]{:S(2)}) collective-permute-start(bf16[2,256,128]{2,1,0:T(8,128)(2,1)S(1)} %get-tuple-element.29), channel_id=1, source_target_pairs={{0,8},{8,16},{16,24},{24,0},{32,40},{40,48},{48,56},{56,32},{64,72... | collective-permute-start | bytes 393224 | tf_op jit(solution)/shard_map/ppermute | solution.py:29
  19.1 14.5 %collective-permute-start.4 = (bf16[2,256,128]{2,1,0:T(8,128)(2,1)S(1)}, bf16[2,256,128]{2,1,0:T(8,128)(2,1)S(1)}, u32[]{:S(2)}, u32[]{:S(2)}) collective-permute-start(bf16[2,256,128]{2,1,0:T(8,128)(2,1)S(1)} %get-tuple-element.30), channel_id=1, source_target_pairs={{0,16},{8,24},{16,0},{24,8},{32,48},{40,56},{48,32},{56,40},{64,80... | collective-permute-start | bytes 393224 | tf_op jit(solution)/shard_map/ppermute | solution.py:29
  21.5 15.0 %collective-permute-start.5 = (bf16[2,256,128]{2,1,0:T(8,128)(2,1)S(1)}, bf16[2,256,128]{2,1,0:T(8,128)(2,1)S(1)}, u32[]{:S(2)}, u32[]{:S(2)}) collective-permute-start(bf16[2,256,128]{2,1,0:T(8,128)(2,1)S(1)} %get-tuple-element.31), channel_id=1, source_target_pairs={{0,24},{8,0},{16,8},{24,16},{32,56},{40,32},{48,40},{56,48},{64,88... | collective-permute-start | bytes 393224 | tf_op jit(solution)/shard_map/ppermute | solution.py:29
  23.0 16.4 %collective-permute-start.6 = (bf16[2,256,128]{2,1,0:T(8,128)(2,1)S(1)}, bf16[2,256,128]{2,1,0:T(8,128)(2,1)S(1)}, u32[]{:S(2)}, u32[]{:S(2)}) collective-permute-start(bf16[2,256,128]{2,1,0:T(8,128)(2,1)S(1)} %get-tuple-element.24.refs_0_.refs_1_), channel_id=1, source_target_pairs={{0,32},{8,40},{16,48},{24,56},{32,64},{40,72},{48,80},{56,88},{64,... | collective-permute-start | bytes 393224 | tf_op jit(solution)/shard_map/ppermute | solution.py:39
  26.9 15.4 %collective-permute-start.13 = (bf16[2,2,64,128]{3,2,1,0:T(8,128)(2,1)S(1)}, bf16[2,2,64,128]{3,2,1,0:T(8,128)(2,1)S(1)}, u32[]{:S(2)}, u32[]{:S(2)}) collective-permute-start(bf16[2,2,64,128]{3,2,1,0:T(8,128)(2,1)S(1)} %pad_maximum_fusion), channel_id=1, source_target_pairs={{0,192},{8,200},{16,208},{24,216},{32,224},{40,232},{48,240},{56,2... | collective-permute-start | bytes 196616 | tf_op jit(solution)/shard_map/ppermute | solution.py:39
  32.3 13.7 %collective-permute-start.7 = (bf16[2,256,128]{2,1,0:T(8,128)(2,1)S(1)}, bf16[2,256,128]{2,1,0:T(8,128)(2,1)S(1)}, u32[]{:S(2)}, u32[]{:S(2)}) collective-permute-start(bf16[2,256,128]{2,1,0:T(8,128)(2,1)S(1)} %collective-permute-done.refs_1_.refs_2_), channel_id=1, source_target_pairs={{0,32},{8,40},{16,48},{24,56},{32,64},{40,72},{48,80},{56,88},{64,... | collective-permute-start | bytes 393224 | tf_op jit(solution)/shard_map/ppermute | solution.py:39
  33.6 12.4 %collective-permute-start.8 = (bf16[2,256,128]{2,1,0:T(8,128)(2,1)S(1)}, bf16[2,256,128]{2,1,0:T(8,128)(2,1)S(1)}, u32[]{:S(2)}, u32[]{:S(2)}) collective-permute-start(bf16[2,256,128]{2,1,0:T(8,128)(2,1)S(1)} %collective-permute-done.1.refs_2_.refs_3_), channel_id=1, source_target_pairs={{0,32},{8,40},{16,48},{24,56},{32,64},{40,72},{48,80},{56,88},{64,... | collective-permute-start | bytes 393224 | tf_op jit(solution)/shard_map/ppermute | solution.py:39
  36.5 9.5 %collective-permute-start.9 = (bf16[2,256,128]{2,1,0:T(8,128)(2,1)S(1)}, bf16[2,256,128]{2,1,0:T(8,128)(2,1)S(1)}, u32[]{:S(2)}, u32[]{:S(2)}) collective-permute-start(bf16[2,256,128]{2,1,0:T(8,128)(2,1)S(1)} %collective-permute-done.2.refs_3_.refs_4_), channel_id=1, source_target_pairs={{0,32},{8,40},{16,48},{24,56},{32,64},{40,72},{48,80},{56,88},{64,... | collective-permute-start | bytes 393224 | tf_op jit(solution)/shard_map/ppermute | solution.py:39
  39.4 4.8 %collective-permute-start.12 = (bf16[2,2,64,128]{3,2,1,0:T(8,128)(2,1)S(1)}, bf16[2,2,64,128]{3,2,1,0:T(8,128)(2,1)S(1)}, u32[]{:S(2)}, u32[]{:S(2)}) collective-permute-start(bf16[2,2,64,128]{3,2,1,0:T(8,128)(2,1)S(1)} %pad_maximum_fusion), channel_id=1, source_target_pairs={{0,128},{8,136},{16,144},{24,152},{32,160},{40,168},{48,176},{56,1... | collective-permute-start | bytes 196616 | tf_op jit(solution)/shard_map/ppermute | solution.py:39
  42.3 3.7 %collective-permute-start.11 = (bf16[2,2,64,128]{3,2,1,0:T(8,128)(2,1)S(1)}, bf16[2,2,64,128]{3,2,1,0:T(8,128)(2,1)S(1)}, u32[]{:S(2)}, u32[]{:S(2)}) collective-permute-start(bf16[2,2,64,128]{3,2,1,0:T(8,128)(2,1)S(1)} %pad_maximum_fusion), channel_id=1, source_target_pairs={{0,64},{8,72},{16,80},{24,88},{32,96},{40,104},{48,112},{56,120},{... | collective-permute-start | bytes 196616 | tf_op jit(solution)/shard_map/ppermute | solution.py:39
  58.4 27.0 %collective-permute-start.17 = (bf16[2,1024,128]{2,1,0:T(8,128)(2,1)S(1)}, bf16[2,1024,128]{2,1,0:T(8,128)(2,1)S(1)}, u32[]{:S(2)}, u32[]{:S(2)}) collective-permute-start(bf16[2,1024,128]{2,1,0:T(8,128)(2,1)S(1)} %get-tuple-element.37), channel_id=1, source_target_pairs={{32,0},{40,8},{48,16},{56,24},{64,32},{72,40},{80,48},{88,56},{96,... | collective-permute-start | bytes 1572872 | tf_op jit(solution)/shard_map/ppermute | solution.py:39
  59.7 14.9 %collective-permute-start.18 = (bf16[2,2,64,128]{3,2,1,0:T(8,128)(2,1)S(1)}, bf16[2,2,64,128]{3,2,1,0:T(8,128)(2,1)S(1)}, u32[]{:S(2)}, u32[]{:S(2)}) collective-permute-start(bf16[2,2,64,128]{3,2,1,0:T(8,128)(2,1)S(1)} %get-tuple-element.38), channel_id=1, source_target_pairs={{64,0},{72,8},{80,16},{88,24},{96,32},{104,40},{112,48},{120,56},{... | collective-permute-start | bytes 196616 | tf_op jit(solution)/shard_map/ppermute | solution.py:39
  61.0 13.6 %collective-permute-start.19 = (bf16[2,2,64,128]{3,2,1,0:T(8,128)(2,1)S(1)}, bf16[2,2,64,128]{3,2,1,0:T(8,128)(2,1)S(1)}, u32[]{:S(2)}, u32[]{:S(2)}) collective-permute-start(bf16[2,2,64,128]{3,2,1,0:T(8,128)(2,1)S(1)} %get-tuple-element.39), channel_id=1, source_target_pairs={{128,0},{136,8},{144,16},{152,24},{160,32},{168,40},{176,48},{184,... | collective-permute-start | bytes 196616 | tf_op jit(solution)/shard_map/ppermute | solution.py:39
  62.3 12.3 %collective-permute-start.20 = (bf16[2,2,64,128]{3,2,1,0:T(8,128)(2,1)S(1)}, bf16[2,2,64,128]{3,2,1,0:T(8,128)(2,1)S(1)}, u32[]{:S(2)}, u32[]{:S(2)}) collective-permute-start(bf16[2,2,64,128]{3,2,1,0:T(8,128)(2,1)S(1)} %get-tuple-element.40), channel_id=1, source_target_pairs={{192,0},{200,8},{208,16},{216,24},{224,32},{232,40},{240,48},{248,... | collective-permute-start | bytes 196616 | tf_op jit(solution)/shard_map/ppermute | solution.py:39
  74.7 10.8 %collective-permute-start.21 = (bf16[2,64,128]{2,1,0:T(8,128)(2,1)S(1)}, bf16[2,64,128]{2,1,0:T(8,128)(2,1)S(1)}, u32[]{:S(2)}, u32[]{:S(2)}) collective-permute-start(bf16[2,64,128]{2,1,0:T(8,128)(2,1)S(1)} %fusion), channel_id=1, source_target_pairs={{32,0},{40,8},{48,16},{56,24},{64,32},{72,40},{80,48},{88,56},{96,... | collective-permute-start | bytes 98312 | tf_op jit(solution)/shard_map/ppermute | solution.py:39
  76.0 16.5 %collective-permute-start.14 = (bf16[256,128]{1,0:T(8,128)(2,1)S(1)}, bf16[256,128]{1,0:T(8,128)(2,1)S(1)}, u32[]{:S(2)}, u32[]{:S(2)}) collective-permute-start(bf16[256,128]{1,0:T(8,128)(2,1)S(1)} %get-tuple-element.33), channel_id=1, source_target_pairs={{0,8},{8,16},{16,24},{24,0},{32,40},{40,48},{48,56},{56,32},{64,72... | collective-permute-start | bytes 196616 | tf_op jit(solution)/shard_map/ppermute | solution.py:29
  86.2 10.5 %collective-permute-start.22 = (bf16[2,256,128]{2,1,0:T(8,128)(2,1)S(1)}, bf16[2,256,128]{2,1,0:T(8,128)(2,1)S(1)}, u32[]{:S(2)}, u32[]{:S(2)}) collective-permute-start(bf16[2,256,128]{2,1,0:T(8,128)(2,1)S(1)} %get-tuple-element.42), channel_id=1, source_target_pairs={{0,8},{8,16},{16,24},{24,0},{32,40},{40,48},{48,56},{56,32},{64,72... | collective-permute-start | bytes 393224 | tf_op jit(solution)/shard_map/ppermute | solution.py:29
  87.6 9.1 %collective-permute-start.23 = (bf16[2,256,128]{2,1,0:T(8,128)(2,1)S(1)}, bf16[2,256,128]{2,1,0:T(8,128)(2,1)S(1)}, u32[]{:S(2)}, u32[]{:S(2)}) collective-permute-start(bf16[2,256,128]{2,1,0:T(8,128)(2,1)S(1)} %get-tuple-element.43), channel_id=1, source_target_pairs={{0,16},{8,24},{16,0},{24,8},{32,48},{40,56},{48,32},{56,40},{64,80... | collective-permute-start | bytes 393224 | tf_op jit(solution)/shard_map/ppermute | solution.py:29
  88.6 8.1 %collective-permute-start.24 = (bf16[2,256,128]{2,1,0:T(8,128)(2,1)S(1)}, bf16[2,256,128]{2,1,0:T(8,128)(2,1)S(1)}, u32[]{:S(2)}, u32[]{:S(2)}) collective-permute-start(bf16[2,256,128]{2,1,0:T(8,128)(2,1)S(1)} %get-tuple-element.44), channel_id=1, source_target_pairs={{0,24},{8,0},{16,8},{24,16},{32,56},{40,32},{48,40},{56,48},{64,88... | collective-permute-start | bytes 393224 | tf_op jit(solution)/shard_map/ppermute | solution.py:29
  90.6 5.8 %collective-permute-start.15 = (bf16[256,128]{1,0:T(8,128)(2,1)S(1)}, bf16[256,128]{1,0:T(8,128)(2,1)S(1)}, u32[]{:S(2)}, u32[]{:S(2)}) collective-permute-start(bf16[256,128]{1,0:T(8,128)(2,1)S(1)} %get-tuple-element.34), channel_id=1, source_target_pairs={{0,16},{8,24},{16,0},{24,8},{32,48},{40,56},{48,32},{56,40},{64,80... | collective-permute-start | bytes 196616 | tf_op jit(solution)/shard_map/ppermute | solution.py:29
  92.5 4.3 %collective-permute-start.16 = (bf16[256,128]{1,0:T(8,128)(2,1)S(1)}, bf16[256,128]{1,0:T(8,128)(2,1)S(1)}, u32[]{:S(2)}, u32[]{:S(2)}) collective-permute-start(bf16[256,128]{1,0:T(8,128)(2,1)S(1)} %get-tuple-element.35), channel_id=1, source_target_pairs={{0,24},{8,0},{16,8},{24,16},{32,56},{40,32},{48,40},{56,48},{64,88... | collective-permute-start | bytes 196616 | tf_op jit(solution)/shard_map/ppermute | solution.py:29

commit v2 on v1

v2 whole, which is shorter than its diff:
```python
import functools

import jax
import jax.numpy as jnp
from jax import lax
from jax.experimental import pallas as pl
from jax.experimental.pallas import tpu as pltpu
from jax.sharding import PartitionSpec as P

COLS = 4
SLAB = 256
HD = 128
ROW = COLS * SLAB
NEG = -1e30
SCALE = HD**-0.5
LOG2E = 1.4426950408889634
FAR8 = ROW // 8
FAR16 = ROW // 16
FAR32 = ROW // 32
FARK = FAR8 + 2 * FAR16 + 4 * FAR32
C2 = SCALE * LOG2E
F32 = jnp.float32
BF16 = jnp.bfloat16


def across(value, step, planes):
    pairs = [
        (p * COLS + c, p * COLS + (c + step) % COLS) for p in range(planes) for c in range(COLS)
    ]
    return lax.ppermute(value, "seq", pairs)


def along(value, step, planes):
    pairs = [
        (p * COLS + c, (p + step) % planes * COLS + c) for p in range(planes) for c in range(COLS)
    ]
    return lax.ppermute(value, "seq", pairs)


def place():
    pos = lax.axis_index("seq")
    return pos // COLS, pos % COLS


def mm(left, right, dims):
    return lax.dot_general(left, right, (dims, ((), ())), preferred_element_type=F32)


def nn(left, right):
    return mm(left, right, ((1,), (0,)))


def nt(left, right):
    return mm(left, right, ((1,), (1,)))


def tn(left, right):
    return mm(left, right, ((0,), (0,)))


def call(kernel, out, scratch=(), smem=(), nin=0):
    here = pltpu.VMEM
    specs = [pl.BlockSpec(memory_space=pltpu.SMEM if i in smem else here) for i in range(nin)]
    return pl.pallas_call(
        kernel,
        out_shape=out,
        in_specs=specs,
        out_specs=jax.tree.map(lambda _: pl.BlockSpec(memory_space=here), out),
        scratch_shapes=scratch,
        compiler_params=pltpu.CompilerParams(vmem_limit_bytes=24 << 20),
        cost_estimate=pl.CostEstimate(flops=1, bytes_accessed=1, transcendentals=0),
    )


def pack_kernel(one_ref, two_ref, *out_refs):
    _, col = place()
    for step in range(COLS):
        lanes = pl.ds(pl.multiple_of(((col + step) % COLS) * HD, HD), HD)
        out_refs[step][0] = one_ref[:, lanes]
        out_refs[step][1] = two_ref[:, lanes]


def pack(one, two):
    piece = jax.ShapeDtypeStruct((2, SLAB, HD), BF16)
    return call(pack_kernel, [piece] * COLS, nin=2)(one, two)


def pick(stride, rest, rows, width):
    r = lax.broadcasted_iota(jnp.int32, (rows, width), 0)
    c = lax.broadcasted_iota(jnp.int32, (rows, width), 1)
    return (c == r * stride + rest).astype(BF16)


def rows_of(block):
    return pl.ds(block * SLAB, SLAB)


def stack_kernel(*refs):
    _, col = place()
    row_ref = refs[COLS]
    for step in range(COLS):
        slab = (col - step + COLS) % COLS
        rows = pl.ds(pl.multiple_of(slab * SLAB, SLAB), SLAB)
        for which in range(2):
            row_ref[which, rows] = refs[step][which]


def stack(pieces):
    return call(stack_kernel, jax.ShapeDtypeStruct((2, ROW, HD), BF16), nin=COLS)(*pieces)


def pair_kernel(off_ref, mine_ref, back_ref, wide_ref, slim_ref):
    _, col = place()
    off = off_ref[col]
    by16 = pick(16, off % 16, SLAB // 16, SLAB)
    by32 = pick(32, off % 32, SLAB // 32, SLAB)
    for j, ref in enumerate((mine_ref, back_ref)):
        for which in range(2):
            wide = [nn(by16, ref[which, rows_of(b)]) for b in range(COLS)]
            slim = [nn(by32, ref[which, rows_of(b)]) for b in range(COLS)]
            wide_ref[j, which] = jnp.concatenate(wide, axis=0).astype(BF16)
            slim_ref[j, which] = jnp.concatenate(slim, axis=0).astype(BF16)


def pair_up(offsets, mine, back):
    out = [
        jax.ShapeDtypeStruct((2, 2, FAR16, HD), BF16),
        jax.ShapeDtypeStruct((2, 2, FAR32, HD), BF16),
    ]
    return call(pair_kernel, out, smem=(0,), nin=3)(offsets, mine, back)


def depth_of(index, off):
    rest = (index - off) & 31
    total = jnp.zeros(index.shape, F32)
    for level in range(1, 6):
        total = total + ((rest & (2**level - 1)) == 0).astype(F32)
    return total


def iota(shape, axis):
    return lax.broadcasted_iota(jnp.int32, shape, axis)


def thinned(thin8, from_ref, few_ref):
    for which in range(2):
        for b in range(COLS):
            rows = pl.ds(b * (SLAB // 8), SLAB // 8)
            few_ref[which, rows] = nn(thin8, from_ref[which, rows_of(b)]).astype(BF16)


def first_own_kernel(off_ref, kv_ref, *refs):
    qg = refs[:COLS]
    stat_ref, qg_ref, tab_ref, few_ref, sc = refs[COLS:]
    _, col = place()
    off = off_ref[col]
    thin8 = pick(8, off % 8, SLAB // 8, SLAB)
    for step in range(COLS):
        slab = (col - step + COLS) % COLS
        rows = pl.ds(pl.multiple_of(slab * SLAB, SLAB), SLAB)
        for which in range(2):
            qg_ref[which, rows] = qg[step][which]
    thinned(thin8, qg_ref, few_ref)
    deep_k = depth_of(iota((SLAB, HD), 0), off)
    deep_k = jnp.concatenate([deep_k, deep_k], axis=1)
    deep_q = depth_of(iota((8, SLAB), 1), off)[:1]
    both = jnp.minimum(deep_k, deep_q)
    tab_ref[0] = 1.0 + jnp.maximum(both - 1.0, 0.0)
    tab_ref[1] = 1.0 + both
    stat_ref[...] = jnp.zeros((8, ROW), F32)
    seen = iota((SLAB, SLAB), 0) <= iota((SLAB, SLAB), 1)
    for qb in range(COLS):
        q = qg_ref[0, rows_of(qb)]
        g = qg_ref[1, rows_of(qb)]
        m = None
        for kb in range(qb + 1):
            s = nt(kv_ref[0, rows_of(kb)], q) * C2
            if kb == qb:
                s = jnp.where(seen, s, NEG)
            sc[rows_of(kb)] = s
            top = jnp.max(s, axis=0, keepdims=True)
            m = top if m is None else jnp.maximum(m, top)
        total = jnp.zeros((1, SLAB), F32)
        dot = jnp.zeros((1, SLAB), F32)
        for kb in range(qb + 1):
            e = jnp.exp2(sc[rows_of(kb)] - m)
            dp = nt(kv_ref[1, rows_of(kb)], g) * tab_ref[int(kb // 2 == qb // 2)]
            total = total + jnp.sum(
                e * tab_ref[int(kb // 2 == qb // 2)], axis=0, keepdims=True
            )
            dot = dot + jnp.sum(e.astype(BF16).astype(F32) * dp, axis=0, keepdims=True)
        lanes = pl.ds(qb * SLAB, SLAB)
        stat_ref[0:1, lanes] = m
        stat_ref[1:2, lanes] = total
        stat_ref[2:3, lanes] = dot


def first_own(offsets, kv, qg):
    out = [
        jax.ShapeDtypeStruct((8, ROW), F32),
        jax.ShapeDtypeStruct((2, ROW, HD), BF16),
        jax.ShapeDtypeStruct((2, SLAB, SLAB), F32),
        jax.ShapeDtypeStruct((2, FAR8, HD), BF16),
    ]
    scratch = [pltpu.VMEM((ROW, SLAB), F32)]
    return call(first_own_kernel, out, scratch, smem=(0,), nin=2 + COLS)(
        offsets, kv, *qg
    )


def first_prev_kernel(
    off_ref, kv_ref, qg_ref, so_ref, stat_ref, some_ref, few_ref, sc
):
    plane, col = place()
    rest8 = off_ref[col] % 8
    thinned(pick(8, rest8, SLAB // 8, SLAB), kv_ref, few_ref)
    there = plane > 0
    stat_ref[...] = jnp.zeros((8, ROW), F32)
    seen = iota((SLAB, SLAB), 0) > iota((SLAB, SLAB), 1)
    for qb in range(COLS):
        q = qg_ref[0, rows_of(qb)]
        g = qg_ref[1, rows_of(qb)]
        m = None
        for kb in range(qb, COLS):
            s = nt(kv_ref[0, rows_of(kb)], q) * C2
            if kb == qb:
                s = jnp.where(seen, s, NEG)
            sc[rows_of(kb)] = s
            top = jnp.max(s, axis=0, keepdims=True)
            m = top if m is None else jnp.maximum(m, top)
        total = jnp.zeros((1, SLAB), F32)
        dot = jnp.zeros((1, SLAB), F32)
        for kb in range(qb, COLS):
            s = sc[rows_of(kb)]
            e = jnp.exp2(s - m)
            if kb == qb:
                e = jnp.where(seen, e, 0.0)
            total = total + jnp.sum(e, axis=0, keepdims=True)
            dp = nt(kv_ref[1, rows_of(kb)], g)
            dot = dot + jnp.sum(e.astype(BF16).astype(F32) * dp, axis=0, keepdims=True)
        lanes = pl.ds(qb * SLAB, SLAB)
        mp = jnp.where(there, m, NEG)
        mo = so_ref[0:1, lanes]
        m = jnp.maximum(mo, mp)
        fo = jnp.exp2(mo - m)
        fp = jnp.where(there, jnp.exp2(mp - m), 0.0)
        stat_ref[0:1, lanes] = m
        stat_ref[1:2, lanes] = so_ref[1:2, lanes] * fo + total * fp
        stat_ref[2:3, lanes] = so_ref[2:3, lanes] * fo + dot * fp
    some_ref[...] = lax.dot_general(
        stat_ref[...], every8(rest8), (((1,), (1,)), ((), ())),
        precision=lax.Precision.HIGHEST, preferred_element_type=F32,
    )


def every8(rest8):
    return (iota((FAR8, ROW), 1) == iota((FAR8, ROW), 0) * 8 + rest8).astype(F32)


def first_prev(offsets, kv, qg, stat_own):
    out = [
        jax.ShapeDtypeStruct((8, ROW), F32),
        jax.ShapeDtypeStruct((8, FAR8), F32),
        jax.ShapeDtypeStruct((2, FAR8, HD), BF16),
    ]
    scratch = [pltpu.VMEM((ROW, SLAB), F32)]
    return call(first_prev_kernel, out, scratch, smem=(0,), nin=4)(
        offsets, kv, qg, stat_own
    )


def far_kernel(
    off_ref, kv8_ref, qg8_ref, g2_ref, g4_ref, g6_ref, stat_ref, some_ref,
    fin_ref, h2_ref, h4_ref, h6_ref, dqf_ref, pf_ref, kf, vf, near,
):
    plane, col = place()
    off = off_ref[col]
    rest8 = off % 8
    kf[pl.ds(0, FAR8)] = kv8_ref[0]
    vf[pl.ds(0, FAR8)] = kv8_ref[1]
    lo = FAR8
    for ref, size in ((g2_ref, FAR16), (g4_ref, FAR32), (g6_ref, FAR32)):
        for j in range(2):
            kf[pl.ds(lo, size)] = ref[j, 0]
            vf[pl.ds(lo, size)] = ref[j, 1]
            lo += size
    qs = qg8_ref[0]
    gs = qg8_ref[1]
    r = iota((FARK, HD), 0)
    mid = r - FAR8
    end = mid - 2 * FAR16
    back = jnp.where(r < FAR8, 1, jnp.where(end < 0, 2 + mid // FAR16, 4 + end // FAR32))
    spot = jnp.where(
        r < FAR8,
        r * 8 + rest8,
        jnp.where(end < 0, (mid % FAR16) * 16 + off % 16, (end % FAR32) * 32 + off % 32),
    )
    other = plane - back
    first = jnp.where(
        other < 0,
        9,
        jnp.where(other // 2 == plane // 2, 3, jnp.where(other // 4 == plane // 4, 4, 5)),
    )
    deep_q = depth_of(iota((8, FAR8), 1) * 8 + rest8, off)[:1]
    deep = jnp.minimum(deep_q, depth_of(spot, off))
    times = jnp.maximum(deep - first.astype(F32) + 1.0, 0.0)
    s = jnp.where(times > 0.0, nt(kf[...], qs) * C2, NEG)
    dp = nt(vf[...], gs)
    m_f = jnp.max(s, axis=0, keepdims=True)
    e = jnp.exp2(s - m_f)
    l_f = jnp.sum(e * times, axis=0, keepdims=True)
    d_f = jnp.sum(e.astype(BF16).astype(F32) * (dp * times), axis=0, keepdims=True)

    m_n, l_n, d_n = some_ref[0:1], some_ref[1:2], some_ref[2:3]
    m_s = jnp.maximum(m_n, m_f)
    fn = jnp.exp2(m_n - m_s)
    ff = jnp.exp2(m_f - m_s)
    l_s = l_n * fn + l_f * ff
    log_s = m_s + jnp.log2(l_s)
    dot_s = (d_n * fn + d_f * ff) / l_s
    near[...] = jnp.zeros((8, FAR8), F32)
    near[0:1] = log_s
    near[1:2] = dot_s
    wide = lax.dot_general(
        near[...], every8(rest8), (((1,), (0,)), ((), ())),
        precision=lax.Precision.HIGHEST, preferred_element_type=F32,
    )
    hit = (iota((8, ROW), 1) % 8 == rest8)[:1]
    fin_ref[...] = jnp.zeros((8, ROW), F32)
    total = stat_ref[1:2]
    fin_ref[0:1] = jnp.where(hit, wide[0:1], stat_ref[0:1] + jnp.log2(total))
    fin_ref[1:2] = jnp.where(hit, wide[1:2], stat_ref[2:3] / total)

    p = jnp.exp2(s - log_s) * times
    ds = (p * (dp - dot_s)).astype(BF16)
    dk = nn(ds, qs)
    dv = nn(p.astype(BF16), gs)
    dqf_ref[...] = tn(ds, kf[...])
    pf_ref[0] = dk[:FAR8]
    pf_ref[1] = dv[:FAR8]
    lo = FAR8
    for ref, size in ((h2_ref, FAR16), (h4_ref, FAR32), (h6_ref, FAR32)):
        for j in range(2):
            ref[j, 0] = dk[lo : lo + size].astype(BF16)
            ref[j, 1] = dv[lo : lo + size].astype(BF16)
            lo += size


def far_part(offsets, kv8, qg8, far, stat, some):
    out = [
        jax.ShapeDtypeStruct((8, ROW), F32),
        jax.ShapeDtypeStruct((2, 2, FAR16, HD), BF16),
        jax.ShapeDtypeStruct((2, 2, FAR32, HD), BF16),
        jax.ShapeDtypeStruct((2, 2, FAR32, HD), BF16),
        jax.ShapeDtypeStruct((FAR8, HD), F32),
        jax.ShapeDtypeStruct((2, FAR8, HD), F32),
    ]
    scratch = [
        pltpu.VMEM((FARK, HD), BF16),
        pltpu.VMEM((FARK, HD), BF16),
        pltpu.VMEM((8, FAR8), F32),
    ]
    return call(far_kernel, out, scratch, smem=(0,), nin=8)(
        offsets, kv8, qg8, *far, stat, some
    )


def back_prev_kernel(kv_ref, qg_ref, fin_ref, acc, dq_ref):
    plane, _ = place()
    there = plane > 0
    seen = iota((SLAB, SLAB), 0) > iota((SLAB, SLAB), 1)
    for kb in range(COLS):
        k = kv_ref[0, rows_of(kb)]
        v = kv_ref[1, rows_of(kb)]
        dk = jnp.zeros((SLAB, HD), F32)
        dv = jnp.zeros((SLAB, HD), F32)
        for qb in range(kb + 1):
            lanes = pl.ds(qb * SLAB, SLAB)
            q = qg_ref[0, rows_of(qb)]
            g = qg_ref[1, rows_of(qb)]
            log = jnp.where(there, fin_ref[0:1, lanes], -NEG)
            s = nt(k, q) * C2 - log
            if kb == qb:
                s = jnp.where(seen, s, NEG)
            p = jnp.exp2(s)
            ds = (p * (nt(v, g) - fin_ref[1:2, lanes])).astype(BF16)
            dv = dv + nn(p.astype(BF16), g)
            dk = dk + nn(ds, q)
            part = tn(k, ds)
            dq_ref[:, lanes] = part if kb == qb else dq_ref[:, lanes] + part
        acc[0, rows_of(kb)] = dk
        acc[1, rows_of(kb)] = dv


def back_prev(kv, qg, fin):
    out = [jax.ShapeDtypeStruct((2, ROW, HD), F32), jax.ShapeDtypeStruct((HD, ROW), F32)]
    return call(back_prev_kernel, out, nin=3)(kv, qg, fin)


def merge_kernel(off_ref, prev_ref, pf_ref, a2_ref, a4_ref, a6_ref, out_ref, acc):
    _, col = place()
    off = off_ref[col]
    every8th = pl.ds(off % 8, FAR8, stride=8)
    every16 = pl.ds(off % 16, FAR16, stride=16)
    every32 = pl.ds(off % 32, FAR32, stride=32)
    for which in range(2):
        acc[...] = prev_ref[which]
        acc[every8th, :] = acc[every8th, :] + pf_ref[which]
        acc[every16, :] = acc[every16, :] + a2_ref[1, which].astype(F32)
        acc[every32, :] = acc[every32, :] + (
            a4_ref[1, which].astype(F32) + a6_ref[1, which].astype(F32)
        )
        out_ref[which] = acc[...].astype(BF16)


def merge(offsets, prev, pf, a2, a4, a6):
    out = jax.ShapeDtypeStruct((2, ROW, HD), BF16)
    return call(merge_kernel, out, [pltpu.VMEM((ROW, HD), F32)], smem=(0,), nin=6)(
        offsets, prev, pf, a2, a4, a6
    )


def back_own_kernel(off_ref, kv_ref, qg_ref, fin_ref, tab_ref, dqp_ref, dqf_ref, *refs):
    dq_out = refs[:COLS]
    own_ref, dqt, dq = refs[COLS:]
    _, col = place()
    strided = pl.ds(off_ref[col] % 8, FAR8, stride=8)
    seen = iota((SLAB, SLAB), 0) <= iota((SLAB, SLAB), 1)
    for qb in range(COLS):
        lanes = pl.ds(qb * SLAB, SLAB)
        q = qg_ref[0, rows_of(qb)]
        g = qg_ref[1, rows_of(qb)]
        dq_sum = dqp_ref[:, lanes]
        for kb in range(qb + 1):
            k = kv_ref[0, rows_of(kb)]
            s = nt(k, q) * C2 - fin_ref[0:1, lanes]
            if kb == qb:
                s = jnp.where(seen, s, NEG)
            p = jnp.exp2(s) * tab_ref[int(kb // 2 == qb // 2)]
            ds = (p * (nt(kv_ref[1, rows_of(kb)], g) - fin_ref[1:2, lanes])).astype(BF16)
            dv = nn(p.astype(BF16), g)
            dk = nn(ds, q)
            dq_sum = dq_sum + tn(k, ds)
            if kb == qb:
                own_ref[0, rows_of(kb)] = dk
                own_ref[1, rows_of(kb)] = dv
            else:
                own_ref[0, rows_of(kb)] += dk
                own_ref[1, rows_of(kb)] += dv
        dq[rows_of(qb)] = dq_sum.T
    dq[strided, :] = dq[strided, :] + dqf_ref[...]
    for step in range(COLS):
        rows = pl.ds(pl.multiple_of(((col + step) % COLS) * SLAB, SLAB), SLAB)
        dq_out[step][...] = (dq[rows] * SCALE).astype(BF16)


def back_own(offsets, kv, qg, fin, tab, dqp, dqf):
    out = [jax.ShapeDtypeStruct((SLAB, HD), BF16)] * COLS + [
        jax.ShapeDtypeStruct((2, ROW, HD), F32)
    ]
    scratch = [pltpu.VMEM((HD, ROW), F32), pltpu.VMEM((ROW, HD), F32)]
    return call(back_own_kernel, out, scratch, smem=(0,), nin=7)(
        offsets, kv, qg, fin, tab, dqp, dqf
    )


def join_kernel(off_ref, own_ref, near_ref, a2_ref, a4_ref, a6_ref, *refs):
    out = refs[:COLS]
    acc = refs[COLS]
    _, col = place()
    off = off_ref[col]
    every16 = pl.ds(off % 16, FAR16, stride=16)
    every32 = pl.ds(off % 32, FAR32, stride=32)
    for which in range(2):
        acc[...] = own_ref[which] + near_ref[which].astype(F32)
        acc[every16, :] = acc[every16, :] + a2_ref[0, which].astype(F32)
        acc[every32, :] = acc[every32, :] + (
            a4_ref[0, which].astype(F32) + a6_ref[0, which].astype(F32)
        )
        for step in range(COLS):
            rows = pl.ds(pl.multiple_of(((col + step) % COLS) * SLAB, SLAB), SLAB)
            value = acc[rows]
            if which == 0:
                value = value * SCALE
            out[step][which] = value.astype(BF16)


def join(offsets, own, near, a2, a4, a6):
    piece = jax.ShapeDtypeStruct((2, SLAB, HD), BF16)
    return call(
        join_kernel, [piece] * COLS, [pltpu.VMEM((ROW, HD), F32)], smem=(0,), nin=6
    )(offsets, own, near, a2, a4, a6)


def spread_kernel(*refs):
    dq_in = refs[:COLS]
    kv_in = refs[COLS : 2 * COLS]
    q_ref, k_ref, v_ref = refs[2 * COLS :]
    _, col = place()
    for step in range(COLS):
        lanes = pl.ds(pl.multiple_of(((col - step + COLS) % COLS) * HD, HD), HD)
        q_ref[:, lanes] = dq_in[step][...]
        k_ref[:, lanes] = kv_in[step][0]
        v_ref[:, lanes] = kv_in[step][1]


def spread(dq, dkv):
    out = jax.ShapeDtypeStruct((SLAB, COLS * HD), BF16)
    return call(spread_kernel, [out] * 3, nin=2 * COLS)(*dq, *dkv)


def body(planes, query_states, key_states, value_states, out_grad, head_offsets):
    def exchange(pieces):
        return [pieces[0]] + [across(pieces[s], s, planes) for s in range(1, COLS)]

    kv = exchange(pack(key_states, value_states))
    qg = exchange(pack(query_states, out_grad))
    row = stack(kv)
    prev = along(row, 1, planes)
    stat_own, qg, tab, qg8 = first_own(head_offsets, row, qg)
    prev, stat_own = lax.optimization_barrier((prev, stat_own))
    wide, slim = pair_up(head_offsets, row, prev)
    far = [along(wide, 2, planes), along(slim, 4, planes), along(slim, 6, planes)]
    stat, some, kv8 = first_prev(head_offsets, prev, qg, stat_own)
    fin, h2, h4, h6, dqf, pf = far_part(head_offsets, kv8, qg8, far, stat, some)
    a2, a4, a6 = [along(h, -step, planes) for h, step in ((h2, 2), (h4, 4), (h6, 6))]
    prev_grad, dqp = back_prev(prev, qg, fin)
    results = back_own(head_offsets, row, qg, fin, tab, dqp, dqf)
    own, prev_grad = lax.optimization_barrier((results[COLS], prev_grad))
    near = along(merge(head_offsets, prev_grad, pf, a2, a4, a6), -1, planes)
    dq = exchange(results[:COLS])
    near, *dq = lax.optimization_barrier((near, *dq))
    dkv = exchange(join(head_offsets, own, near, a2, a4, a6))
    return tuple(spread(dq, dkv))


def solution(mesh):
    spec = P(("batch", "seq"), "head")
    planes = mesh.shape["seq"] // COLS
    return jax.shard_map(
        functools.partial(body, planes),
        mesh=mesh,
        in_specs=(spec, spec, spec, spec, P("head")),
        out_specs=(spec, spec, spec),
        check_vma=False,
    )
```

time: 98.3 us -> 79.6 us (0.81)
  starting transfers between devices: 50.6 us -> 39.1 us
  waiting for transfers between devices: 29.2 us -> 21.6 us
    ppermute x13 -> x8, waiting for transfers between devices: 21.2 us -> 5.25 us  [along(): return lax.ppermute(value, 'seq', pairs)]
    ppermute x13 -> x8, starting transfers between devices: 31.2 us -> 18.6 us  [along(): return lax.ppermute(value, 'seq', pairs)]
    ppermute x12, waiting for transfers between devices: 8.03 us -> 16.4 us  [across(): return lax.ppermute(value, 'seq', pairs)]
    ppermute x12, starting transfers between devices: 19.3 us -> 20.5 us  [across(): return lax.ppermute(value, 'seq', pairs)]
    pallas_call x2 -> x8, Pallas kernels: 13.1 us -> 14 us  [the longest x1 3.26 us: back_own(): call(back_own_kernel, out, scratch, smem=(0,), nin=7)]
  transfers between devices with their start and end apart: 25 -> 20, of which waited for: 8 -> 14; matrix products, arithmetic and copies ran while one was open for 0% -> 0% of each run, Pallas kernels for 1% -> 13%
where the time goes in v2:
time: 79.6 us; the launch traced here: 79.4 us
  starting transfers between devices  39.1 us (49%)
  waiting for transfers between devices  21.6 us (27%)
  Pallas kernels  16 us (20%)
  local copies, waits for them, and re-layouts  1.9 us (2%)
    ppermute x12, starting transfers between devices, across(): return lax.ppermute(value, 'seq', pairs)  20.5 us
    ppermute x8, starting transfers between devices, along(): return lax.ppermute(value, 'seq', pairs)  18.6 us
    ppermute x12, waiting for transfers between devices, across(): return lax.ppermute(value, 'seq', pairs)  16.4 us
    ppermute x8, waiting for transfers between devices, along(): return lax.ppermute(value, 'seq', pairs)  5.25 us
    pallas_call x1, Pallas kernels, back_own(): call(back_own_kernel, out, scratch, smem=(0,), nin=7)  3.26 us
    pallas_call x1, Pallas kernels, first_prev(): call(first_prev_kernel, out, scratch, smem=(0,), nin=4)  2.64 us
    pallas_call x1, Pallas kernels, back_prev(): return call(back_prev_kernel, out, nin=3)(kv, qg, fin)  2.49 us
    pallas_call x1, Pallas kernels, first_own(): call(first_own_kernel, out, scratch, smem=(0,), nin=2 + COLS)  2.2 us
  transfers between devices with their start and end apart: 20, of which 14 were waited for; matrix products, arithmetic and copies ran while one was open for 0% of the time, Pallas kernels for 13%

profile of v2, /device:TPU:8, one launch (start us, length us, event | category | flops | bytes accessed | tf_op | source)
XLA Modules:
  0.0 79.4 jit_solution(5042916159588819578)
XLA Ops:
  0.6 0.0 copy-start
  0.6 0.9 %copy-done = bf16[256,512]{1,0:T(8,128)(2,1)S(1)} copy-done((bf16[256,512]{1,0:T(8,128)(2,1)S(1)}, bf16[256,512]{1,0:T(8,128)(2,1)}, u32[]{:S(2)}) %copy-start) | copy-done | bytes 262168
  1.6 0.0 copy-start.1
  1.6 0.9 %copy-done.1 = bf16[256,512]{1,0:T(8,128)(2,1)S(1)} copy-done((bf16[256,512]{1,0:T(8,128)(2,1)S(1)}, bf16[256,512]{1,0:T(8,128)(2,1)}, u32[]{:S(2)}) %copy-start.1) | copy-done | bytes 262168
  2.5 0.1 shard_map.76
  2.6 1.6 %collective-permute-start = (bf16[2,256,128]{2,1,0:T(8,128)(2,1)S(1)}, bf16[2,256,128]{2,1,0:T(8,128)(2,1)S(1)}, u32[]{:S(2)}, u32[]{:S(2)}) collective-permute-start(bf16[2,256,128]{2,1,0:T(8,128)(2,1)S(1)} %get-tuple-element.47), channel_id=1, source_target_pairs={{0,8},{8,16},{16,24},{24,0},{32,40},{40,48},{48,56},{56,32},{64,72... | collective-permute-start | bytes 393224 | tf_op jit(solution)/shard_map/ppermute | solution.py:30
  4.2 2.7 %collective-permute-start.1 = (bf16[2,256,128]{2,1,0:T(8,128)(2,1)S(1)}, bf16[2,256,128]{2,1,0:T(8,128)(2,1)S(1)}, u32[]{:S(2)}, u32[]{:S(2)}) collective-permute-start(bf16[2,256,128]{2,1,0:T(8,128)(2,1)S(1)} %get-tuple-element.48), channel_id=1, source_target_pairs={{0,16},{8,24},{16,0},{24,8},{32,48},{40,56},{48,32},{56,40},{64,80... | collective-permute-start | bytes 393224 | tf_op jit(solution)/shard_map/ppermute | solution.py:30
  6.9 1.4 %collective-permute-start.2 = (bf16[2,256,128]{2,1,0:T(8,128)(2,1)S(1)}, bf16[2,256,128]{2,1,0:T(8,128)(2,1)S(1)}, u32[]{:S(2)}, u32[]{:S(2)}) collective-permute-start(bf16[2,256,128]{2,1,0:T(8,128)(2,1)S(1)} %get-tuple-element.49), channel_id=1, source_target_pairs={{0,24},{8,0},{16,8},{24,16},{32,56},{40,32},{48,40},{56,48},{64,88... | collective-permute-start | bytes 393224 | tf_op jit(solution)/shard_map/ppermute | solution.py:30
  8.4 1.0 %collective-permute-done.refs_1_ = bf16[2,256,128]{2,1,0:T(8,128)(2,1)S(1)} collective-permute-done((bf16[2,256,128]{2,1,0:T(8,128)(2,1)S(1)}, bf16[2,256,128]{2,1,0:T(8,128)(2,1)S(1)}, u32[]{:S(2)}, u32[]{:S(2)}) %collective-permute-start) | collective-permute-done | bytes 131104 | tf_op jit(solution)/shard_map/ppermute | solution.py:30
  9.3 3.6 %collective-permute-done.1.refs_2_ = bf16[2,256,128]{2,1,0:T(8,128)(2,1)S(1)} collective-permute-done((bf16[2,256,128]{2,1,0:T(8,128)(2,1)S(1)}, bf16[2,256,128]{2,1,0:T(8,128)(2,1)S(1)}, u32[]{:S(2)}, u32[]{:S(2)}) %collective-permute-start.1) | collective-permute-done | bytes 131104 | tf_op jit(solution)/shard_map/ppermute | solution.py:30
  13.0 0.0 collective-permute-done.2.refs_3_
  13.0 0.0 copy-start.2
  13.0 0.0 copy-start.3
  13.0 0.1 shard_map.77.kv_ref.mine_ref
  13.0 2.0 %collective-permute-start.6 = (bf16[2,1024,128]{2,1,0:T(8,128)(2,1)S(1)}, bf16[2,1024,128]{2,1,0:T(8,128)(2,1)S(1)}, u32[]{:S(2)}, u32[]{:S(2)}) collective-permute-start(bf16[2,1024,128]{2,1,0:T(8,128)(2,1)S(1)} %shard_map.77.kv_ref.mine_ref), channel_id=1, source_target_pairs={{0,32},{8,40},{16,48},{24,56},{32,64},{40,72},{48,80},{56,88},{64,... | collective-permute-start | bytes 1572872 | tf_op jit(solution)/shard_map/ppermute | solution.py:37
  15.0 0.0 copy-done.2
  15.0 0.0 copy-done.3
  15.0 0.1 shard_map.78
  15.1 1.4 %collective-permute-start.3 = (bf16[2,256,128]{2,1,0:T(8,128)(2,1)S(1)}, bf16[2,256,128]{2,1,0:T(8,128)(2,1)S(1)}, u32[]{:S(2)}, u32[]{:S(2)}) collective-permute-start(bf16[2,256,128]{2,1,0:T(8,128)(2,1)S(1)} %get-tuple-element.51), channel_id=1, source_target_pairs={{0,8},{8,16},{16,24},{24,0},{32,40},{40,48},{48,56},{56,32},{64,72... | collective-permute-start | bytes 393224 | tf_op jit(solution)/shard_map/ppermute | solution.py:30
  16.5 2.4 %collective-permute-start.4 = (bf16[2,256,128]{2,1,0:T(8,128)(2,1)S(1)}, bf16[2,256,128]{2,1,0:T(8,128)(2,1)S(1)}, u32[]{:S(2)}, u32[]{:S(2)}) collective-permute-start(bf16[2,256,128]{2,1,0:T(8,128)(2,1)S(1)} %get-tuple-element.52), channel_id=1, source_target_pairs={{0,16},{8,24},{16,0},{24,8},{32,48},{40,56},{48,32},{56,40},{64,80... | collective-permute-start | bytes 393224 | tf_op jit(solution)/shard_map/ppermute | solution.py:30
  18.9 0.0 copy-start.4
  18.9 1.6 %collective-permute-start.5 = (bf16[2,256,128]{2,1,0:T(8,128)(2,1)S(1)}, bf16[2,256,128]{2,1,0:T(8,128)(2,1)S(1)}, u32[]{:S(2)}, u32[]{:S(2)}) collective-permute-start(bf16[2,256,128]{2,1,0:T(8,128)(2,1)S(1)} %get-tuple-element.53), channel_id=1, source_target_pairs={{0,24},{8,0},{16,8},{24,16},{32,56},{40,32},{48,40},{56,48},{64,88... | collective-permute-start | bytes 393224 | tf_op jit(solution)/shard_map/ppermute | solution.py:30
  20.5 2.1 %collective-permute-done.3.refs_1_ = bf16[2,256,128]{2,1,0:T(8,128)(2,1)S(1)} collective-permute-done((bf16[2,256,128]{2,1,0:T(8,128)(2,1)S(1)}, bf16[2,256,128]{2,1,0:T(8,128)(2,1)S(1)}, u32[]{:S(2)}, u32[]{:S(2)}) %collective-permute-start.3) | collective-permute-done | bytes 131104 | tf_op jit(solution)/shard_map/ppermute | solution.py:30
  22.6 1.4 %collective-permute-done.4.refs_2_ = bf16[2,256,128]{2,1,0:T(8,128)(2,1)S(1)} collective-permute-done((bf16[2,256,128]{2,1,0:T(8,128)(2,1)S(1)}, bf16[2,256,128]{2,1,0:T(8,128)(2,1)S(1)}, u32[]{:S(2)}, u32[]{:S(2)}) %collective-permute-start.4) | collective-permute-done | bytes 131104 | tf_op jit(solution)/shard_map/ppermute | solution.py:30
  24.0 0.1 collective-permute-done.5.refs_3_
  24.1 0.0 copy-done.4
  24.1 2.2 %shard_map.79 = (f32[8,1024]{1,0:T(8,128)S(1)}, bf16[2,1024,128]{2,1,0:T(8,128)(2,1)S(1)}, f32[2,256,256]{2,1,0:T(8,128)S(1)}, bf16[2,128,128]{2,1,0:T(8,128)(2,1)S(1)}) custom-call(s32[4]{0:T(128)S(1)} %copy-done.4, bf16[2,1024,128]{2,1,0:T(8,128)(2,1)S(1)} %shard_map.77.kv_ref.mine_ref, bf16[2,256,128]{2,1,0:T(8,128)(2,1)S(1)} %get-tuple-element.50.refs_0_, ...), custom_call_target="tpu_custom_call" | custom-call | flops 1 | bytes 1 | tf_op jit(solution)/shard_map/pallas_call | solution.py:206
  26.3 3.7 %collective-permute-done.6.kv_ref.back_ref = bf16[2,1024,128]{2,1,0:T(8,128)(2,1)S(1)} collective-permute-done((bf16[2,1024,128]{2,1,0:T(8,128)(2,1)S(1)}, bf16[2,1024,128]{2,1,0:T(8,128)(2,1)S(1)}, u32[]{:S(2)}, u32[]{:S(2)}) %collective-permute-start.6) | collective-permute-done | bytes 524320 | tf_op jit(solution)/shard_map/ppermute | solution.py:37
  30.0 0.9 %shard_map.81 = (bf16[2,2,64,128]{3,2,1,0:T(8,128)(2,1)S(1)}, bf16[2,2,32,128]{3,2,1,0:T(8,128)(2,1)S(1)}) custom-call(s32[4]{0:T(128)S(1)} %copy-done.4, bf16[2,1024,128]{2,1,0:T(8,128)(2,1)S(1)} %shard_map.77.kv_ref.mine_ref, bf16[2,1024,128]{2,1,0:T(8,128)(2,1)S(1)} %collective-permute-done.6.kv_ref.back_ref), custom_call_target="tpu_custom_call" | custom-call | flops 1 | bytes 1 | tf_op jit(solution)/shard_map/pallas_call | solution.py:130
  30.9 0.1 collective-permute-start.7
  31.0 4.1 %collective-permute-start.9 = (bf16[2,2,32,128]{3,2,1,0:T(8,128)(2,1)S(1)}, bf16[2,2,32,128]{3,2,1,0:T(8,128)(2,1)S(1)}, u32[]{:S(2)}, u32[]{:S(2)}) collective-permute-start(bf16[2,2,32,128]{3,2,1,0:T(8,128)(2,1)S(1)} %get-tuple-element.61), channel_id=1, source_target_pairs={{0,192},{8,200},{16,208},{24,216},{32,224},{40,232},{48,240},{56,2... | collective-permute-start | bytes 98312 | tf_op jit(solution)/shard_map/ppermute | solution.py:37
  35.1 4.3 %collective-permute-start.8 = (bf16[2,2,32,128]{3,2,1,0:T(8,128)(2,1)S(1)}, bf16[2,2,32,128]{3,2,1,0:T(8,128)(2,1)S(1)}, u32[]{:S(2)}, u32[]{:S(2)}) collective-permute-start(bf16[2,2,32,128]{3,2,1,0:T(8,128)(2,1)S(1)} %get-tuple-element.61), channel_id=1, source_target_pairs={{0,128},{8,136},{16,144},{24,152},{32,160},{40,168},{48,176},{56,1... | collective-permute-start | bytes 98312 | tf_op jit(solution)/shard_map/ppermute | solution.py:37
  39.4 2.6 %shard_map.80 = (f32[8,1024]{1,0:T(8,128)S(1)}, f32[8,128]{1,0:T(8,128)S(1)}, bf16[2,128,128]{2,1,0:T(8,128)(2,1)S(1)}) custom-call(s32[4]{0:T(128)S(1)} %copy-done.4, bf16[2,1024,128]{2,1,0:T(8,128)(2,1)S(1)} %collective-permute-done.6.kv_ref.back_ref, bf16[2,1024,128]{2,1,0:T(8,128)(2,1)S(1)} %get-tuple-element.54.qg_ref, ...), custom_call_target="tpu_custom_call" | custom-call | flops 1 | bytes 1 | tf_op jit(solution)/shard_map/pallas_call | solution.py:267
  42.1 0.0 collective-permute-done.9.g6_ref
  42.1 0.9 %collective-permute-done.8.g4_ref = bf16[2,2,32,128]{3,2,1,0:T(8,128)(2,1)S(1)} collective-permute-done((bf16[2,2,32,128]{3,2,1,0:T(8,128)(2,1)S(1)}, bf16[2,2,32,128]{3,2,1,0:T(8,128)(2,1)S(1)}, u32[]{:S(2)}, u32[]{:S(2)}) %collective-permute-start.8) | collective-permute-done | bytes 32800 | tf_op jit(solution)/shard_map/ppermute | solution.py:37
  43.0 0.0 collective-permute-done.7.g2_ref
  43.0 1.6 %shard_map.82 = (f32[8,1024]{1,0:T(8,128)S(1)}, bf16[2,2,64,128]{3,2,1,0:T(8,128)(2,1)S(1)}, bf16[2,2,32,128]{3,2,1,0:T(8,128)(2,1)S(1)}, bf16[2,2,32,128]{3,2,1...) custom-call(s32[4]{0:T(128)S(1)} %copy-done.4, ...), custom_call_target="tpu_custom_call" | custom-call | flops 1 | bytes 1 | tf_op jit(solution)/shard_map/pallas_call | solution.py:363
  44.6 1.4 %collective-permute-start.10 = (bf16[2,2,64,128]{3,2,1,0:T(8,128)(2,1)S(1)}, bf16[2,2,64,128]{3,2,1,0:T(8,128)(2,1)S(1)}, u32[]{:S(2)}, u32[]{:S(2)}) collective-permute-start(bf16[2,2,64,128]{3,2,1,0:T(8,128)(2,1)S(1)} %get-tuple-element.72), channel_id=1, source_target_pairs={{0,192},{8,200},{16,208},{24,216},{32,224},{40,232},{48,240},{56,2... | collective-permute-start | bytes 196616 | tf_op jit(solution)/shard_map/ppermute | solution.py:37
  46.0 3.2 %collective-permute-start.11 = (bf16[2,2,32,128]{3,2,1,0:T(8,128)(2,1)S(1)}, bf16[2,2,32,128]{3,2,1,0:T(8,128)(2,1)S(1)}, u32[]{:S(2)}, u32[]{:S(2)}) collective-permute-start(bf16[2,2,32,128]{3,2,1,0:T(8,128)(2,1)S(1)} %get-tuple-element.73), channel_id=1, source_target_pairs={{0,128},{8,136},{16,144},{24,152},{32,160},{40,168},{48,176},{56,1... | collective-permute-start | bytes 98312 | tf_op jit(solution)/shard_map/ppermute | solution.py:37
  49.3 2.8 %collective-permute-start.12 = (bf16[2,2,32,128]{3,2,1,0:T(8,128)(2,1)S(1)}, bf16[2,2,32,128]{3,2,1,0:T(8,128)(2,1)S(1)}, u32[]{:S(2)}, u32[]{:S(2)}) collective-permute-start(bf16[2,2,32,128]{3,2,1,0:T(8,128)(2,1)S(1)} %get-tuple-element.74), channel_id=1, source_target_pairs={{0,64},{8,72},{16,80},{24,88},{32,96},{40,104},{48,112},{56,120},{... | collective-permute-start | bytes 98312 | tf_op jit(solution)/shard_map/ppermute | solution.py:37
  52.1 2.5 %shard_map.83 = (f32[2,1024,128]{2,1,0:T(8,128)S(1)}, f32[128,1024]{1,0:T(8,128)S(1)}) custom-call(bf16[2,1024,128]{2,1,0:T(8,128)(2,1)S(1)} %collective-permute-done.6.kv_ref.back_ref, bf16[2,1024,128]{2,1,0:T(8,128)(2,1)S(1)} %get-tuple-element.54.qg_ref, f32[8,1024]{1,0:T(8,128)S(1)} %get-tuple-element.64.fin_ref), custom_call_target="tpu_custom_call" | custom-call | flops 1 | bytes 1 | tf_op jit(solution)/shard_map/pallas_call | solution.py:397
  54.6 3.3 %shard_map.84 = (bf16[256,128]{1,0:T(8,128)(2,1)S(1)}, bf16[256,128]{1,0:T(8,128)(2,1)S(1)}, bf16[256,128]{1,0:T(8,128)(2,1)S(1)}, bf16[256,128]{1,0:T(8,128)(2,1)S(1)}, f32[2,1024,128]{2,1,0:T(8,128)S(1)}) custom-call(s32[4]{0:T(128)S(1)} %copy-done.4, bf16[2,1024,128]{2,1,0:T(8,128)(2,1)S(1)} %shard_map.77.kv_ref.mine_ref, ...), custom_call_target="tpu_custom_call" | custom-call | flops 1 | bytes 1 | tf_op jit(solution)/shard_map/pallas_call | solution.py:462
  57.8 0.0 collective-permute-done.11.a4_ref
  57.8 0.0 collective-permute-done.12.a6_ref
  57.9 0.0 collective-permute-done.10.a2_ref
  57.9 0.8 %shard_map.85 = bf16[2,1024,128]{2,1,0:T(8,128)(2,1)S(1)} custom-call(s32[4]{0:T(128)S(1)} %copy-done.4, f32[2,1024,128]{2,1,0:T(8,128)S(1)} %get-tuple-element.70.prev_ref, f32[2,128,128]{2,1,0:T(8,128)S(1)} %get-tuple-element.71.pf_ref, bf16[2,2,64,128]{3,2,1,0:T(8,128)(2,1)S(1)} %collective-permute-done.10.a2_ref, ...), custom_call_target="tpu_custom_call" | custom-call | flops 1 | bytes 1 | tf_op jit(solution)/shard_map/pallas_call | solution.py:418
  58.7 0.6 collective-permute-start.13
  59.3 1.6 %collective-permute-start.14 = (bf16[256,128]{1,0:T(8,128)(2,1)S(1)}, bf16[256,128]{1,0:T(8,128)(2,1)S(1)}, u32[]{:S(2)}, u32[]{:S(2)}) collective-permute-start(bf16[256,128]{1,0:T(8,128)(2,1)S(1)} %get-tuple-element.76), channel_id=1, source_target_pairs={{0,8},{8,16},{16,24},{24,0},{32,40},{40,48},{48,56},{56,32},{64,72... | collective-permute-start | bytes 196616 | tf_op jit(solution)/shard_map/ppermute | solution.py:30
  60.9 2.6 %collective-permute-start.15 = (bf16[256,128]{1,0:T(8,128)(2,1)S(1)}, bf16[256,128]{1,0:T(8,128)(2,1)S(1)}, u32[]{:S(2)}, u32[]{:S(2)}) collective-permute-start(bf16[256,128]{1,0:T(8,128)(2,1)S(1)} %get-tuple-element.77), channel_id=1, source_target_pairs={{0,16},{8,24},{16,0},{24,8},{32,48},{40,56},{48,32},{56,40},{64,80... | collective-permute-start | bytes 196616 | tf_op jit(solution)/shard_map/ppermute | solution.py:30
  63.4 0.7 collective-permute-start.16
  64.2 0.6 collective-permute-done.14.refs_1_
  64.8 1.9 %collective-permute-done.15.refs_2_ = bf16[256,128]{1,0:T(8,128)(2,1)S(1)} collective-permute-done((bf16[256,128]{1,0:T(8,128)(2,1)S(1)}, bf16[256,128]{1,0:T(8,128)(2,1)S(1)}, u32[]{:S(2)}, u32[]{:S(2)}) %collective-permute-start.15) | collective-permute-done | bytes 65568 | tf_op jit(solution)/shard_map/ppermute | solution.py:30
  66.6 1.1 %collective-permute-done.16.refs_3_ = bf16[256,128]{1,0:T(8,128)(2,1)S(1)} collective-permute-done((bf16[256,128]{1,0:T(8,128)(2,1)S(1)}, bf16[256,128]{1,0:T(8,128)(2,1)S(1)}, u32[]{:S(2)}, u32[]{:S(2)}) %collective-permute-start.16) | collective-permute-done | bytes 65568 | tf_op jit(solution)/shard_map/ppermute | solution.py:30
  67.7 0.6 collective-permute-done.13.near_ref
  68.3 0.8 %shard_map.86 = (bf16[2,256,128]{2,1,0:T(8,128)(2,1)S(1)}, bf16[2,256,128]{2,1,0:T(8,128)(2,1)S(1)}, bf16[2,256,128]{2,1,0:T(8,128)(2,1)S(1)}, bf16[2,256,128]{2,1,0:T(8,128)(2,1)S(1)}) custom-call(s32[4]{0:T(128)S(1)} %copy-done.4, f32[2,1024,128]{2,1,0:T(8,128)S(1)} %get-tuple-element.83.own_ref, ...), custom_call_target="tpu_custom_call" | custom-call | flops 1 | bytes 1 | tf_op jit(solution)/shard_map/pallas_call | solution.py:490
  69.2 1.8 %collective-permute-start.17 = (bf16[2,256,128]{2,1,0:T(8,128)(2,1)S(1)}, bf16[2,256,128]{2,1,0:T(8,128)(2,1)S(1)}, u32[]{:S(2)}, u32[]{:S(2)}) collective-permute-start(bf16[2,256,128]{2,1,0:T(8,128)(2,1)S(1)} %get-tuple-element.86), channel_id=1, source_target_pairs={{0,8},{8,16},{16,24},{24,0},{32,40},{40,48},{48,56},{56,32},{64,72... | collective-permute-start | bytes 393224 | tf_op jit(solution)/shard_map/ppermute | solution.py:30
  70.9 2.5 %collective-permute-start.18 = (bf16[2,256,128]{2,1,0:T(8,128)(2,1)S(1)}, bf16[2,256,128]{2,1,0:T(8,128)(2,1)S(1)}, u32[]{:S(2)}, u32[]{:S(2)}) collective-permute-start(bf16[2,256,128]{2,1,0:T(8,128)(2,1)S(1)} %get-tuple-element.87), channel_id=1, source_target_pairs={{0,16},{8,24},{16,0},{24,8},{32,48},{40,56},{48,32},{56,40},{64,80... | collective-permute-start | bytes 393224 | tf_op jit(solution)/shard_map/ppermute | solution.py:30
  73.4 0.3 collective-permute-start.19
  73.7 1.7 %collective-permute-done.17.refs_5_ = bf16[2,256,128]{2,1,0:T(8,128)(2,1)S(1)} collective-permute-done((bf16[2,256,128]{2,1,0:T(8,128)(2,1)S(1)}, bf16[2,256,128]{2,1,0:T(8,128)(2,1)S(1)}, u32[]{:S(2)}, u32[]{:S(2)}) %collective-permute-start.17) | collective-permute-done | bytes 131104 | tf_op jit(solution)/shard_map/ppermute | solution.py:30
  75.4 2.3 %collective-permute-done.18.refs_6_ = bf16[2,256,128]{2,1,0:T(8,128)(2,1)S(1)} collective-permute-done((bf16[2,256,128]{2,1,0:T(8,128)(2,1)S(1)}, bf16[2,256,128]{2,1,0:T(8,128)(2,1)S(1)}, u32[]{:S(2)}, u32[]{:S(2)}) %collective-permute-start.18) | collective-permute-done | bytes 131104 | tf_op jit(solution)/shard_map/ppermute | solution.py:30
  77.8 0.6 collective-permute-done.19.refs_7_
  78.4 1.0 %shard_map.87 = (bf16[256,512]{1,0:T(8,128)(2,1)}, bf16[256,512]{1,0:T(8,128)(2,1)}, bf16[256,512]{1,0:T(8,128)(2,1)}) custom-call(bf16[256,128]{1,0:T(8,128)(2,1)S(1)} %get-tuple-element.79.refs_0_, bf16[256,128]{1,0:T(8,128)(2,1)S(1)} %collective-permute-done.14.refs_1_, bf16[256,128]{1,0:T(8,128)(2,1)S(1)} %collective-permute-done.15.refs_2_, ...), custom_call_target="tpu_custom_call" | custom-call | flops 1 | bytes 1 | tf_op jit(solution)/shard_map/pallas_call | solution.py:509
Async XLA Ops:
  0.6 1.0 %copy-start = (bf16[256,512]{1,0:T(8,128)(2,1)S(1)}, bf16[256,512]{1,0:T(8,128)(2,1)}, u32[]{:S(2)}) copy-start(bf16[256,512]{1,0:T(8,128)(2,1)} %one_ref.2) | copy-start | bytes 786436
  1.6 0.9 %copy-start.1 = (bf16[256,512]{1,0:T(8,128)(2,1)S(1)}, bf16[256,512]{1,0:T(8,128)(2,1)}, u32[]{:S(2)}) copy-start(bf16[256,512]{1,0:T(8,128)(2,1)} %two_ref.2) | copy-start | bytes 786436
  2.6 6.7 %collective-permute-start = (bf16[2,256,128]{2,1,0:T(8,128)(2,1)S(1)}, bf16[2,256,128]{2,1,0:T(8,128)(2,1)S(1)}, u32[]{:S(2)}, u32[]{:S(2)}) collective-permute-start(bf16[2,256,128]{2,1,0:T(8,128)(2,1)S(1)} %get-tuple-element.47), channel_id=1, source_target_pairs={{0,8},{8,16},{16,24},{24,0},{32,40},{40,48},{48,56},{56,32},{64,72... | collective-permute-start | bytes 393224 | tf_op jit(solution)/shard_map/ppermute | solution.py:30
  4.2 8.7 %collective-permute-start.1 = (bf16[2,256,128]{2,1,0:T(8,128)(2,1)S(1)}, bf16[2,256,128]{2,1,0:T(8,128)(2,1)S(1)}, u32[]{:S(2)}, u32[]{:S(2)}) collective-permute-start(bf16[2,256,128]{2,1,0:T(8,128)(2,1)S(1)} %get-tuple-element.48), channel_id=1, source_target_pairs={{0,16},{8,24},{16,0},{24,8},{32,48},{40,56},{48,32},{56,40},{64,80... | collective-permute-start | bytes 393224 | tf_op jit(solution)/shard_map/ppermute | solution.py:30
  6.9 6.0 %collective-permute-start.2 = (bf16[2,256,128]{2,1,0:T(8,128)(2,1)S(1)}, bf16[2,256,128]{2,1,0:T(8,128)(2,1)S(1)}, u32[]{:S(2)}, u32[]{:S(2)}) collective-permute-start(bf16[2,256,128]{2,1,0:T(8,128)(2,1)S(1)} %get-tuple-element.49), channel_id=1, source_target_pairs={{0,24},{8,0},{16,8},{24,16},{32,56},{40,32},{48,40},{56,48},{64,88... | collective-permute-start | bytes 393224 | tf_op jit(solution)/shard_map/ppermute | solution.py:30
  13.0 2.1 %copy-start.2 = (bf16[256,512]{1,0:T(8,128)(2,1)S(1)}, bf16[256,512]{1,0:T(8,128)(2,1)}, u32[]{:S(2)}) copy-start(bf16[256,512]{1,0:T(8,128)(2,1)} %one_ref.3) | copy-start | bytes 786436
  13.0 2.1 %copy-start.3 = (bf16[256,512]{1,0:T(8,128)(2,1)S(1)}, bf16[256,512]{1,0:T(8,128)(2,1)}, u32[]{:S(2)}) copy-start(bf16[256,512]{1,0:T(8,128)(2,1)} %two_ref.3) | copy-start | bytes 786436
  13.0 17.0 %collective-permute-start.6 = (bf16[2,1024,128]{2,1,0:T(8,128)(2,1)S(1)}, bf16[2,1024,128]{2,1,0:T(8,128)(2,1)S(1)}, u32[]{:S(2)}, u32[]{:S(2)}) collective-permute-start(bf16[2,1024,128]{2,1,0:T(8,128)(2,1)S(1)} %shard_map.77.kv_ref.mine_ref), channel_id=1, source_target_pairs={{0,32},{8,40},{16,48},{24,56},{32,64},{40,72},{48,80},{56,88},{64,... | collective-permute-start | bytes 1572872 | tf_op jit(solution)/shard_map/ppermute | solution.py:37
  15.1 7.5 %collective-permute-start.3 = (bf16[2,256,128]{2,1,0:T(8,128)(2,1)S(1)}, bf16[2,256,128]{2,1,0:T(8,128)(2,1)S(1)}, u32[]{:S(2)}, u32[]{:S(2)}) collective-permute-start(bf16[2,256,128]{2,1,0:T(8,128)(2,1)S(1)} %get-tuple-element.51), channel_id=1, source_target_pairs={{0,8},{8,16},{16,24},{24,0},{32,40},{40,48},{48,56},{56,32},{64,72... | collective-permute-start | bytes 393224 | tf_op jit(solution)/shard_map/ppermute | solution.py:30
  16.5 7.5 %collective-permute-start.4 = (bf16[2,256,128]{2,1,0:T(8,128)(2,1)S(1)}, bf16[2,256,128]{2,1,0:T(8,128)(2,1)S(1)}, u32[]{:S(2)}, u32[]{:S(2)}) collective-permute-start(bf16[2,256,128]{2,1,0:T(8,128)(2,1)S(1)} %get-tuple-element.52), channel_id=1, source_target_pairs={{0,16},{8,24},{16,0},{24,8},{32,48},{40,56},{48,32},{56,40},{64,80... | collective-permute-start | bytes 393224 | tf_op jit(solution)/shard_map/ppermute | solution.py:30
  18.9 5.1 %copy-start.4 = (s32[4]{0:T(128)S(1)}, s32[4]{0:T(128)}, u32[]{:S(2)}) copy-start(s32[4]{0:T(128)} %off_ref.13) | copy-start | bytes 52
  18.9 5.1 %collective-permute-start.5 = (bf16[2,256,128]{2,1,0:T(8,128)(2,1)S(1)}, bf16[2,256,128]{2,1,0:T(8,128)(2,1)S(1)}, u32[]{:S(2)}, u32[]{:S(2)}) collective-permute-start(bf16[2,256,128]{2,1,0:T(8,128)(2,1)S(1)} %get-tuple-element.53), channel_id=1, source_target_pairs={{0,24},{8,0},{16,8},{24,16},{32,56},{40,32},{48,40},{56,48},{64,88... | collective-permute-start | bytes 393224 | tf_op jit(solution)/shard_map/ppermute | solution.py:30
  30.9 12.0 %collective-permute-start.7 = (bf16[2,2,64,128]{3,2,1,0:T(8,128)(2,1)S(1)}, bf16[2,2,64,128]{3,2,1,0:T(8,128)(2,1)S(1)}, u32[]{:S(2)}, u32[]{:S(2)}) collective-permute-start(bf16[2,2,64,128]{3,2,1,0:T(8,128)(2,1)S(1)} %get-tuple-element.60), channel_id=1, source_target_pairs={{0,64},{8,72},{16,80},{24,88},{32,96},{40,104},{48,112},{56,120},{... | collective-permute-start | bytes 196616 | tf_op jit(solution)/shard_map/ppermute | solution.py:37
  31.0 11.1 %collective-permute-start.9 = (bf16[2,2,32,128]{3,2,1,0:T(8,128)(2,1)S(1)}, bf16[2,2,32,128]{3,2,1,0:T(8,128)(2,1)S(1)}, u32[]{:S(2)}, u32[]{:S(2)}) collective-permute-start(bf16[2,2,32,128]{3,2,1,0:T(8,128)(2,1)S(1)} %get-tuple-element.61), channel_id=1, source_target_pairs={{0,192},{8,200},{16,208},{24,216},{32,224},{40,232},{48,240},{56,2... | collective-permute-start | bytes 98312 | tf_op jit(solution)/shard_map/ppermute | solution.py:37
  35.1 7.8 %collective-permute-start.8 = (bf16[2,2,32,128]{3,2,1,0:T(8,128)(2,1)S(1)}, bf16[2,2,32,128]{3,2,1,0:T(8,128)(2,1)S(1)}, u32[]{:S(2)}, u32[]{:S(2)}) collective-permute-start(bf16[2,2,32,128]{3,2,1,0:T(8,128)(2,1)S(1)} %get-tuple-element.61), channel_id=1, source_target_pairs={{0,128},{8,136},{16,144},{24,152},{32,160},{40,168},{48,176},{56,1... | collective-permute-start | bytes 98312 | tf_op jit(solution)/shard_map/ppermute | solution.py:37
  44.6 13.3 %collective-permute-start.10 = (bf16[2,2,64,128]{3,2,1,0:T(8,128)(2,1)S(1)}, bf16[2,2,64,128]{3,2,1,0:T(8,128)(2,1)S(1)}, u32[]{:S(2)}, u32[]{:S(2)}) collective-permute-start(bf16[2,2,64,128]{3,2,1,0:T(8,128)(2,1)S(1)} %get-tuple-element.72), channel_id=1, source_target_pairs={{0,192},{8,200},{16,208},{24,216},{32,224},{40,232},{48,240},{56,2... | collective-permute-start | bytes 196616 | tf_op jit(solution)/shard_map/ppermute | solution.py:37
  46.0 11.8 %collective-permute-start.11 = (bf16[2,2,32,128]{3,2,1,0:T(8,128)(2,1)S(1)}, bf16[2,2,32,128]{3,2,1,0:T(8,128)(2,1)S(1)}, u32[]{:S(2)}, u32[]{:S(2)}) collective-permute-start(bf16[2,2,32,128]{3,2,1,0:T(8,128)(2,1)S(1)} %get-tuple-element.73), channel_id=1, source_target_pairs={{0,128},{8,136},{16,144},{24,152},{32,160},{40,168},{48,176},{56,1... | collective-permute-start | bytes 98312 | tf_op jit(solution)/shard_map/ppermute | solution.py:37
  49.3 8.6 %collective-permute-start.12 = (bf16[2,2,32,128]{3,2,1,0:T(8,128)(2,1)S(1)}, bf16[2,2,32,128]{3,2,1,0:T(8,128)(2,1)S(1)}, u32[]{:S(2)}, u32[]{:S(2)}) collective-permute-start(bf16[2,2,32,128]{3,2,1,0:T(8,128)(2,1)S(1)} %get-tuple-element.74), channel_id=1, source_target_pairs={{0,64},{8,72},{16,80},{24,88},{32,96},{40,104},{48,112},{56,120},{... | collective-permute-start | bytes 98312 | tf_op jit(solution)/shard_map/ppermute | solution.py:37
  58.7 9.6 %collective-permute-start.13 = (bf16[2,1024,128]{2,1,0:T(8,128)(2,1)S(1)}, bf16[2,1024,128]{2,1,0:T(8,128)(2,1)S(1)}, u32[]{:S(2)}, u32[]{:S(2)}) collective-permute-start(bf16[2,1024,128]{2,1,0:T(8,128)(2,1)S(1)} %shard_map.85), channel_id=1, source_target_pairs={{0,224},{8,232},{16,240},{24,248},{32,0},{40,8},{48,16},{56,24},{6... | collective-permute-start | bytes 1572872 | tf_op jit(solution)/shard_map/ppermute | solution.py:37
  59.3 5.5 %collective-permute-start.14 = (bf16[256,128]{1,0:T(8,128)(2,1)S(1)}, bf16[256,128]{1,0:T(8,128)(2,1)S(1)}, u32[]{:S(2)}, u32[]{:S(2)}) collective-permute-start(bf16[256,128]{1,0:T(8,128)(2,1)S(1)} %get-tuple-element.76), channel_id=1, source_target_pairs={{0,8},{8,16},{16,24},{24,0},{32,40},{40,48},{48,56},{56,32},{64,72... | collective-permute-start | bytes 196616 | tf_op jit(solution)/shard_map/ppermute | solution.py:30
  60.9 5.8 %collective-permute-start.15 = (bf16[256,128]{1,0:T(8,128)(2,1)S(1)}, bf16[256,128]{1,0:T(8,128)(2,1)S(1)}, u32[]{:S(2)}, u32[]{:S(2)}) collective-permute-start(bf16[256,128]{1,0:T(8,128)(2,1)S(1)} %get-tuple-element.77), channel_id=1, source_target_pairs={{0,16},{8,24},{16,0},{24,8},{32,48},{40,56},{48,32},{56,40},{64,80... | collective-permute-start | bytes 196616 | tf_op jit(solution)/shard_map/ppermute | solution.py:30
  63.4 4.3 %collective-permute-start.16 = (bf16[256,128]{1,0:T(8,128)(2,1)S(1)}, bf16[256,128]{1,0:T(8,128)(2,1)S(1)}, u32[]{:S(2)}, u32[]{:S(2)}) collective-permute-start(bf16[256,128]{1,0:T(8,128)(2,1)S(1)} %get-tuple-element.78), channel_id=1, source_target_pairs={{0,24},{8,0},{16,8},{24,16},{32,56},{40,32},{48,40},{56,48},{64,88... | collective-permute-start | bytes 196616 | tf_op jit(solution)/shard_map/ppermute | solution.py:30
  69.2 6.3 %collective-permute-start.17 = (bf16[2,256,128]{2,1,0:T(8,128)(2,1)S(1)}, bf16[2,256,128]{2,1,0:T(8,128)(2,1)S(1)}, u32[]{:S(2)}, u32[]{:S(2)}) collective-permute-start(bf16[2,256,128]{2,1,0:T(8,128)(2,1)S(1)} %get-tuple-element.86), channel_id=1, source_target_pairs={{0,8},{8,16},{16,24},{24,0},{32,40},{40,48},{48,56},{56,32},{64,72... | collective-permute-start | bytes 393224 | tf_op jit(solution)/shard_map/ppermute | solution.py:30
  70.9 6.8 %collective-permute-start.18 = (bf16[2,256,128]{2,1,0:T(8,128)(2,1)S(1)}, bf16[2,256,128]{2,1,0:T(8,128)(2,1)S(1)}, u32[]{:S(2)}, u32[]{:S(2)}) collective-permute-start(bf16[2,256,128]{2,1,0:T(8,128)(2,1)S(1)} %get-tuple-element.87), channel_id=1, source_target_pairs={{0,16},{8,24},{16,0},{24,8},{32,48},{40,56},{48,32},{56,40},{64,80... | collective-permute-start | bytes 393224 | tf_op jit(solution)/shard_map/ppermute | solution.py:30
  73.4 5.0 %collective-permute-start.19 = (bf16[2,256,128]{2,1,0:T(8,128)(2,1)S(1)}, bf16[2,256,128]{2,1,0:T(8,128)(2,1)S(1)}, u32[]{:S(2)}, u32[]{:S(2)}) collective-permute-start(bf16[2,256,128]{2,1,0:T(8,128)(2,1)S(1)} %get-tuple-element.88), channel_id=1, source_target_pairs={{0,24},{8,0},{16,8},{24,16},{32,56},{40,32},{48,40},{56,48},{64,88... | collective-permute-start | bytes 393224 | tf_op jit(solution)/shard_map/ppermute | solution.py:30

commit v3 on v2

--- a/solution.py
+++ b/solution.py
@@ -17,6 +17,8 @@
 FAR8 = ROW // 8
 FAR16 = ROW // 16
 FAR32 = ROW // 32
+THIN16 = SLAB // 16
+THIN32 = SLAB // 32
 FARK = FAR8 + 2 * FAR16 + 4 * FAR32
 C2 = SCALE * LOG2E
 F32 = jnp.float32
@@ -96,38 +98,48 @@
 
 
 def stack_kernel(*refs):
-    _, col = place()
-    row_ref = refs[COLS]
+    out_ref = refs[COLS - 1]
+    for i in range(COLS - 1):
+        for which in range(2):
+            out_ref[which, rows_of(i)] = refs[i][which]
+
+
+def stack(pieces):
+    out = jax.ShapeDtypeStruct((2, ROW - SLAB, HD), BF16)
+    return call(stack_kernel, out, nin=COLS - 1)(*pieces)
+
+
+def place_rows(out_ref, col, step, which, value):
+    slab = (col - step + COLS) % COLS
+    out_ref[which, pl.ds(pl.multiple_of(slab * SLAB, SLAB), SLAB)] = value
+
+
+def pair_kernel(off_ref, *refs):
+    mine = refs[:COLS]
+    first_ref, rest_ref, prev_ref, wide_ref, slim_ref = refs[COLS:]
+    _, col = place()
+    off = off_ref[col]
+    by16 = pick(16, off % 16, THIN16, SLAB)
+    by32 = pick(32, off % 32, THIN32, SLAB)
     for step in range(COLS):
         slab = (col - step + COLS) % COLS
-        rows = pl.ds(pl.multiple_of(slab * SLAB, SLAB), SLAB)
+        few = pl.ds(pl.multiple_of(slab * THIN16, THIN16), THIN16)
+        less = pl.ds(pl.multiple_of(slab * THIN32, THIN32), THIN32)
         for which in range(2):
-            row_ref[which, rows] = refs[step][which]
-
-
-def stack(pieces):
-    return call(stack_kernel, jax.ShapeDtypeStruct((2, ROW, HD), BF16), nin=COLS)(*pieces)
-
-
-def pair_kernel(off_ref, mine_ref, back_ref, wide_ref, slim_ref):
-    _, col = place()
-    off = off_ref[col]
-    by16 = pick(16, off % 16, SLAB // 16, SLAB)
-    by32 = pick(32, off % 32, SLAB // 32, SLAB)
-    for j, ref in enumerate((mine_ref, back_ref)):
-        for which in range(2):
-            wide = [nn(by16, ref[which, rows_of(b)]) for b in range(COLS)]
-            slim = [nn(by32, ref[which, rows_of(b)]) for b in range(COLS)]
-            wide_ref[j, which] = jnp.concatenate(wide, axis=0).astype(BF16)
-            slim_ref[j, which] = jnp.concatenate(slim, axis=0).astype(BF16)
-
-
-def pair_up(offsets, mine, back):
+            back = first_ref[which] if step == 0 else rest_ref[which, rows_of(step - 1)]
+            place_rows(prev_ref, col, step, which, back)
+            for j, value in enumerate((mine[step][which], back)):
+                wide_ref[j, which, few] = nn(by16, value).astype(BF16)
+                slim_ref[j, which, less] = nn(by32, value).astype(BF16)
+
+
+def pair_up(offsets, mine, first, rest):
     out = [
+        jax.ShapeDtypeStruct((2, ROW, HD), BF16),
         jax.ShapeDtypeStruct((2, 2, FAR16, HD), BF16),
         jax.ShapeDtypeStruct((2, 2, FAR32, HD), BF16),
     ]
-    return call(pair_kernel, out, smem=(0,), nin=3)(offsets, mine, back)
+    return call(pair_kernel, out, smem=(0,), nin=3 + COLS)(offsets, *mine, first, rest)
 
 
 def depth_of(index, off):
@@ -149,17 +161,17 @@
             few_ref[which, rows] = nn(thin8, from_ref[which, rows_of(b)]).astype(BF16)
 
 
-def first_own_kernel(off_ref, kv_ref, *refs):
-    qg = refs[:COLS]
-    stat_ref, qg_ref, tab_ref, few_ref, sc = refs[COLS:]
+def first_own_kernel(off_ref, *refs):
+    kv = refs[:COLS]
+    qg = refs[COLS : 2 * COLS]
+    stat_ref, kv_ref, qg_ref, tab_ref, few_ref, sc = refs[2 * COLS :]
     _, col = place()
     off = off_ref[col]
     thin8 = pick(8, off % 8, SLAB // 8, SLAB)
     for step in range(COLS):
-        slab = (col - step + COLS) % COLS
-        rows = pl.ds(pl.multiple_of(slab * SLAB, SLAB), SLAB)
         for which in range(2):
-            qg_ref[which, rows] = qg[step][which]
+            place_rows(kv_ref, col, step, which, kv[step][which])
+            place_rows(qg_ref, col, step, which, qg[step][which])
     thinned(thin8, qg_ref, few_ref)
     deep_k = depth_of(iota((SLAB, HD), 0), off)
     deep_k = jnp.concatenate([deep_k, deep_k], axis=1)
@@ -199,12 +211,13 @@
     out = [
         jax.ShapeDtypeStruct((8, ROW), F32),
         jax.ShapeDtypeStruct((2, ROW, HD), BF16),
+        jax.ShapeDtypeStruct((2, ROW, HD), BF16),
         jax.ShapeDtypeStruct((2, SLAB, SLAB), F32),
         jax.ShapeDtypeStruct((2, FAR8, HD), BF16),
     ]
     scratch = [pltpu.VMEM((ROW, SLAB), F32)]
-    return call(first_own_kernel, out, scratch, smem=(0,), nin=2 + COLS)(
-        offsets, kv, *qg
+    return call(first_own_kernel, out, scratch, smem=(0,), nin=1 + 2 * COLS)(
+        offsets, *kv, *qg
     )
 
 
@@ -247,14 +260,19 @@
         stat_ref[0:1, lanes] = m
         stat_ref[1:2, lanes] = so_ref[1:2, lanes] * fo + total * fp
         stat_ref[2:3, lanes] = so_ref[2:3, lanes] * fo + dot * fp
-    some_ref[...] = lax.dot_general(
-        stat_ref[...], every8(rest8), (((1,), (1,)), ((), ())),
-        precision=lax.Precision.HIGHEST, preferred_element_type=F32,
-    )
+    some_ref[...] = moved(stat_ref[...], every8(rest8), ((1,), (1,)))
 
 
 def every8(rest8):
-    return (iota((FAR8, ROW), 1) == iota((FAR8, ROW), 0) * 8 + rest8).astype(F32)
+    return (iota((FAR8, ROW), 1) == iota((FAR8, ROW), 0) * 8 + rest8).astype(BF16)
+
+
+def moved(values, chosen, dims):
+    high = values.astype(BF16)
+    rest = values - high.astype(F32)
+    mid = rest.astype(BF16)
+    low = (rest - mid.astype(F32)).astype(BF16)
+    return mm(high, chosen, dims) + mm(mid, chosen, dims) + mm(low, chosen, dims)
 
 
 def first_prev(offsets, kv, qg, stat_own):
@@ -321,10 +339,7 @@
     near[...] = jnp.zeros((8, FAR8), F32)
     near[0:1] = log_s
     near[1:2] = dot_s
-    wide = lax.dot_general(
-        near[...], every8(rest8), (((1,), (0,)), ((), ())),
-        precision=lax.Precision.HIGHEST, preferred_element_type=F32,
-    )
+    wide = moved(near[...], every8(rest8), ((1,), (0,)))
     hit = (iota((8, ROW), 1) % 8 == rest8)[:1]
     fin_ref[...] = jnp.zeros((8, ROW), F32)
     total = stat_ref[1:2]
@@ -421,8 +436,7 @@
 
 
 def back_own_kernel(off_ref, kv_ref, qg_ref, fin_ref, tab_ref, dqp_ref, dqf_ref, *refs):
-    dq_out = refs[:COLS]
-    own_ref, dqt, dq = refs[COLS:]
+    own_ref, dq_ref, dq = refs
     _, col = place()
     strided = pl.ds(off_ref[col] % 8, FAR8, stride=8)
     seen = iota((SLAB, SLAB), 0) <= iota((SLAB, SLAB), 1)
@@ -449,22 +463,18 @@
                 own_ref[1, rows_of(kb)] += dv
         dq[rows_of(qb)] = dq_sum.T
     dq[strided, :] = dq[strided, :] + dqf_ref[...]
-    for step in range(COLS):
-        rows = pl.ds(pl.multiple_of(((col + step) % COLS) * SLAB, SLAB), SLAB)
-        dq_out[step][...] = (dq[rows] * SCALE).astype(BF16)
+    dq_ref[...] = (dq[...] * SCALE).astype(BF16)
 
 
 def back_own(offsets, kv, qg, fin, tab, dqp, dqf):
-    out = [jax.ShapeDtypeStruct((SLAB, HD), BF16)] * COLS + [
-        jax.ShapeDtypeStruct((2, ROW, HD), F32)
-    ]
-    scratch = [pltpu.VMEM((HD, ROW), F32), pltpu.VMEM((ROW, HD), F32)]
+    out = [jax.ShapeDtypeStruct((2, ROW, HD), F32), jax.ShapeDtypeStruct((ROW, HD), BF16)]
+    scratch = [pltpu.VMEM((ROW, HD), F32)]
     return call(back_own_kernel, out, scratch, smem=(0,), nin=7)(
         offsets, kv, qg, fin, tab, dqp, dqf
     )
 
 
-def join_kernel(off_ref, own_ref, near_ref, a2_ref, a4_ref, a6_ref, *refs):
+def join_kernel(off_ref, dq_ref, own_ref, near_ref, a2_ref, a4_ref, a6_ref, *refs):
     out = refs[:COLS]
     acc = refs[COLS]
     _, col = place()
@@ -482,31 +492,30 @@
             value = acc[rows]
             if which == 0:
                 value = value * SCALE
+                out[step][2] = dq_ref[rows]
             out[step][which] = value.astype(BF16)
 
 
-def join(offsets, own, near, a2, a4, a6):
-    piece = jax.ShapeDtypeStruct((2, SLAB, HD), BF16)
+def join(offsets, dq, own, near, a2, a4, a6):
+    piece = jax.ShapeDtypeStruct((3, SLAB, HD), BF16)
     return call(
-        join_kernel, [piece] * COLS, [pltpu.VMEM((ROW, HD), F32)], smem=(0,), nin=6
-    )(offsets, own, near, a2, a4, a6)
+        join_kernel, [piece] * COLS, [pltpu.VMEM((ROW, HD), F32)], smem=(0,), nin=7
+    )(offsets, dq, own, near, a2, a4, a6)
 
 
 def spread_kernel(*refs):
-    dq_in = refs[:COLS]
-    kv_in = refs[COLS : 2 * COLS]
-    q_ref, k_ref, v_ref = refs[2 * COLS :]
+    q_ref, k_ref, v_ref = refs[COLS:]
     _, col = place()
     for step in range(COLS):
         lanes = pl.ds(pl.multiple_of(((col - step + COLS) % COLS) * HD, HD), HD)
-        q_ref[:, lanes] = dq_in[step][...]
-        k_ref[:, lanes] = kv_in[step][0]
-        v_ref[:, lanes] = kv_in[step][1]
-
-
-def spread(dq, dkv):
+        q_ref[:, lanes] = refs[step][2]
+        k_ref[:, lanes] = refs[step][0]
+        v_ref[:, lanes] = refs[step][1]
+
+
+def spread(pieces):
     out = jax.ShapeDtypeStruct((SLAB, COLS * HD), BF16)
-    return call(spread_kernel, [out] * 3, nin=2 * COLS)(*dq, *dkv)
+    return call(spread_kernel, [out] * 3, nin=COLS)(*pieces)
 
 
 def body(planes, query_states, key_states, value_states, out_grad, head_offsets):
@@ -515,23 +524,21 @@
 
     kv = exchange(pack(key_states, value_states))
     qg = exchange(pack(query_states, out_grad))
-    row = stack(kv)
-    prev = along(row, 1, planes)
-    stat_own, qg, tab, qg8 = first_own(head_offsets, row, qg)
-    prev, stat_own = lax.optimization_barrier((prev, stat_own))
-    wide, slim = pair_up(head_offsets, row, prev)
+    first = along(kv[0], 1, planes)
+    first, *rest = lax.optimization_barrier((first, *kv[1:]))
+    rest = along(stack(rest), 1, planes)
+    prev, wide, slim = pair_up(head_offsets, kv, first, rest)
+    prev, qg[0] = lax.optimization_barrier((prev, qg[0]))
+    stat_own, row, qg, tab, qg8 = first_own(head_offsets, kv, qg)
     far = [along(wide, 2, planes), along(slim, 4, planes), along(slim, 6, planes)]
     stat, some, kv8 = first_prev(head_offsets, prev, qg, stat_own)
     fin, h2, h4, h6, dqf, pf = far_part(head_offsets, kv8, qg8, far, stat, some)
     a2, a4, a6 = [along(h, -step, planes) for h, step in ((h2, 2), (h4, 4), (h6, 6))]
     prev_grad, dqp = back_prev(prev, qg, fin)
-    results = back_own(head_offsets, row, qg, fin, tab, dqp, dqf)
-    own, prev_grad = lax.optimization_barrier((results[COLS], prev_grad))
     near = along(merge(head_offsets, prev_grad, pf, a2, a4, a6), -1, planes)
-    dq = exchange(results[:COLS])
-    near, *dq = lax.optimization_barrier((near, *dq))
-    dkv = exchange(join(head_offsets, own, near, a2, a4, a6))
-    return tuple(spread(dq, dkv))
+    own, dq = back_own(head_offsets, row, qg, fin, tab, dqp, dqf)
+    pieces = exchange(join(head_offsets, dq, own, near, a2, a4, a6))
+    return tuple(spread(pieces))
 
 
 def solution(mesh):

time: 79.6 us -> 75 us (0.942)
  starting transfers between devices: 39.1 us -> 30.7 us
  waiting for transfers between devices: 21.6 us -> 25.7 us
    ppermute x8 -> x9, waiting for transfers between devices: 5.25 us -> 17.6 us  [along(): return lax.ppermute(value, 'seq', pairs)]
    ppermute x12 -> x9, waiting for transfers between devices: 16.4 us -> 8.15 us  [across(): return lax.ppermute(value, 'seq', pairs)]
    ppermute x12 -> x9, starting transfers between devices: 20.5 us -> 13.6 us  [across(): return lax.ppermute(value, 'seq', pairs)]
    ppermute x8 -> x9, starting transfers between devices: 18.6 us -> 17 us  [along(): return lax.ppermute(value, 'seq', pairs)]
  transfers between devices with their start and end apart: 20 -> 18, of which waited for: 14 -> 8; matrix products, arithmetic and copies ran while one was open for 0% -> 0% of each run, Pallas kernels for 13% -> 15%
where the time goes in v3:
time: 75 us; the launch traced here: 74.8 us
  starting transfers between devices  30.7 us (41%)
  waiting for transfers between devices  25.7 us (34%)
  Pallas kernels  15.7 us (21%)
  local copies, waits for them, and re-layouts  1.9 us (3%)
  between operations  0.79 us (1%)
    ppermute x9, waiting for transfers between devices, along(): return lax.ppermute(value, 'seq', pairs)  17.6 us
    ppermute x9, starting transfers between devices, along(): return lax.ppermute(value, 'seq', pairs)  17 us
    ppermute x9, starting transfers between devices, across(): return lax.ppermute(value, 'seq', pairs)  13.6 us
    ppermute x9, waiting for transfers between devices, across(): return lax.ppermute(value, 'seq', pairs)  8.15 us
    pallas_call x1, Pallas kernels, back_own(): call(back_own_kernel, out, scratch, smem=(0,), nin=7)  3.25 us
    pallas_call x1, Pallas kernels, back_prev(): return call(back_prev_kernel, out, nin=3)(kv, qg, fin)  2.5 us
    pallas_call x1, Pallas kernels, first_prev(): call(first_prev_kernel, out, scratch, smem=(0,), nin=4)  2.41 us
    pallas_call x1, Pallas kernels, first_own(): call(first_own_kernel, out, scratch, smem=(0,), nin=1 + 2 * COLS)  2.18 us
  transfers between devices with their start and end apart: 18, of which 8 were waited for; matrix products, arithmetic and copies ran while one was open for 0% of the time, Pallas kernels for 15%

profile of v3, /device:TPU:8, one launch (start us, length us, event | category | flops | bytes accessed | tf_op | source)
XLA Modules:
  0.0 74.8 jit_solution(6398902907146648725)
XLA Ops:
  0.6 0.0 copy-start
  0.6 0.9 %copy-done = bf16[256,512]{1,0:T(8,128)(2,1)S(1)} copy-done((bf16[256,512]{1,0:T(8,128)(2,1)S(1)}, bf16[256,512]{1,0:T(8,128)(2,1)}, u32[]{:S(2)}) %copy-start) | copy-done | bytes 262168
  1.6 0.0 copy-start.1
  1.6 0.9 %copy-done.1 = bf16[256,512]{1,0:T(8,128)(2,1)S(1)} copy-done((bf16[256,512]{1,0:T(8,128)(2,1)S(1)}, bf16[256,512]{1,0:T(8,128)(2,1)}, u32[]{:S(2)}) %copy-start.1) | copy-done | bytes 262168
  2.5 0.1 shard_map.76
  2.6 1.6 %collective-permute-start = (bf16[2,256,128]{2,1,0:T(8,128)(2,1)S(1)}, bf16[2,256,128]{2,1,0:T(8,128)(2,1)S(1)}, u32[]{:S(2)}, u32[]{:S(2)}) collective-permute-start(bf16[2,256,128]{2,1,0:T(8,128)(2,1)S(1)} %get-tuple-element.43), channel_id=1, source_target_pairs={{0,8},{8,16},{16,24},{24,0},{32,40},{40,48},{48,56},{56,32},{64,72... | collective-permute-start | bytes 393224 | tf_op jit(solution)/shard_map/ppermute | solution.py:32
  4.2 2.7 %collective-permute-start.1 = (bf16[2,256,128]{2,1,0:T(8,128)(2,1)S(1)}, bf16[2,256,128]{2,1,0:T(8,128)(2,1)S(1)}, u32[]{:S(2)}, u32[]{:S(2)}) collective-permute-start(bf16[2,256,128]{2,1,0:T(8,128)(2,1)S(1)} %get-tuple-element.44), channel_id=1, source_target_pairs={{0,16},{8,24},{16,0},{24,8},{32,48},{40,56},{48,32},{56,40},{64,80... | collective-permute-start | bytes 393224 | tf_op jit(solution)/shard_map/ppermute | solution.py:32
  6.9 1.4 %collective-permute-start.2 = (bf16[2,256,128]{2,1,0:T(8,128)(2,1)S(1)}, bf16[2,256,128]{2,1,0:T(8,128)(2,1)S(1)}, u32[]{:S(2)}, u32[]{:S(2)}) collective-permute-start(bf16[2,256,128]{2,1,0:T(8,128)(2,1)S(1)} %get-tuple-element.45), channel_id=1, source_target_pairs={{0,24},{8,0},{16,8},{24,16},{32,56},{40,32},{48,40},{56,48},{64,88... | collective-permute-start | bytes 393224 | tf_op jit(solution)/shard_map/ppermute | solution.py:32
  8.4 0.0 copy-start.2
  8.4 0.0 copy-start.3
  8.4 1.9 %collective-permute-start.3 = (bf16[2,256,128]{2,1,0:T(8,128)(2,1)S(1)}, bf16[2,256,128]{2,1,0:T(8,128)(2,1)S(1)}, u32[]{:S(2)}, u32[]{:S(2)}) collective-permute-start(bf16[2,256,128]{2,1,0:T(8,128)(2,1)S(1)} %get-tuple-element.42.refs_0_), channel_id=1, source_target_pairs={{0,32},{8,40},{16,48},{24,56},{32,64},{40,72},{48,80},{56,88},{64,... | collective-permute-start | bytes 393224 | tf_op jit(solution)/shard_map/ppermute | solution.py:39
  10.3 0.0 collective-permute-done.refs_0_.refs_1_
  10.3 2.7 %collective-permute-done.1.refs_1_.refs_2_ = bf16[2,256,128]{2,1,0:T(8,128)(2,1)S(1)} collective-permute-done((bf16[2,256,128]{2,1,0:T(8,128)(2,1)S(1)}, bf16[2,256,128]{2,1,0:T(8,128)(2,1)S(1)}, u32[]{:S(2)}, u32[]{:S(2)}) %collective-permute-start.1) | collective-permute-done | bytes 131104 | tf_op jit(solution)/shard_map/ppermute | solution.py:32
  13.0 0.0 collective-permute-done.2.refs_2_.refs_3_
  13.0 4.2 %collective-permute-done.3.refs_4_ = bf16[2,256,128]{2,1,0:T(8,128)(2,1)S(1)} collective-permute-done((bf16[2,256,128]{2,1,0:T(8,128)(2,1)S(1)}, bf16[2,256,128]{2,1,0:T(8,128)(2,1)S(1)}, u32[]{:S(2)}, u32[]{:S(2)}) %collective-permute-start.3) | collective-permute-done | bytes 131104 | tf_op jit(solution)/shard_map/ppermute | solution.py:39
  17.2 0.1 collective-permute-start.4
  17.3 0.0 copy-done.2
  17.3 0.0 copy-done.3
  17.3 0.1 shard_map.79
  17.4 0.7 collective-permute-start.5
  18.1 0.0 copy-start.4
  18.1 0.9 %collective-permute-start.6 = (bf16[2,256,128]{2,1,0:T(8,128)(2,1)S(1)}, bf16[2,256,128]{2,1,0:T(8,128)(2,1)S(1)}, u32[]{:S(2)}, u32[]{:S(2)}) collective-permute-start(bf16[2,256,128]{2,1,0:T(8,128)(2,1)S(1)} %get-tuple-element.54), channel_id=1, source_target_pairs={{0,16},{8,24},{16,0},{24,8},{32,48},{40,56},{48,32},{56,40},{64,80... | collective-permute-start | bytes 393224 | tf_op jit(solution)/shard_map/ppermute | solution.py:32
  19.0 1.9 %collective-permute-start.7 = (bf16[2,256,128]{2,1,0:T(8,128)(2,1)S(1)}, bf16[2,256,128]{2,1,0:T(8,128)(2,1)S(1)}, u32[]{:S(2)}, u32[]{:S(2)}) collective-permute-start(bf16[2,256,128]{2,1,0:T(8,128)(2,1)S(1)} %get-tuple-element.55), channel_id=1, source_target_pairs={{0,24},{8,0},{16,8},{24,16},{32,56},{40,32},{48,40},{56,48},{64,88... | collective-permute-start | bytes 393224 | tf_op jit(solution)/shard_map/ppermute | solution.py:32
  20.9 6.7 %collective-permute-done.4.refs_5_ = bf16[2,768,128]{2,1,0:T(8,128)(2,1)S(1)} collective-permute-done((bf16[2,768,128]{2,1,0:T(8,128)(2,1)S(1)}, bf16[2,768,128]{2,1,0:T(8,128)(2,1)S(1)}, u32[]{:S(2)}, u32[]{:S(2)}) %collective-permute-start.4) | collective-permute-done | bytes 393248 | tf_op jit(solution)/shard_map/ppermute | solution.py:39
  27.6 0.0 copy-done.4
  27.6 1.0 %shard_map.78 = (bf16[2,1024,128]{2,1,0:T(8,128)(2,1)S(1)}, bf16[2,2,64,128]{3,2,1,0:T(8,128)(2,1)S(1)}, bf16[2,2,32,128]{3,2,1,0:T(8,128)(2,1)S(1)}) custom-call(s32[4]{0:T(128)S(1)} %copy-done.4, bf16[2,256,128]{2,1,0:T(8,128)(2,1)S(1)} %get-tuple-element.42.refs_0_, bf16[2,256,128]{2,1,0:T(8,128)(2,1)S(1)} %collective-permute-done.refs_0_.refs_1_, ...), custom_call_target="tpu_custom_call" | custom-call | flops 1 | bytes 1 | tf_op jit(solution)/shard_map/pallas_call | solution.py:142
  28.6 0.1 collective-permute-start.8
  28.7 4.1 %collective-permute-start.10 = (bf16[2,2,32,128]{3,2,1,0:T(8,128)(2,1)S(1)}, bf16[2,2,32,128]{3,2,1,0:T(8,128)(2,1)S(1)}, u32[]{:S(2)}, u32[]{:S(2)}) collective-permute-start(bf16[2,2,32,128]{3,2,1,0:T(8,128)(2,1)S(1)} %get-tuple-element.63), channel_id=1, source_target_pairs={{0,192},{8,200},{16,208},{24,216},{32,224},{40,232},{48,240},{56,2... | collective-permute-start | bytes 98312 | tf_op jit(solution)/shard_map/ppermute | solution.py:39
  32.8 0.0 collective-permute-done.5.refs_5_
  32.8 4.6 %collective-permute-start.9 = (bf16[2,2,32,128]{3,2,1,0:T(8,128)(2,1)S(1)}, bf16[2,2,32,128]{3,2,1,0:T(8,128)(2,1)S(1)}, u32[]{:S(2)}, u32[]{:S(2)}) collective-permute-start(bf16[2,2,32,128]{3,2,1,0:T(8,128)(2,1)S(1)} %get-tuple-element.63), channel_id=1, source_target_pairs={{0,128},{8,136},{16,144},{24,152},{32,160},{40,168},{48,176},{56,1... | collective-permute-start | bytes 98312 | tf_op jit(solution)/shard_map/ppermute | solution.py:39
  37.4 0.0 collective-permute-done.6.refs_6_
  37.4 0.0 collective-permute-done.7.refs_7_
  37.4 2.2 %shard_map.80 = (f32[8,1024]{1,0:T(8,128)S(1)}, bf16[2,1024,128]{2,1,0:T(8,128)(2,1)S(1)}, bf16[2,1024,128]{2,1,0:T(8,128)(2,1)S(1)}, f32[2,256,256]{2,1,0:T(8,128)S(1)}, bf16[2,128,128]{2,1,0:T(8,128)(2,1)S(1)}) custom-call(s32[4]{0:T(128)S(1)} %copy-done.4, bf16[2,256,128]{2,1,0:T(8,128)(2,1)S(1)} %get-tuple-element.42.refs_0_, ...), custom_call_target="tpu_custom_call" | custom-call | flops 1 | bytes 1 | tf_op jit(solution)/shard_map/pallas_call | solution.py:219
  39.6 2.4 %shard_map.81 = (f32[8,1024]{1,0:T(8,128)S(1)}, f32[8,128]{1,0:T(8,128)S(1)}, bf16[2,128,128]{2,1,0:T(8,128)(2,1)S(1)}) custom-call(s32[4]{0:T(128)S(1)} %copy-done.4, bf16[2,1024,128]{2,1,0:T(8,128)(2,1)S(1)} %get-tuple-element.58.kv_ref, bf16[2,1024,128]{2,1,0:T(8,128)(2,1)S(1)} %get-tuple-element.57.qg_ref, f32[8,1024]{1,0:T(8,128)S(1)} %get-tuple-element.59.so_ref), custom_call_target="tpu_custom_call" | custom-call | flops 1 | bytes 1 | tf_op jit(solution)/shard_map/pallas_call | solution.py:285
  42.0 0.0 collective-permute-done.10.g6_ref
  42.0 0.0 collective-permute-done.9.g4_ref
  42.0 0.0 collective-permute-done.8.g2_ref
  42.1 1.5 %shard_map.82 = (f32[8,1024]{1,0:T(8,128)S(1)}, bf16[2,2,64,128]{3,2,1,0:T(8,128)(2,1)S(1)}, bf16[2,2,32,128]{3,2,1,0:T(8,128)(2,1)S(1)}, bf16[2,2,32,128]{3,2,1...) custom-call(s32[4]{0:T(128)S(1)} %copy-done.4, ...), custom_call_target="tpu_custom_call" | custom-call | flops 1 | bytes 1 | tf_op jit(solution)/shard_map/pallas_call | solution.py:378
  43.6 0.1 collective-permute-start.11
  43.7 3.3 %collective-permute-start.12 = (bf16[2,2,32,128]{3,2,1,0:T(8,128)(2,1)S(1)}, bf16[2,2,32,128]{3,2,1,0:T(8,128)(2,1)S(1)}, u32[]{:S(2)}, u32[]{:S(2)}) collective-permute-start(bf16[2,2,32,128]{3,2,1,0:T(8,128)(2,1)S(1)} %get-tuple-element.75), channel_id=1, source_target_pairs={{0,128},{8,136},{16,144},{24,152},{32,160},{40,168},{48,176},{56,1... | collective-permute-start | bytes 98312 | tf_op jit(solution)/shard_map/ppermute | solution.py:39
  46.9 2.8 %collective-permute-start.13 = (bf16[2,2,32,128]{3,2,1,0:T(8,128)(2,1)S(1)}, bf16[2,2,32,128]{3,2,1,0:T(8,128)(2,1)S(1)}, u32[]{:S(2)}, u32[]{:S(2)}) collective-permute-start(bf16[2,2,32,128]{3,2,1,0:T(8,128)(2,1)S(1)} %get-tuple-element.76), channel_id=1, source_target_pairs={{0,64},{8,72},{16,80},{24,88},{32,96},{40,104},{48,112},{56,120},{... | collective-permute-start | bytes 98312 | tf_op jit(solution)/shard_map/ppermute | solution.py:39
  49.7 2.5 %shard_map.83 = (f32[2,1024,128]{2,1,0:T(8,128)S(1)}, f32[128,1024]{1,0:T(8,128)S(1)}) custom-call(bf16[2,1024,128]{2,1,0:T(8,128)(2,1)S(1)} %get-tuple-element.58.kv_ref, bf16[2,1024,128]{2,1,0:T(8,128)(2,1)S(1)} %get-tuple-element.57.qg_ref, f32[8,1024]{1,0:T(8,128)S(1)} %get-tuple-element.66.fin_ref), custom_call_target="tpu_custom_call" | custom-call | flops 1 | bytes 1 | tf_op jit(solution)/shard_map/pallas_call | solution.py:412
  52.2 0.0 collective-permute-done.12.a4_ref
  52.3 0.7 collective-permute-done.13.a6_ref
  52.9 0.0 collective-permute-done.11.a2_ref
  53.0 0.8 %shard_map.85 = bf16[2,1024,128]{2,1,0:T(8,128)(2,1)S(1)} custom-call(s32[4]{0:T(128)S(1)} %copy-done.4, f32[2,1024,128]{2,1,0:T(8,128)S(1)} %get-tuple-element.72.prev_ref, f32[2,128,128]{2,1,0:T(8,128)S(1)} %get-tuple-element.73.pf_ref, bf16[2,2,64,128]{3,2,1,0:T(8,128)(2,1)S(1)} %collective-permute-done.11.a2_ref, ...), custom_call_target="tpu_custom_call" | custom-call | flops 1 | bytes 1 | tf_op jit(solution)/shard_map/pallas_call | solution.py:433
  53.8 0.1 collective-permute-start.14
  53.9 3.3 %shard_map.84 = (f32[2,1024,128]{2,1,0:T(8,128)S(1)}, bf16[1024,128]{1,0:T(8,128)(2,1)S(1)}) custom-call(s32[4]{0:T(128)S(1)} %copy-done.4, bf16[2,1024,128]{2,1,0:T(8,128)(2,1)S(1)} %get-tuple-element.56.kv_ref, bf16[2,1024,128]{2,1,0:T(8,128)(2,1)S(1)} %get-tuple-element.57.qg_ref, f32[8,1024]{1,0:T(8,128)S(1)} %get-tuple-element.66.fin_ref, ...), custom_call_target="tpu_custom_call" | custom-call | flops 1 | bytes 1 | tf_op jit(solution)/shard_map/pallas_call | solution.py:472
  57.1 5.9 %collective-permute-done.14.near_ref = bf16[2,1024,128]{2,1,0:T(8,128)(2,1)S(1)} collective-permute-done((bf16[2,1024,128]{2,1,0:T(8,128)(2,1)S(1)}, bf16[2,1024,128]{2,1,0:T(8,128)(2,1)S(1)}, u32[]{:S(2)}, u32[]{:S(2)}) %collective-permute-start.14) | collective-permute-done | bytes 524320 | tf_op jit(solution)/shard_map/ppermute | solution.py:39
  63.0 0.8 %shard_map.86 = (bf16[3,256,128]{2,1,0:T(8,128)(2,1)S(1)}, bf16[3,256,128]{2,1,0:T(8,128)(2,1)S(1)}, bf16[3,256,128]{2,1,0:T(8,128)(2,1)S(1)}, bf16[3,256,128]{2,1,0:T(8,128)(2,1)S(1)}) custom-call(s32[4]{0:T(128)S(1)} %copy-done.4, bf16[1024,128]{1,0:T(8,128)(2,1)S(1)} %get-tuple-element.70.dq_ref, f32[2,1024,128]{2,1,0:T(8,128)S(1)} %get-tuple-element.71.own_ref, ...), custom_call_target="tpu_custom_call" | custom-call | flops 1 | bytes 1 | tf_op jit(solution)/shard_map/pallas_call | solution.py:501
  63.9 0.9 %collective-permute-start.15 = (bf16[3,256,128]{2,1,0:T(8,128)(2,1)S(1)}, bf16[3,256,128]{2,1,0:T(8,128)(2,1)S(1)}, u32[]{:S(2)}, u32[]{:S(2)}) collective-permute-start(bf16[3,256,128]{2,1,0:T(8,128)(2,1)S(1)} %get-tuple-element.78), channel_id=1, source_target_pairs={{0,8},{8,16},{16,24},{24,0},{32,40},{40,48},{48,56},{56,32},{64,72... | collective-permute-start | bytes 589832 | tf_op jit(solution)/shard_map/ppermute | solution.py:32
  64.8 2.9 %collective-permute-start.16 = (bf16[3,256,128]{2,1,0:T(8,128)(2,1)S(1)}, bf16[3,256,128]{2,1,0:T(8,128)(2,1)S(1)}, u32[]{:S(2)}, u32[]{:S(2)}) collective-permute-start(bf16[3,256,128]{2,1,0:T(8,128)(2,1)S(1)} %get-tuple-element.79), channel_id=1, source_target_pairs={{0,16},{8,24},{16,0},{24,8},{32,48},{40,56},{48,32},{56,40},{64,80... | collective-permute-start | bytes 589832 | tf_op jit(solution)/shard_map/ppermute | solution.py:32
  67.7 0.6 collective-permute-start.17
  68.3 2.5 %collective-permute-done.15.refs_1_ = bf16[3,256,128]{2,1,0:T(8,128)(2,1)S(1)} collective-permute-done((bf16[3,256,128]{2,1,0:T(8,128)(2,1)S(1)}, bf16[3,256,128]{2,1,0:T(8,128)(2,1)S(1)}, u32[]{:S(2)}, u32[]{:S(2)}) %collective-permute-start.15) | collective-permute-done | bytes 196640 | tf_op jit(solution)/shard_map/ppermute | solution.py:32
  70.8 2.6 %collective-permute-done.16.refs_2_ = bf16[3,256,128]{2,1,0:T(8,128)(2,1)S(1)} collective-permute-done((bf16[3,256,128]{2,1,0:T(8,128)(2,1)S(1)}, bf16[3,256,128]{2,1,0:T(8,128)(2,1)S(1)}, u32[]{:S(2)}, u32[]{:S(2)}) %collective-permute-start.16) | collective-permute-done | bytes 196640 | tf_op jit(solution)/shard_map/ppermute | solution.py:32
  73.5 0.3 collective-permute-done.17.refs_3_
  73.8 1.0 %shard_map.87 = (bf16[256,512]{1,0:T(8,128)(2,1)}, bf16[256,512]{1,0:T(8,128)(2,1)}, bf16[256,512]{1,0:T(8,128)(2,1)}) custom-call(bf16[3,256,128]{2,1,0:T(8,128)(2,1)S(1)} %get-tuple-element.77.refs_0_, bf16[3,256,128]{2,1,0:T(8,128)(2,1)S(1)} %collective-permute-done.15.refs_1_, bf16[3,256,128]{2,1,0:T(8,128)(2,1)S(1)} %collective-permute-done.16.refs_2_, ...), custom_call_target="tpu_custom_call" | custom-call | flops 1 | bytes 1 | tf_op jit(solution)/shard_map/pallas_call | solution.py:518
  (1 shorter events, 0.0 us)
Async XLA Ops:
  0.6 1.0 %copy-start = (bf16[256,512]{1,0:T(8,128)(2,1)S(1)}, bf16[256,512]{1,0:T(8,128)(2,1)}, u32[]{:S(2)}) copy-start(bf16[256,512]{1,0:T(8,128)(2,1)} %one_ref.2) | copy-start | bytes 786436
  1.6 0.9 %copy-start.1 = (bf16[256,512]{1,0:T(8,128)(2,1)S(1)}, bf16[256,512]{1,0:T(8,128)(2,1)}, u32[]{:S(2)}) copy-start(bf16[256,512]{1,0:T(8,128)(2,1)} %two_ref.2) | copy-start | bytes 786436
  2.6 7.7 %collective-permute-start = (bf16[2,256,128]{2,1,0:T(8,128)(2,1)S(1)}, bf16[2,256,128]{2,1,0:T(8,128)(2,1)S(1)}, u32[]{:S(2)}, u32[]{:S(2)}) collective-permute-start(bf16[2,256,128]{2,1,0:T(8,128)(2,1)S(1)} %get-tuple-element.43), channel_id=1, source_target_pairs={{0,8},{8,16},{16,24},{24,0},{32,40},{40,48},{48,56},{56,32},{64,72... | collective-permute-start | bytes 393224 | tf_op jit(solution)/shard_map/ppermute | solution.py:32
  4.2 8.7 %collective-permute-start.1 = (bf16[2,256,128]{2,1,0:T(8,128)(2,1)S(1)}, bf16[2,256,128]{2,1,0:T(8,128)(2,1)S(1)}, u32[]{:S(2)}, u32[]{:S(2)}) collective-permute-start(bf16[2,256,128]{2,1,0:T(8,128)(2,1)S(1)} %get-tuple-element.44), channel_id=1, source_target_pairs={{0,16},{8,24},{16,0},{24,8},{32,48},{40,56},{48,32},{56,40},{64,80... | collective-permute-start | bytes 393224 | tf_op jit(solution)/shard_map/ppermute | solution.py:32
  6.9 6.0 %collective-permute-start.2 = (bf16[2,256,128]{2,1,0:T(8,128)(2,1)S(1)}, bf16[2,256,128]{2,1,0:T(8,128)(2,1)S(1)}, u32[]{:S(2)}, u32[]{:S(2)}) collective-permute-start(bf16[2,256,128]{2,1,0:T(8,128)(2,1)S(1)} %get-tuple-element.45), channel_id=1, source_target_pairs={{0,24},{8,0},{16,8},{24,16},{32,56},{40,32},{48,40},{56,48},{64,88... | collective-permute-start | bytes 393224 | tf_op jit(solution)/shard_map/ppermute | solution.py:32
  8.4 8.9 %copy-start.2 = (bf16[256,512]{1,0:T(8,128)(2,1)S(1)}, bf16[256,512]{1,0:T(8,128)(2,1)}, u32[]{:S(2)}) copy-start(bf16[256,512]{1,0:T(8,128)(2,1)} %one_ref.3) | copy-start | bytes 786436
  8.4 8.9 %copy-start.3 = (bf16[256,512]{1,0:T(8,128)(2,1)S(1)}, bf16[256,512]{1,0:T(8,128)(2,1)}, u32[]{:S(2)}) copy-start(bf16[256,512]{1,0:T(8,128)(2,1)} %two_ref.3) | copy-start | bytes 786436
  8.4 8.8 %collective-permute-start.3 = (bf16[2,256,128]{2,1,0:T(8,128)(2,1)S(1)}, bf16[2,256,128]{2,1,0:T(8,128)(2,1)S(1)}, u32[]{:S(2)}, u32[]{:S(2)}) collective-permute-start(bf16[2,256,128]{2,1,0:T(8,128)(2,1)S(1)} %get-tuple-element.42.refs_0_), channel_id=1, source_target_pairs={{0,32},{8,40},{16,48},{24,56},{32,64},{40,72},{48,80},{56,88},{64,... | collective-permute-start | bytes 393224 | tf_op jit(solution)/shard_map/ppermute | solution.py:39
  17.2 10.4 %collective-permute-start.4 = (bf16[2,768,128]{2,1,0:T(8,128)(2,1)S(1)}, bf16[2,768,128]{2,1,0:T(8,128)(2,1)S(1)}, u32[]{:S(2)}, u32[]{:S(2)}) collective-permute-start(bf16[2,768,128]{2,1,0:T(8,128)(2,1)S(1)} %shard_map.77), channel_id=1, source_target_pairs={{0,32},{8,40},{16,48},{24,56},{32,64},{40,72},{48,80},{56,88},{64,... | collective-permute-start | bytes 1179656 | tf_op jit(solution)/shard_map/ppermute | solution.py:39
  17.4 15.4 %collective-permute-start.5 = (bf16[2,256,128]{2,1,0:T(8,128)(2,1)S(1)}, bf16[2,256,128]{2,1,0:T(8,128)(2,1)S(1)}, u32[]{:S(2)}, u32[]{:S(2)}) collective-permute-start(bf16[2,256,128]{2,1,0:T(8,128)(2,1)S(1)} %get-tuple-element.53), channel_id=1, source_target_pairs={{0,8},{8,16},{16,24},{24,0},{32,40},{40,48},{48,56},{56,32},{64,72... | collective-permute-start | bytes 393224 | tf_op jit(solution)/shard_map/ppermute | solution.py:32
  18.1 9.5 %copy-start.4 = (s32[4]{0:T(128)S(1)}, s32[4]{0:T(128)}, u32[]{:S(2)}) copy-start(s32[4]{0:T(128)} %off_ref.13) | copy-start | bytes 52
  18.1 19.3 %collective-permute-start.6 = (bf16[2,256,128]{2,1,0:T(8,128)(2,1)S(1)}, bf16[2,256,128]{2,1,0:T(8,128)(2,1)S(1)}, u32[]{:S(2)}, u32[]{:S(2)}) collective-permute-start(bf16[2,256,128]{2,1,0:T(8,128)(2,1)S(1)} %get-tuple-element.54), channel_id=1, source_target_pairs={{0,16},{8,24},{16,0},{24,8},{32,48},{40,56},{48,32},{56,40},{64,80... | collective-permute-start | bytes 393224 | tf_op jit(solution)/shard_map/ppermute | solution.py:32
  19.0 18.4 %collective-permute-start.7 = (bf16[2,256,128]{2,1,0:T(8,128)(2,1)S(1)}, bf16[2,256,128]{2,1,0:T(8,128)(2,1)S(1)}, u32[]{:S(2)}, u32[]{:S(2)}) collective-permute-start(bf16[2,256,128]{2,1,0:T(8,128)(2,1)S(1)} %get-tuple-element.55), channel_id=1, source_target_pairs={{0,24},{8,0},{16,8},{24,16},{32,56},{40,32},{48,40},{56,48},{64,88... | collective-permute-start | bytes 393224 | tf_op jit(solution)/shard_map/ppermute | solution.py:32
  28.6 13.4 %collective-permute-start.8 = (bf16[2,2,64,128]{3,2,1,0:T(8,128)(2,1)S(1)}, bf16[2,2,64,128]{3,2,1,0:T(8,128)(2,1)S(1)}, u32[]{:S(2)}, u32[]{:S(2)}) collective-permute-start(bf16[2,2,64,128]{3,2,1,0:T(8,128)(2,1)S(1)} %get-tuple-element.62), channel_id=1, source_target_pairs={{0,64},{8,72},{16,80},{24,88},{32,96},{40,104},{48,112},{56,120},{... | collective-permute-start | bytes 196616 | tf_op jit(solution)/shard_map/ppermute | solution.py:39
  28.7 13.3 %collective-permute-start.10 = (bf16[2,2,32,128]{3,2,1,0:T(8,128)(2,1)S(1)}, bf16[2,2,32,128]{3,2,1,0:T(8,128)(2,1)S(1)}, u32[]{:S(2)}, u32[]{:S(2)}) collective-permute-start(bf16[2,2,32,128]{3,2,1,0:T(8,128)(2,1)S(1)} %get-tuple-element.63), channel_id=1, source_target_pairs={{0,192},{8,200},{16,208},{24,216},{32,224},{40,232},{48,240},{56,2... | collective-permute-start | bytes 98312 | tf_op jit(solution)/shard_map/ppermute | solution.py:39
  32.8 9.2 %collective-permute-start.9 = (bf16[2,2,32,128]{3,2,1,0:T(8,128)(2,1)S(1)}, bf16[2,2,32,128]{3,2,1,0:T(8,128)(2,1)S(1)}, u32[]{:S(2)}, u32[]{:S(2)}) collective-permute-start(bf16[2,2,32,128]{3,2,1,0:T(8,128)(2,1)S(1)} %get-tuple-element.63), channel_id=1, source_target_pairs={{0,128},{8,136},{16,144},{24,152},{32,160},{40,168},{48,176},{56,1... | collective-permute-start | bytes 98312 | tf_op jit(solution)/shard_map/ppermute | solution.py:39
  43.6 9.4 %collective-permute-start.11 = (bf16[2,2,64,128]{3,2,1,0:T(8,128)(2,1)S(1)}, bf16[2,2,64,128]{3,2,1,0:T(8,128)(2,1)S(1)}, u32[]{:S(2)}, u32[]{:S(2)}) collective-permute-start(bf16[2,2,64,128]{3,2,1,0:T(8,128)(2,1)S(1)} %get-tuple-element.74), channel_id=1, source_target_pairs={{0,192},{8,200},{16,208},{24,216},{32,224},{40,232},{48,240},{56,2... | collective-permute-start | bytes 196616 | tf_op jit(solution)/shard_map/ppermute | solution.py:39
  43.7 8.6 %collective-permute-start.12 = (bf16[2,2,32,128]{3,2,1,0:T(8,128)(2,1)S(1)}, bf16[2,2,32,128]{3,2,1,0:T(8,128)(2,1)S(1)}, u32[]{:S(2)}, u32[]{:S(2)}) collective-permute-start(bf16[2,2,32,128]{3,2,1,0:T(8,128)(2,1)S(1)} %get-tuple-element.75), channel_id=1, source_target_pairs={{0,128},{8,136},{16,144},{24,152},{32,160},{40,168},{48,176},{56,1... | collective-permute-start | bytes 98312 | tf_op jit(solution)/shard_map/ppermute | solution.py:39
  46.9 6.0 %collective-permute-start.13 = (bf16[2,2,32,128]{3,2,1,0:T(8,128)(2,1)S(1)}, bf16[2,2,32,128]{3,2,1,0:T(8,128)(2,1)S(1)}, u32[]{:S(2)}, u32[]{:S(2)}) collective-permute-start(bf16[2,2,32,128]{3,2,1,0:T(8,128)(2,1)S(1)} %get-tuple-element.76), channel_id=1, source_target_pairs={{0,64},{8,72},{16,80},{24,88},{32,96},{40,104},{48,112},{56,120},{... | collective-permute-start | bytes 98312 | tf_op jit(solution)/shard_map/ppermute | solution.py:39
  53.8 9.3 %collective-permute-start.14 = (bf16[2,1024,128]{2,1,0:T(8,128)(2,1)S(1)}, bf16[2,1024,128]{2,1,0:T(8,128)(2,1)S(1)}, u32[]{:S(2)}, u32[]{:S(2)}) collective-permute-start(bf16[2,1024,128]{2,1,0:T(8,128)(2,1)S(1)} %shard_map.85), channel_id=1, source_target_pairs={{0,224},{8,232},{16,240},{24,248},{32,0},{40,8},{48,16},{56,24},{6... | collective-permute-start | bytes 1572872 | tf_op jit(solution)/shard_map/ppermute | solution.py:39
  63.9 7.0 %collective-permute-start.15 = (bf16[3,256,128]{2,1,0:T(8,128)(2,1)S(1)}, bf16[3,256,128]{2,1,0:T(8,128)(2,1)S(1)}, u32[]{:S(2)}, u32[]{:S(2)}) collective-permute-start(bf16[3,256,128]{2,1,0:T(8,128)(2,1)S(1)} %get-tuple-element.78), channel_id=1, source_target_pairs={{0,8},{8,16},{16,24},{24,0},{32,40},{40,48},{48,56},{56,32},{64,72... | collective-permute-start | bytes 589832 | tf_op jit(solution)/shard_map/ppermute | solution.py:32
  64.8 8.7 %collective-permute-start.16 = (bf16[3,256,128]{2,1,0:T(8,128)(2,1)S(1)}, bf16[3,256,128]{2,1,0:T(8,128)(2,1)S(1)}, u32[]{:S(2)}, u32[]{:S(2)}) collective-permute-start(bf16[3,256,128]{2,1,0:T(8,128)(2,1)S(1)} %get-tuple-element.79), channel_id=1, source_target_pairs={{0,16},{8,24},{16,0},{24,8},{32,48},{40,56},{48,32},{56,40},{64,80... | collective-permute-start | bytes 589832 | tf_op jit(solution)/shard_map/ppermute | solution.py:32
  67.7 6.1 %collective-permute-start.17 = (bf16[3,256,128]{2,1,0:T(8,128)(2,1)S(1)}, bf16[3,256,128]{2,1,0:T(8,128)(2,1)S(1)}, u32[]{:S(2)}, u32[]{:S(2)}) collective-permute-start(bf16[3,256,128]{2,1,0:T(8,128)(2,1)S(1)} %get-tuple-element.80), channel_id=1, source_target_pairs={{0,24},{8,0},{16,8},{24,16},{32,56},{40,32},{48,40},{56,48},{64,88... | collective-permute-start | bytes 589832 | tf_op jit(solution)/shard_map/ppermute | solution.py:32

commit v4 on v3

--- a/solution.py
+++ b/solution.py
@@ -25,6 +25,9 @@
 BF16 = jnp.bfloat16
 
 
+ORDER = (0, 2, 1, 3)
+
+
 def across(value, step, planes):
     pairs = [
         (p * COLS + c, p * COLS + (c + step) % COLS) for p in range(planes) for c in range(COLS)
@@ -114,9 +117,9 @@
     out_ref[which, pl.ds(pl.multiple_of(slab * SLAB, SLAB), SLAB)] = value
 
 
-def pair_kernel(off_ref, *refs):
+def prep_kernel(off_ref, *refs):
     mine = refs[:COLS]
-    first_ref, rest_ref, prev_ref, wide_ref, slim_ref = refs[COLS:]
+    row_ref, wide_ref, slim_ref, tab_ref = refs[COLS:]
     _, col = place()
     off = off_ref[col]
     by16 = pick(16, off % 16, THIN16, SLAB)
@@ -126,20 +129,55 @@
         few = pl.ds(pl.multiple_of(slab * THIN16, THIN16), THIN16)
         less = pl.ds(pl.multiple_of(slab * THIN32, THIN32), THIN32)
         for which in range(2):
-            back = first_ref[which] if step == 0 else rest_ref[which, rows_of(step - 1)]
+            value = mine[step][which]
+            place_rows(row_ref, col, step, which, value)
+            wide_ref[which, few] = nn(by16, value).astype(BF16)
+            slim_ref[which, less] = nn(by32, value).astype(BF16)
+    deep_k = depth_of(iota((SLAB, HD), 0), off)
+    deep_k = jnp.concatenate([deep_k, deep_k], axis=1)
+    deep_q = depth_of(iota((8, SLAB), 1), off)[:1]
+    both = jnp.minimum(deep_k, deep_q)
+    tab_ref[0] = 1.0 + jnp.maximum(both - 1.0, 0.0)
+    tab_ref[1] = 1.0 + both
+
+
+def prepare(offsets, mine):
+    out = [
+        jax.ShapeDtypeStruct((2, ROW, HD), BF16),
+        jax.ShapeDtypeStruct((2, FAR16, HD), BF16),
+        jax.ShapeDtypeStruct((2, FAR32, HD), BF16),
+        jax.ShapeDtypeStruct((2, SLAB, SLAB), F32),
+    ]
+    return call(prep_kernel, out, smem=(0,), nin=1 + COLS)(offsets, *mine)
+
+
+def pair_kernel(off_ref, mw_ref, ms_ref, first_ref, rest_ref, prev_ref, wide_ref, slim_ref):
+    _, col = place()
+    off = off_ref[col]
+    by16 = pick(16, off % 16, THIN16, SLAB)
+    by32 = pick(32, off % 32, THIN32, SLAB)
+    wide_ref[0] = mw_ref[...]
+    slim_ref[0] = ms_ref[...]
+    for step in range(COLS):
+        slab = (col - step + COLS) % COLS
+        few = pl.ds(pl.multiple_of(slab * THIN16, THIN16), THIN16)
+        less = pl.ds(pl.multiple_of(slab * THIN32, THIN32), THIN32)
+        for which in range(2):
+            back = first_ref[which]
+            if step > 0:
+                back = rest_ref[which, rows_of(ORDER.index(step) - 1)]
             place_rows(prev_ref, col, step, which, back)
-            for j, value in enumerate((mine[step][which], back)):
-                wide_ref[j, which, few] = nn(by16, value).astype(BF16)
-                slim_ref[j, which, less] = nn(by32, value).astype(BF16)
-
-
-def pair_up(offsets, mine, first, rest):
+            wide_ref[1, which, few] = nn(by16, back).astype(BF16)
+            slim_ref[1, which, less] = nn(by32, back).astype(BF16)
+
+
+def pair_up(offsets, mine_wide, mine_slim, first, rest):
     out = [
         jax.ShapeDtypeStruct((2, ROW, HD), BF16),
         jax.ShapeDtypeStruct((2, 2, FAR16, HD), BF16),
         jax.ShapeDtypeStruct((2, 2, FAR32, HD), BF16),
     ]
-    return call(pair_kernel, out, smem=(0,), nin=3 + COLS)(offsets, *mine, first, rest)
+    return call(pair_kernel, out, smem=(0,), nin=5)(offsets, mine_wide, mine_slim, first, rest)
 
 
 def depth_of(index, off):
@@ -161,24 +199,16 @@
             few_ref[which, rows] = nn(thin8, from_ref[which, rows_of(b)]).astype(BF16)
 
 
-def first_own_kernel(off_ref, *refs):
-    kv = refs[:COLS]
-    qg = refs[COLS : 2 * COLS]
-    stat_ref, kv_ref, qg_ref, tab_ref, few_ref, sc = refs[2 * COLS :]
+def first_own_kernel(off_ref, kv_ref, tab_ref, *refs):
+    qg = refs[:COLS]
+    stat_ref, qg_ref, few_ref, sc = refs[COLS:]
     _, col = place()
     off = off_ref[col]
     thin8 = pick(8, off % 8, SLAB // 8, SLAB)
     for step in range(COLS):
         for which in range(2):
-            place_rows(kv_ref, col, step, which, kv[step][which])
             place_rows(qg_ref, col, step, which, qg[step][which])
     thinned(thin8, qg_ref, few_ref)
-    deep_k = depth_of(iota((SLAB, HD), 0), off)
-    deep_k = jnp.concatenate([deep_k, deep_k], axis=1)
-    deep_q = depth_of(iota((8, SLAB), 1), off)[:1]
-    both = jnp.minimum(deep_k, deep_q)
-    tab_ref[0] = 1.0 + jnp.maximum(both - 1.0, 0.0)
-    tab_ref[1] = 1.0 + both
     stat_ref[...] = jnp.zeros((8, ROW), F32)
     seen = iota((SLAB, SLAB), 0) <= iota((SLAB, SLAB), 1)
     for qb in range(COLS):
@@ -207,18 +237,14 @@
         stat_ref[2:3, lanes] = dot
 
 
-def first_own(offsets, kv, qg):
+def first_own(offsets, kv, tab, qg):
     out = [
         jax.ShapeDtypeStruct((8, ROW), F32),
         jax.ShapeDtypeStruct((2, ROW, HD), BF16),
-        jax.ShapeDtypeStruct((2, ROW, HD), BF16),
-        jax.ShapeDtypeStruct((2, SLAB, SLAB), F32),
         jax.ShapeDtypeStruct((2, FAR8, HD), BF16),
     ]
     scratch = [pltpu.VMEM((ROW, SLAB), F32)]
-    return call(first_own_kernel, out, scratch, smem=(0,), nin=1 + 2 * COLS)(
-        offsets, *kv, *qg
-    )
+    return call(first_own_kernel, out, scratch, smem=(0,), nin=3 + COLS)(offsets, kv, tab, *qg)
 
 
 def first_prev_kernel(
@@ -380,7 +406,7 @@
     )
 
 
-def back_prev_kernel(kv_ref, qg_ref, fin_ref, acc, dq_ref):
+def back_prev_kernel(kv_ref, qg_ref, fin_ref, acc, ds_ref):
     plane, _ = place()
     there = plane > 0
     seen = iota((SLAB, SLAB), 0) > iota((SLAB, SLAB), 1)
@@ -401,14 +427,13 @@
             ds = (p * (nt(v, g) - fin_ref[1:2, lanes])).astype(BF16)
             dv = dv + nn(p.astype(BF16), g)
             dk = dk + nn(ds, q)
-            part = tn(k, ds)
-            dq_ref[:, lanes] = part if kb == qb else dq_ref[:, lanes] + part
+            ds_ref[rows_of(kb), lanes] = ds
         acc[0, rows_of(kb)] = dk
         acc[1, rows_of(kb)] = dv
 
 
 def back_prev(kv, qg, fin):
-    out = [jax.ShapeDtypeStruct((2, ROW, HD), F32), jax.ShapeDtypeStruct((HD, ROW), F32)]
+    out = [jax.ShapeDtypeStruct((2, ROW, HD), F32), jax.ShapeDtypeStruct((ROW, ROW), BF16)]
     return call(back_prev_kernel, out, nin=3)(kv, qg, fin)
 
 
@@ -435,7 +460,9 @@
     )
 
 
-def back_own_kernel(off_ref, kv_ref, qg_ref, fin_ref, tab_ref, dqp_ref, dqf_ref, *refs):
+def back_own_kernel(
+    off_ref, kv_ref, qg_ref, fin_ref, tab_ref, prev_ref, ds_ref, dqf_ref, *refs
+):
     own_ref, dq_ref, dq = refs
     _, col = place()
     strided = pl.ds(off_ref[col] % 8, FAR8, stride=8)
@@ -444,7 +471,9 @@
         lanes = pl.ds(qb * SLAB, SLAB)
         q = qg_ref[0, rows_of(qb)]
         g = qg_ref[1, rows_of(qb)]
-        dq_sum = dqp_ref[:, lanes]
+        dq_sum = tn(prev_ref[0, rows_of(qb)], ds_ref[rows_of(qb), lanes])
+        for kb in range(qb + 1, COLS):
+            dq_sum = dq_sum + tn(prev_ref[0, rows_of(kb)], ds_ref[rows_of(kb), lanes])
         for kb in range(qb + 1):
             k = kv_ref[0, rows_of(kb)]
             s = nt(k, q) * C2 - fin_ref[0:1, lanes]
@@ -466,11 +495,11 @@
     dq_ref[...] = (dq[...] * SCALE).astype(BF16)
 
 
-def back_own(offsets, kv, qg, fin, tab, dqp, dqf):
+def back_own(offsets, kv, qg, fin, tab, prev, ds, dqf):
     out = [jax.ShapeDtypeStruct((2, ROW, HD), F32), jax.ShapeDtypeStruct((ROW, HD), BF16)]
     scratch = [pltpu.VMEM((ROW, HD), F32)]
-    return call(back_own_kernel, out, scratch, smem=(0,), nin=7)(
-        offsets, kv, qg, fin, tab, dqp, dqf
+    return call(back_own_kernel, out, scratch, smem=(0,), nin=8)(
+        offsets, kv, qg, fin, tab, prev, ds, dqf
     )
 
 
@@ -506,16 +535,16 @@
 def spread_kernel(*refs):
     q_ref, k_ref, v_ref = refs[COLS:]
     _, col = place()
-    for step in range(COLS):
+    for ref, step in zip(refs[:COLS], ORDER):
         lanes = pl.ds(pl.multiple_of(((col - step + COLS) % COLS) * HD, HD), HD)
-        q_ref[:, lanes] = refs[step][2]
-        k_ref[:, lanes] = refs[step][0]
-        v_ref[:, lanes] = refs[step][1]
+        q_ref[:, lanes] = ref[2]
+        k_ref[:, lanes] = ref[0]
+        v_ref[:, lanes] = ref[1]
 
 
 def spread(pieces):
     out = jax.ShapeDtypeStruct((SLAB, COLS * HD), BF16)
-    return call(spread_kernel, [out] * 3, nin=COLS)(*pieces)
+    return call(spread_kernel, [out] * 3, nin=COLS)(*[pieces[step] for step in ORDER])
 
 
 def body(planes, query_states, key_states, value_states, out_grad, head_offsets):
@@ -525,18 +554,19 @@
     kv = exchange(pack(key_states, value_states))
     qg = exchange(pack(query_states, out_grad))
     first = along(kv[0], 1, planes)
-    first, *rest = lax.optimization_barrier((first, *kv[1:]))
+    first, *rest = lax.optimization_barrier((first, *[kv[step] for step in ORDER[1:]]))
     rest = along(stack(rest), 1, planes)
-    prev, wide, slim = pair_up(head_offsets, kv, first, rest)
+    row, mine_wide, mine_slim, tab = prepare(head_offsets, kv)
+    prev, wide, slim = pair_up(head_offsets, mine_wide, mine_slim, first, rest)
     prev, qg[0] = lax.optimization_barrier((prev, qg[0]))
-    stat_own, row, qg, tab, qg8 = first_own(head_offsets, kv, qg)
+    stat_own, qg, qg8 = first_own(head_offsets, row, tab, qg)
     far = [along(wide, 2, planes), along(slim, 4, planes), along(slim, 6, planes)]
     stat, some, kv8 = first_prev(head_offsets, prev, qg, stat_own)
     fin, h2, h4, h6, dqf, pf = far_part(head_offsets, kv8, qg8, far, stat, some)
     a2, a4, a6 = [along(h, -step, planes) for h, step in ((h2, 2), (h4, 4), (h6, 6))]
-    prev_grad, dqp = back_prev(prev, qg, fin)
+    prev_grad, ds = back_prev(prev, qg, fin)
     near = along(merge(head_offsets, prev_grad, pf, a2, a4, a6), -1, planes)
-    own, dq = back_own(head_offsets, row, qg, fin, tab, dqp, dqf)
+    own, dq = back_own(head_offsets, row, qg, fin, tab, prev, ds, dqf)
     pieces = exchange(join(head_offsets, dq, own, near, a2, a4, a6))
     return tuple(spread(pieces))
 

time: 75 us -> 74.3 us (level)
  waiting for transfers between devices: 25.7 us -> 21.4 us
  local copies, waits for them, and re-layouts: 1.9 us -> 4.44 us
    ppermute x9, waiting for transfers between devices: 17.6 us -> 14.4 us  [along(): return lax.ppermute(value, 'seq', pairs)]
    unnamed x10, local copies, waits for them, and re-layouts: 1.9 us -> 4.44 us
    ppermute x9, waiting for transfers between devices: 8.15 us -> 7.01 us  [across(): return lax.ppermute(value, 'seq', pairs)]
    pallas_call x4 -> x5, Pallas kernels: 7.41 us -> 8.31 us  [the longest x1 3.42 us: back_own(): call(back_own_kernel, out, scratch, smem=(0,), nin=8)]
  transfers between devices with their start and end apart: 18 -> 18, of which waited for: 8 -> 7; matrix products, arithmetic and copies ran while one was open for 0% -> 0% of each run, Pallas kernels for 15% -> 16%
where the time goes in v4:
time: 74.3 us; the launch traced here: 74.1 us
  starting transfers between devices  31.3 us (42%)
  waiting for transfers between devices  21.4 us (29%)
  Pallas kernels  16.1 us (22%)
  local copies, waits for them, and re-layouts  4.44 us (6%)
  between operations  0.78 us (1%)
    ppermute x9, starting transfers between devices, along(): return lax.ppermute(value, 'seq', pairs)  17.1 us
    ppermute x9, waiting for transfers between devices, along(): return lax.ppermute(value, 'seq', pairs)  14.4 us
    ppermute x9, starting transfers between devices, across(): return lax.ppermute(value, 'seq', pairs)  14.2 us
    ppermute x9, waiting for transfers between devices, across(): return lax.ppermute(value, 'seq', pairs)  7.01 us
    unnamed x10, local copies, waits for them, and re-layouts  4.44 us
    pallas_call x1, Pallas kernels, back_own(): call(back_own_kernel, out, scratch, smem=(0,), nin=8)  3.42 us
    pallas_call x1, Pallas kernels, first_prev(): call(first_prev_kernel, out, scratch, smem=(0,), nin=4)  2.4 us
    pallas_call x1, Pallas kernels, first_own(): call(first_own_kernel, out, scratch, smem=(0,), nin=3 + COLS)  2.1 us
  transfers between devices with their start and end apart: 18, of which 7 were waited for; matrix products, arithmetic and copies ran while one was open for 0% of the time, Pallas kernels for 16%

profile of v4, /device:TPU:8, one launch (start us, length us, event | category | flops | bytes accessed | tf_op | source)
XLA Modules:
  0.0 74.1 jit_solution(185234987763057124)
XLA Ops:
  0.6 0.0 copy-start
  0.6 0.9 %copy-done = bf16[256,512]{1,0:T(8,128)(2,1)S(1)} copy-done((bf16[256,512]{1,0:T(8,128)(2,1)S(1)}, bf16[256,512]{1,0:T(8,128)(2,1)}, u32[]{:S(2)}) %copy-start) | copy-done | bytes 262168
  1.6 0.0 copy-start.1
  1.6 0.9 %copy-done.1 = bf16[256,512]{1,0:T(8,128)(2,1)S(1)} copy-done((bf16[256,512]{1,0:T(8,128)(2,1)S(1)}, bf16[256,512]{1,0:T(8,128)(2,1)}, u32[]{:S(2)}) %copy-start.1) | copy-done | bytes 262168
  2.5 0.1 shard_map.76
  2.6 1.6 %collective-permute-start = (bf16[2,256,128]{2,1,0:T(8,128)(2,1)S(1)}, bf16[2,256,128]{2,1,0:T(8,128)(2,1)S(1)}, u32[]{:S(2)}, u32[]{:S(2)}) collective-permute-start(bf16[2,256,128]{2,1,0:T(8,128)(2,1)S(1)} %get-tuple-element.45), channel_id=1, source_target_pairs={{0,8},{8,16},{16,24},{24,0},{32,40},{40,48},{48,56},{56,32},{64,72... | collective-permute-start | bytes 393224 | tf_op jit(solution)/shard_map/ppermute | solution.py:35
  4.2 2.7 %collective-permute-start.1 = (bf16[2,256,128]{2,1,0:T(8,128)(2,1)S(1)}, bf16[2,256,128]{2,1,0:T(8,128)(2,1)S(1)}, u32[]{:S(2)}, u32[]{:S(2)}) collective-permute-start(bf16[2,256,128]{2,1,0:T(8,128)(2,1)S(1)} %get-tuple-element.46), channel_id=1, source_target_pairs={{0,16},{8,24},{16,0},{24,8},{32,48},{40,56},{48,32},{56,40},{64,80... | collective-permute-start | bytes 393224 | tf_op jit(solution)/shard_map/ppermute | solution.py:35
  6.9 1.4 %collective-permute-start.2 = (bf16[2,256,128]{2,1,0:T(8,128)(2,1)S(1)}, bf16[2,256,128]{2,1,0:T(8,128)(2,1)S(1)}, u32[]{:S(2)}, u32[]{:S(2)}) collective-permute-start(bf16[2,256,128]{2,1,0:T(8,128)(2,1)S(1)} %get-tuple-element.47), channel_id=1, source_target_pairs={{0,24},{8,0},{16,8},{24,16},{32,56},{40,32},{48,40},{56,48},{64,88... | collective-permute-start | bytes 393224 | tf_op jit(solution)/shard_map/ppermute | solution.py:35
  8.4 1.9 %collective-permute-start.3 = (bf16[2,256,128]{2,1,0:T(8,128)(2,1)S(1)}, bf16[2,256,128]{2,1,0:T(8,128)(2,1)S(1)}, u32[]{:S(2)}, u32[]{:S(2)}) collective-permute-start(bf16[2,256,128]{2,1,0:T(8,128)(2,1)S(1)} %get-tuple-element.44.refs_0_), channel_id=1, source_target_pairs={{0,32},{8,40},{16,48},{24,56},{32,64},{40,72},{48,80},{56,88},{64,... | collective-permute-start | bytes 393224 | tf_op jit(solution)/shard_map/ppermute | solution.py:42
  10.3 0.0 collective-permute-done.refs_1_
  10.3 2.7 %collective-permute-done.1.refs_2_.refs_0_ = bf16[2,256,128]{2,1,0:T(8,128)(2,1)S(1)} collective-permute-done((bf16[2,256,128]{2,1,0:T(8,128)(2,1)S(1)}, bf16[2,256,128]{2,1,0:T(8,128)(2,1)S(1)}, u32[]{:S(2)}, u32[]{:S(2)}) %collective-permute-start.1) | collective-permute-done | bytes 131104 | tf_op jit(solution)/shard_map/ppermute | solution.py:35
  13.0 0.0 collective-permute-done.2.refs_3_.refs_2_
  13.0 4.2 %collective-permute-done.3.first_ref = bf16[2,256,128]{2,1,0:T(8,128)(2,1)S(1)} collective-permute-done((bf16[2,256,128]{2,1,0:T(8,128)(2,1)S(1)}, bf16[2,256,128]{2,1,0:T(8,128)(2,1)S(1)}, u32[]{:S(2)}, u32[]{:S(2)}) %collective-permute-start.3) | collective-permute-done | bytes 131104 | tf_op jit(solution)/shard_map/ppermute | solution.py:42
  17.2 0.1 collective-permute-start.4
  17.3 0.0 copy-start.2
  17.3 0.9 %copy-done.2 = bf16[256,512]{1,0:T(8,128)(2,1)S(1)} copy-done((bf16[256,512]{1,0:T(8,128)(2,1)S(1)}, bf16[256,512]{1,0:T(8,128)(2,1)}, u32[]{:S(2)}) %copy-start.2) | copy-done | bytes 262168
  18.2 0.0 copy-start.3
  18.2 0.9 %copy-done.3 = bf16[256,512]{1,0:T(8,128)(2,1)S(1)} copy-done((bf16[256,512]{1,0:T(8,128)(2,1)S(1)}, bf16[256,512]{1,0:T(8,128)(2,1)}, u32[]{:S(2)}) %copy-start.3) | copy-done | bytes 262168
  19.2 0.1 shard_map.80
  19.3 0.7 collective-permute-start.5
  20.0 0.9 %collective-permute-start.6 = (bf16[2,256,128]{2,1,0:T(8,128)(2,1)S(1)}, bf16[2,256,128]{2,1,0:T(8,128)(2,1)S(1)}, u32[]{:S(2)}, u32[]{:S(2)}) collective-permute-start(bf16[2,256,128]{2,1,0:T(8,128)(2,1)S(1)} %get-tuple-element.60), channel_id=1, source_target_pairs={{0,16},{8,24},{16,0},{24,8},{32,48},{40,56},{48,32},{56,40},{64,80... | collective-permute-start | bytes 393224 | tf_op jit(solution)/shard_map/ppermute | solution.py:35
  20.8 1.9 %collective-permute-start.7 = (bf16[2,256,128]{2,1,0:T(8,128)(2,1)S(1)}, bf16[2,256,128]{2,1,0:T(8,128)(2,1)S(1)}, u32[]{:S(2)}, u32[]{:S(2)}) collective-permute-start(bf16[2,256,128]{2,1,0:T(8,128)(2,1)S(1)} %get-tuple-element.61), channel_id=1, source_target_pairs={{0,24},{8,0},{16,8},{24,16},{32,56},{40,32},{48,40},{56,48},{64,88... | collective-permute-start | bytes 393224 | tf_op jit(solution)/shard_map/ppermute | solution.py:35
  22.7 0.0 copy-start.4
  22.7 0.7 copy-done.4
  23.4 1.0 %shard_map.77 = (bf16[2,1024,128]{2,1,0:T(8,128)(2,1)S(1)}, bf16[2,64,128]{2,1,0:T(8,128)(2,1)S(1)}, bf16[2,32,128]{2,1,0:T(8,128)(2,1)S(1)}, f32[2,256,256]{2,1,0:T(8,128)S(1)}) custom-call(s32[4]{0:T(128)S(1)} %copy-done.4, bf16[2,256,128]{2,1,0:T(8,128)(2,1)S(1)} %get-tuple-element.44.refs_0_, bf16[2,256,128]{2,1,0:T(8,128)(2,1)S(1)} %collective-permute-done.refs_1_, ...), custom_call_target="tpu_custom_call" | custom-call | flops 1 | bytes 1 | tf_op jit(solution)/shard_map/pallas_call | solution.py:151
  24.4 3.3 %collective-permute-done.4.rest_ref = bf16[2,768,128]{2,1,0:T(8,128)(2,1)S(1)} collective-permute-done((bf16[2,768,128]{2,1,0:T(8,128)(2,1)S(1)}, bf16[2,768,128]{2,1,0:T(8,128)(2,1)S(1)}, u32[]{:S(2)}, u32[]{:S(2)}) %collective-permute-start.4) | collective-permute-done | bytes 393248 | tf_op jit(solution)/shard_map/ppermute | solution.py:42
  27.6 0.8 %shard_map.79 = (bf16[2,1024,128]{2,1,0:T(8,128)(2,1)S(1)}, bf16[2,2,64,128]{3,2,1,0:T(8,128)(2,1)S(1)}, bf16[2,2,32,128]{3,2,1,0:T(8,128)(2,1)S(1)}) custom-call(s32[4]{0:T(128)S(1)} %copy-done.4, bf16[2,64,128]{2,1,0:T(8,128)(2,1)S(1)} %get-tuple-element.50.mw_ref, bf16[2,32,128]{2,1,0:T(8,128)(2,1)S(1)} %get-tuple-element.51.ms_ref, ...), custom_call_target="tpu_custom_call" | custom-call | flops 1 | bytes 1 | tf_op jit(solution)/shard_map/pallas_call | solution.py:180
  28.4 0.1 collective-permute-start.8
  28.5 4.1 %collective-permute-start.10 = (bf16[2,2,32,128]{3,2,1,0:T(8,128)(2,1)S(1)}, bf16[2,2,32,128]{3,2,1,0:T(8,128)(2,1)S(1)}, u32[]{:S(2)}, u32[]{:S(2)}) collective-permute-start(bf16[2,2,32,128]{3,2,1,0:T(8,128)(2,1)S(1)} %get-tuple-element.68), channel_id=1, source_target_pairs={{0,192},{8,200},{16,208},{24,216},{32,224},{40,232},{48,240},{56,2... | collective-permute-start | bytes 98312 | tf_op jit(solution)/shard_map/ppermute | solution.py:42
  32.7 0.0 collective-permute-done.5.refs_1_
  32.7 4.6 %collective-permute-start.9 = (bf16[2,2,32,128]{3,2,1,0:T(8,128)(2,1)S(1)}, bf16[2,2,32,128]{3,2,1,0:T(8,128)(2,1)S(1)}, u32[]{:S(2)}, u32[]{:S(2)}) collective-permute-start(bf16[2,2,32,128]{3,2,1,0:T(8,128)(2,1)S(1)} %get-tuple-element.68), channel_id=1, source_target_pairs={{0,128},{8,136},{16,144},{24,152},{32,160},{40,168},{48,176},{56,1... | collective-permute-start | bytes 98312 | tf_op jit(solution)/shard_map/ppermute | solution.py:42
  37.2 0.0 collective-permute-done.6.refs_2_
  37.2 0.0 collective-permute-done.7.refs_3_
  37.2 2.1 %shard_map.81 = (f32[8,1024]{1,0:T(8,128)S(1)}, bf16[2,1024,128]{2,1,0:T(8,128)(2,1)S(1)}, bf16[2,128,128]{2,1,0:T(8,128)(2,1)S(1)}) custom-call(s32[4]{0:T(128)S(1)} %copy-done.4, bf16[2,1024,128]{2,1,0:T(8,128)(2,1)S(1)} %get-tuple-element.48.kv_ref, f32[2,256,256]{2,1,0:T(8,128)S(1)} %get-tuple-element.49.tab_ref, ...), custom_call_target="tpu_custom_call" | custom-call | flops 1 | bytes 1 | tf_op jit(solution)/shard_map/pallas_call | solution.py:247
  39.3 2.4 %shard_map.82 = (f32[8,1024]{1,0:T(8,128)S(1)}, f32[8,128]{1,0:T(8,128)S(1)}, bf16[2,128,128]{2,1,0:T(8,128)(2,1)S(1)}) custom-call(s32[4]{0:T(128)S(1)} %copy-done.4, bf16[2,1024,128]{2,1,0:T(8,128)(2,1)S(1)} %get-tuple-element.63.kv_ref.prev_ref, bf16[2,1024,128]{2,1,0:T(8,128)(2,1)S(1)} %get-tuple-element.62.qg_ref, f32[8,1024]{1,0:T(8,128)S(1)} %get-tuple-element.64.so_ref), custom_call_target="tpu_custom_call" | custom-call | flops 1 | bytes 1 | tf_op jit(solution)/shard_map/pallas_call | solution.py:311
  41.8 0.0 collective-permute-done.10.g6_ref
  41.8 0.0 collective-permute-done.9.g4_ref
  41.8 0.0 collective-permute-done.8.g2_ref
  41.8 1.5 %shard_map.83 = (f32[8,1024]{1,0:T(8,128)S(1)}, bf16[2,2,64,128]{3,2,1,0:T(8,128)(2,1)S(1)}, bf16[2,2,32,128]{3,2,1,0:T(8,128)(2,1)S(1)}, bf16[2,2,32,128]{3,2,1...) custom-call(s32[4]{0:T(128)S(1)} %copy-done.4, ...), custom_call_target="tpu_custom_call" | custom-call | flops 1 | bytes 1 | tf_op jit(solution)/shard_map/pallas_call | solution.py:404
  43.3 0.1 collective-permute-start.11
  43.4 3.4 %collective-permute-start.12 = (bf16[2,2,32,128]{3,2,1,0:T(8,128)(2,1)S(1)}, bf16[2,2,32,128]{3,2,1,0:T(8,128)(2,1)S(1)}, u32[]{:S(2)}, u32[]{:S(2)}) collective-permute-start(bf16[2,2,32,128]{3,2,1,0:T(8,128)(2,1)S(1)} %get-tuple-element.79), channel_id=1, source_target_pairs={{0,128},{8,136},{16,144},{24,152},{32,160},{40,168},{48,176},{56,1... | collective-permute-start | bytes 98312 | tf_op jit(solution)/shard_map/ppermute | solution.py:42
  46.8 2.8 %collective-permute-start.13 = (bf16[2,2,32,128]{3,2,1,0:T(8,128)(2,1)S(1)}, bf16[2,2,32,128]{3,2,1,0:T(8,128)(2,1)S(1)}, u32[]{:S(2)}, u32[]{:S(2)}) collective-permute-start(bf16[2,2,32,128]{3,2,1,0:T(8,128)(2,1)S(1)} %get-tuple-element.80), channel_id=1, source_target_pairs={{0,64},{8,72},{16,80},{24,88},{32,96},{40,104},{48,112},{56,120},{... | collective-permute-start | bytes 98312 | tf_op jit(solution)/shard_map/ppermute | solution.py:42
  49.6 2.0 %shard_map.84 = (f32[2,1024,128]{2,1,0:T(8,128)S(1)}, bf16[1024,1024]{1,0:T(8,128)(2,1)S(1)}) custom-call(bf16[2,1024,128]{2,1,0:T(8,128)(2,1)S(1)} %get-tuple-element.63.kv_ref.prev_ref, bf16[2,1024,128]{2,1,0:T(8,128)(2,1)S(1)} %get-tuple-element.62.qg_ref, f32[8,1024]{1,0:T(8,128)S(1)} %get-tuple-element.71.fin_ref), custom_call_target="tpu_custom_call" | custom-call | flops 1 | bytes 1 | tf_op jit(solution)/shard_map/pallas_call | solution.py:437
  51.6 0.0 collective-permute-done.12.a4_ref
  51.6 1.1 %collective-permute-done.13.a6_ref = bf16[2,2,32,128]{3,2,1,0:T(8,128)(2,1)S(1)} collective-permute-done((bf16[2,2,32,128]{3,2,1,0:T(8,128)(2,1)S(1)}, bf16[2,2,32,128]{3,2,1,0:T(8,128)(2,1)S(1)}, u32[]{:S(2)}, u32[]{:S(2)}) %collective-permute-start.13) | collective-permute-done | bytes 32800 | tf_op jit(solution)/shard_map/ppermute | solution.py:42
  52.8 0.0 collective-permute-done.11.a2_ref
  52.8 0.8 %shard_map.86 = bf16[2,1024,128]{2,1,0:T(8,128)(2,1)S(1)} custom-call(s32[4]{0:T(128)S(1)} %copy-done.4, f32[2,1024,128]{2,1,0:T(8,128)S(1)} %get-tuple-element.76.prev_ref, f32[2,128,128]{2,1,0:T(8,128)S(1)} %get-tuple-element.77.pf_ref, bf16[2,2,64,128]{3,2,1,0:T(8,128)(2,1)S(1)} %collective-permute-done.11.a2_ref, ...), custom_call_target="tpu_custom_call" | custom-call | flops 1 | bytes 1 | tf_op jit(solution)/shard_map/pallas_call | solution.py:458
  53.6 0.1 collective-permute-start.14
  53.7 3.4 %shard_map.85 = (f32[2,1024,128]{2,1,0:T(8,128)S(1)}, bf16[1024,128]{1,0:T(8,128)(2,1)S(1)}) custom-call(s32[4]{0:T(128)S(1)} %copy-done.4, bf16[2,1024,128]{2,1,0:T(8,128)(2,1)S(1)} %get-tuple-element.48.kv_ref, bf16[2,1024,128]{2,1,0:T(8,128)(2,1)S(1)} %get-tuple-element.62.qg_ref, f32[8,1024]{1,0:T(8,128)S(1)} %get-tuple-element.71.fin_ref, ...), custom_call_target="tpu_custom_call" | custom-call | flops 1 | bytes 1 | tf_op jit(solution)/shard_map/pallas_call | solution.py:501
  57.1 5.7 %collective-permute-done.14.near_ref = bf16[2,1024,128]{2,1,0:T(8,128)(2,1)S(1)} collective-permute-done((bf16[2,1024,128]{2,1,0:T(8,128)(2,1)S(1)}, bf16[2,1024,128]{2,1,0:T(8,128)(2,1)S(1)}, u32[]{:S(2)}, u32[]{:S(2)}) %collective-permute-start.14) | collective-permute-done | bytes 524320 | tf_op jit(solution)/shard_map/ppermute | solution.py:42
  62.9 0.8 %shard_map.87 = (bf16[3,256,128]{2,1,0:T(8,128)(2,1)S(1)}, bf16[3,256,128]{2,1,0:T(8,128)(2,1)S(1)}, bf16[3,256,128]{2,1,0:T(8,128)(2,1)S(1)}, bf16[3,256,128]{2,1,0:T(8,128)(2,1)S(1)}) custom-call(s32[4]{0:T(128)S(1)} %copy-done.4, bf16[1024,128]{1,0:T(8,128)(2,1)S(1)} %get-tuple-element.74.dq_ref, f32[2,1024,128]{2,1,0:T(8,128)S(1)} %get-tuple-element.75.own_ref, ...), custom_call_target="tpu_custom_call" | custom-call | flops 1 | bytes 1 | tf_op jit(solution)/shard_map/pallas_call | solution.py:530
  63.7 1.8 %collective-permute-start.15 = (bf16[3,256,128]{2,1,0:T(8,128)(2,1)S(1)}, bf16[3,256,128]{2,1,0:T(8,128)(2,1)S(1)}, u32[]{:S(2)}, u32[]{:S(2)}) collective-permute-start(bf16[3,256,128]{2,1,0:T(8,128)(2,1)S(1)} %get-tuple-element.82), channel_id=1, source_target_pairs={{0,16},{8,24},{16,0},{24,8},{32,48},{40,56},{48,32},{56,40},{64,80... | collective-permute-start | bytes 589832 | tf_op jit(solution)/shard_map/ppermute | solution.py:35
  65.5 1.4 %collective-permute-start.16 = (bf16[3,256,128]{2,1,0:T(8,128)(2,1)S(1)}, bf16[3,256,128]{2,1,0:T(8,128)(2,1)S(1)}, u32[]{:S(2)}, u32[]{:S(2)}) collective-permute-start(bf16[3,256,128]{2,1,0:T(8,128)(2,1)S(1)} %get-tuple-element.83), channel_id=1, source_target_pairs={{0,8},{8,16},{16,24},{24,0},{32,40},{40,48},{48,56},{56,32},{64,72... | collective-permute-start | bytes 589832 | tf_op jit(solution)/shard_map/ppermute | solution.py:35
  66.9 1.9 %collective-permute-start.17 = (bf16[3,256,128]{2,1,0:T(8,128)(2,1)S(1)}, bf16[3,256,128]{2,1,0:T(8,128)(2,1)S(1)}, u32[]{:S(2)}, u32[]{:S(2)}) collective-permute-start(bf16[3,256,128]{2,1,0:T(8,128)(2,1)S(1)} %get-tuple-element.84), channel_id=1, source_target_pairs={{0,24},{8,0},{16,8},{24,16},{32,56},{40,32},{48,40},{56,48},{64,88... | collective-permute-start | bytes 589832 | tf_op jit(solution)/shard_map/ppermute | solution.py:35
  68.8 2.3 %collective-permute-done.15.refs_1_ = bf16[3,256,128]{2,1,0:T(8,128)(2,1)S(1)} collective-permute-done((bf16[3,256,128]{2,1,0:T(8,128)(2,1)S(1)}, bf16[3,256,128]{2,1,0:T(8,128)(2,1)S(1)}, u32[]{:S(2)}, u32[]{:S(2)}) %collective-permute-start.15) | collective-permute-done | bytes 196640 | tf_op jit(solution)/shard_map/ppermute | solution.py:35
  71.0 2.0 %collective-permute-done.16.refs_2_ = bf16[3,256,128]{2,1,0:T(8,128)(2,1)S(1)} collective-permute-done((bf16[3,256,128]{2,1,0:T(8,128)(2,1)S(1)}, bf16[3,256,128]{2,1,0:T(8,128)(2,1)S(1)}, u32[]{:S(2)}, u32[]{:S(2)}) %collective-permute-start.16) | collective-permute-done | bytes 196640 | tf_op jit(solution)/shard_map/ppermute | solution.py:35
  73.1 0.0 collective-permute-done.17.refs_3_
  73.1 1.0 %shard_map.88 = (bf16[256,512]{1,0:T(8,128)(2,1)}, bf16[256,512]{1,0:T(8,128)(2,1)}, bf16[256,512]{1,0:T(8,128)(2,1)}) custom-call(bf16[3,256,128]{2,1,0:T(8,128)(2,1)S(1)} %get-tuple-element.81.refs_0_, bf16[3,256,128]{2,1,0:T(8,128)(2,1)S(1)} %collective-permute-done.15.refs_1_, bf16[3,256,128]{2,1,0:T(8,128)(2,1)S(1)} %collective-permute-done.16.refs_2_, ...), custom_call_target="tpu_custom_call" | custom-call | flops 1 | bytes 1 | tf_op jit(solution)/shard_map/pallas_call | solution.py:547
  (1 shorter events, 0.0 us)
Async XLA Ops:
  0.6 1.0 %copy-start = (bf16[256,512]{1,0:T(8,128)(2,1)S(1)}, bf16[256,512]{1,0:T(8,128)(2,1)}, u32[]{:S(2)}) copy-start(bf16[256,512]{1,0:T(8,128)(2,1)} %one_ref.2) | copy-start | bytes 786436
  1.6 0.9 %copy-start.1 = (bf16[256,512]{1,0:T(8,128)(2,1)S(1)}, bf16[256,512]{1,0:T(8,128)(2,1)}, u32[]{:S(2)}) copy-start(bf16[256,512]{1,0:T(8,128)(2,1)} %two_ref.2) | copy-start | bytes 786436
  2.6 7.7 %collective-permute-start = (bf16[2,256,128]{2,1,0:T(8,128)(2,1)S(1)}, bf16[2,256,128]{2,1,0:T(8,128)(2,1)S(1)}, u32[]{:S(2)}, u32[]{:S(2)}) collective-permute-start(bf16[2,256,128]{2,1,0:T(8,128)(2,1)S(1)} %get-tuple-element.45), channel_id=1, source_target_pairs={{0,8},{8,16},{16,24},{24,0},{32,40},{40,48},{48,56},{56,32},{64,72... | collective-permute-start | bytes 393224 | tf_op jit(solution)/shard_map/ppermute | solution.py:35
  4.2 8.7 %collective-permute-start.1 = (bf16[2,256,128]{2,1,0:T(8,128)(2,1)S(1)}, bf16[2,256,128]{2,1,0:T(8,128)(2,1)S(1)}, u32[]{:S(2)}, u32[]{:S(2)}) collective-permute-start(bf16[2,256,128]{2,1,0:T(8,128)(2,1)S(1)} %get-tuple-element.46), channel_id=1, source_target_pairs={{0,16},{8,24},{16,0},{24,8},{32,48},{40,56},{48,32},{56,40},{64,80... | collective-permute-start | bytes 393224 | tf_op jit(solution)/shard_map/ppermute | solution.py:35
  6.9 6.0 %collective-permute-start.2 = (bf16[2,256,128]{2,1,0:T(8,128)(2,1)S(1)}, bf16[2,256,128]{2,1,0:T(8,128)(2,1)S(1)}, u32[]{:S(2)}, u32[]{:S(2)}) collective-permute-start(bf16[2,256,128]{2,1,0:T(8,128)(2,1)S(1)} %get-tuple-element.47), channel_id=1, source_target_pairs={{0,24},{8,0},{16,8},{24,16},{32,56},{40,32},{48,40},{56,48},{64,88... | collective-permute-start | bytes 393224 | tf_op jit(solution)/shard_map/ppermute | solution.py:35
  8.4 8.8 %collective-permute-start.3 = (bf16[2,256,128]{2,1,0:T(8,128)(2,1)S(1)}, bf16[2,256,128]{2,1,0:T(8,128)(2,1)S(1)}, u32[]{:S(2)}, u32[]{:S(2)}) collective-permute-start(bf16[2,256,128]{2,1,0:T(8,128)(2,1)S(1)} %get-tuple-element.44.refs_0_), channel_id=1, source_target_pairs={{0,32},{8,40},{16,48},{24,56},{32,64},{40,72},{48,80},{56,88},{64,... | collective-permute-start | bytes 393224 | tf_op jit(solution)/shard_map/ppermute | solution.py:42
  17.2 10.4 %collective-permute-start.4 = (bf16[2,768,128]{2,1,0:T(8,128)(2,1)S(1)}, bf16[2,768,128]{2,1,0:T(8,128)(2,1)S(1)}, u32[]{:S(2)}, u32[]{:S(2)}) collective-permute-start(bf16[2,768,128]{2,1,0:T(8,128)(2,1)S(1)} %shard_map.78), channel_id=1, source_target_pairs={{0,32},{8,40},{16,48},{24,56},{32,64},{40,72},{48,80},{56,88},{64,... | collective-permute-start | bytes 1179656 | tf_op jit(solution)/shard_map/ppermute | solution.py:42
  17.3 1.0 %copy-start.2 = (bf16[256,512]{1,0:T(8,128)(2,1)S(1)}, bf16[256,512]{1,0:T(8,128)(2,1)}, u32[]{:S(2)}) copy-start(bf16[256,512]{1,0:T(8,128)(2,1)} %one_ref.3) | copy-start | bytes 786436
  18.2 0.9 %copy-start.3 = (bf16[256,512]{1,0:T(8,128)(2,1)S(1)}, bf16[256,512]{1,0:T(8,128)(2,1)}, u32[]{:S(2)}) copy-start(bf16[256,512]{1,0:T(8,128)(2,1)} %two_ref.3) | copy-start | bytes 786436
  19.3 13.4 %collective-permute-start.5 = (bf16[2,256,128]{2,1,0:T(8,128)(2,1)S(1)}, bf16[2,256,128]{2,1,0:T(8,128)(2,1)S(1)}, u32[]{:S(2)}, u32[]{:S(2)}) collective-permute-start(bf16[2,256,128]{2,1,0:T(8,128)(2,1)S(1)} %get-tuple-element.59), channel_id=1, source_target_pairs={{0,8},{8,16},{16,24},{24,0},{32,40},{40,48},{48,56},{56,32},{64,72... | collective-permute-start | bytes 393224 | tf_op jit(solution)/shard_map/ppermute | solution.py:35
  20.0 17.3 %collective-permute-start.6 = (bf16[2,256,128]{2,1,0:T(8,128)(2,1)S(1)}, bf16[2,256,128]{2,1,0:T(8,128)(2,1)S(1)}, u32[]{:S(2)}, u32[]{:S(2)}) collective-permute-start(bf16[2,256,128]{2,1,0:T(8,128)(2,1)S(1)} %get-tuple-element.60), channel_id=1, source_target_pairs={{0,16},{8,24},{16,0},{24,8},{32,48},{40,56},{48,32},{56,40},{64,80... | collective-permute-start | bytes 393224 | tf_op jit(solution)/shard_map/ppermute | solution.py:35
  20.8 16.4 %collective-permute-start.7 = (bf16[2,256,128]{2,1,0:T(8,128)(2,1)S(1)}, bf16[2,256,128]{2,1,0:T(8,128)(2,1)S(1)}, u32[]{:S(2)}, u32[]{:S(2)}) collective-permute-start(bf16[2,256,128]{2,1,0:T(8,128)(2,1)S(1)} %get-tuple-element.61), channel_id=1, source_target_pairs={{0,24},{8,0},{16,8},{24,16},{32,56},{40,32},{48,40},{56,48},{64,88... | collective-permute-start | bytes 393224 | tf_op jit(solution)/shard_map/ppermute | solution.py:35
  22.7 0.7 copy-start.4
  28.4 13.4 %collective-permute-start.8 = (bf16[2,2,64,128]{3,2,1,0:T(8,128)(2,1)S(1)}, bf16[2,2,64,128]{3,2,1,0:T(8,128)(2,1)S(1)}, u32[]{:S(2)}, u32[]{:S(2)}) collective-permute-start(bf16[2,2,64,128]{3,2,1,0:T(8,128)(2,1)S(1)} %get-tuple-element.67), channel_id=1, source_target_pairs={{0,64},{8,72},{16,80},{24,88},{32,96},{40,104},{48,112},{56,120},{... | collective-permute-start | bytes 196616 | tf_op jit(solution)/shard_map/ppermute | solution.py:42
  28.5 13.2 %collective-permute-start.10 = (bf16[2,2,32,128]{3,2,1,0:T(8,128)(2,1)S(1)}, bf16[2,2,32,128]{3,2,1,0:T(8,128)(2,1)S(1)}, u32[]{:S(2)}, u32[]{:S(2)}) collective-permute-start(bf16[2,2,32,128]{3,2,1,0:T(8,128)(2,1)S(1)} %get-tuple-element.68), channel_id=1, source_target_pairs={{0,192},{8,200},{16,208},{24,216},{32,224},{40,232},{48,240},{56,2... | collective-permute-start | bytes 98312 | tf_op jit(solution)/shard_map/ppermute | solution.py:42
  32.7 9.1 %collective-permute-start.9 = (bf16[2,2,32,128]{3,2,1,0:T(8,128)(2,1)S(1)}, bf16[2,2,32,128]{3,2,1,0:T(8,128)(2,1)S(1)}, u32[]{:S(2)}, u32[]{:S(2)}) collective-permute-start(bf16[2,2,32,128]{3,2,1,0:T(8,128)(2,1)S(1)} %get-tuple-element.68), channel_id=1, source_target_pairs={{0,128},{8,136},{16,144},{24,152},{32,160},{40,168},{48,176},{56,1... | collective-permute-start | bytes 98312 | tf_op jit(solution)/shard_map/ppermute | solution.py:42
  43.3 9.5 %collective-permute-start.11 = (bf16[2,2,64,128]{3,2,1,0:T(8,128)(2,1)S(1)}, bf16[2,2,64,128]{3,2,1,0:T(8,128)(2,1)S(1)}, u32[]{:S(2)}, u32[]{:S(2)}) collective-permute-start(bf16[2,2,64,128]{3,2,1,0:T(8,128)(2,1)S(1)} %get-tuple-element.78), channel_id=1, source_target_pairs={{0,192},{8,200},{16,208},{24,216},{32,224},{40,232},{48,240},{56,2... | collective-permute-start | bytes 196616 | tf_op jit(solution)/shard_map/ppermute | solution.py:42
  43.4 8.2 %collective-permute-start.12 = (bf16[2,2,32,128]{3,2,1,0:T(8,128)(2,1)S(1)}, bf16[2,2,32,128]{3,2,1,0:T(8,128)(2,1)S(1)}, u32[]{:S(2)}, u32[]{:S(2)}) collective-permute-start(bf16[2,2,32,128]{3,2,1,0:T(8,128)(2,1)S(1)} %get-tuple-element.79), channel_id=1, source_target_pairs={{0,128},{8,136},{16,144},{24,152},{32,160},{40,168},{48,176},{56,1... | collective-permute-start | bytes 98312 | tf_op jit(solution)/shard_map/ppermute | solution.py:42
  46.8 6.0 %collective-permute-start.13 = (bf16[2,2,32,128]{3,2,1,0:T(8,128)(2,1)S(1)}, bf16[2,2,32,128]{3,2,1,0:T(8,128)(2,1)S(1)}, u32[]{:S(2)}, u32[]{:S(2)}) collective-permute-start(bf16[2,2,32,128]{3,2,1,0:T(8,128)(2,1)S(1)} %get-tuple-element.80), channel_id=1, source_target_pairs={{0,64},{8,72},{16,80},{24,88},{32,96},{40,104},{48,112},{56,120},{... | collective-permute-start | bytes 98312 | tf_op jit(solution)/shard_map/ppermute | solution.py:42
  53.6 9.3 %collective-permute-start.14 = (bf16[2,1024,128]{2,1,0:T(8,128)(2,1)S(1)}, bf16[2,1024,128]{2,1,0:T(8,128)(2,1)S(1)}, u32[]{:S(2)}, u32[]{:S(2)}) collective-permute-start(bf16[2,1024,128]{2,1,0:T(8,128)(2,1)S(1)} %shard_map.86), channel_id=1, source_target_pairs={{0,224},{8,232},{16,240},{24,248},{32,0},{40,8},{48,16},{56,24},{6... | collective-permute-start | bytes 1572872 | tf_op jit(solution)/shard_map/ppermute | solution.py:42
  63.7 7.3 %collective-permute-start.15 = (bf16[3,256,128]{2,1,0:T(8,128)(2,1)S(1)}, bf16[3,256,128]{2,1,0:T(8,128)(2,1)S(1)}, u32[]{:S(2)}, u32[]{:S(2)}) collective-permute-start(bf16[3,256,128]{2,1,0:T(8,128)(2,1)S(1)} %get-tuple-element.82), channel_id=1, source_target_pairs={{0,16},{8,24},{16,0},{24,8},{32,48},{40,56},{48,32},{56,40},{64,80... | collective-permute-start | bytes 589832 | tf_op jit(solution)/shard_map/ppermute | solution.py:35
  65.5 7.6 %collective-permute-start.16 = (bf16[3,256,128]{2,1,0:T(8,128)(2,1)S(1)}, bf16[3,256,128]{2,1,0:T(8,128)(2,1)S(1)}, u32[]{:S(2)}, u32[]{:S(2)}) collective-permute-start(bf16[3,256,128]{2,1,0:T(8,128)(2,1)S(1)} %get-tuple-element.83), channel_id=1, source_target_pairs={{0,8},{8,16},{16,24},{24,0},{32,40},{40,48},{48,56},{56,32},{64,72... | collective-permute-start | bytes 589832 | tf_op jit(solution)/shard_map/ppermute | solution.py:35
  66.9 6.2 %collective-permute-start.17 = (bf16[3,256,128]{2,1,0:T(8,128)(2,1)S(1)}, bf16[3,256,128]{2,1,0:T(8,128)(2,1)S(1)}, u32[]{:S(2)}, u32[]{:S(2)}) collective-permute-start(bf16[3,256,128]{2,1,0:T(8,128)(2,1)S(1)} %get-tuple-element.84), channel_id=1, source_target_pairs={{0,24},{8,0},{16,8},{24,16},{32,56},{40,32},{48,40},{56,48},{64,88... | collective-permute-start | bytes 589832 | tf_op jit(solution)/shard_map/ppermute | solution.py:35
